TPU v7x, 512 devices: a whole 4x4x16 slice. The times are simulated.
512 devices in a mesh: row: 16 (over x, y), col: 32 (over z, core).
Axes of the slice: x: 4, y: 4, z: 16, core: 2. Of those that a mesh axis runs over, the one named last changes fastest.
Arguments:
- member_outputs: float32 [3, 8192, 512], P(None, ('row', 'col')), may hold values from -6 to 6
- pivot_inverse_matrices: bfloat16 [2, 8192, 8192], P(None, 'col', 'row'), may hold values from -1 to 1.25, as said below
- former_subdiagonal_tiles: bfloat16 [2, 8192, 8192], P(None, 'row', 'col'), may hold values from -0.125 to 0.125
- latter_subdiagonal_tiles: bfloat16 [1, 8192, 8192], P(None, 'row', 'col'), may hold values from -0.125 to 0.125
Outputs:
- whitened: bfloat16 [2, 8192, 512], P(None, 'col')
- trailing: float32 [1, 8192, 512], P(None, ('row', 'col'))
- projections: float32 [256, 512], replicated
Inputs may be any that keep to these rules, and one draw needn't show every extreme that they name: `pivot_inverse_matrices`: each block is lower triangular with a positive diagonal: the inverse of a diagonal block of the error covariance's Cholesky factor.
All inputs are finite; a program needn't handle non-finite values.
Results may differ from a plain program's by a relative error of at most 0.0057.
Values may be sent and summed in bfloat16 or wider, within the bound.
No kernel may reach another device: no remote copies, remote signals or barrier semaphores. Data moves between devices by JAX's collectives and lax.ppermute only.
A program may use at most 64 MiB of HBM per device.

v0:
```python
import jax
import jax.numpy as jnp
from jax import lax
from jax.sharding import PartitionSpec as P


def standardize_prior_deviations(partition_height, reciprocal_matrix):
    partial_value = jnp.dot(
        reciprocal_matrix,
        lax.all_gather(partition_height.astype(jnp.bfloat16), "col", axis=0, tiled=True),
        preferred_element_type=jnp.float32,
    )
    return lax.psum(partial_value, "row")


def make_term(panel_tiles, white_bf):
    return jnp.einsum("tij,jk->itk", panel_tiles, white_bf, preferred_element_type=jnp.float32)


def body(
    member_outputs, pivot_inverse_matrices, former_subdiagonal_tiles, latter_subdiagonal_tiles
):
    starting_cheap_cholesky = standardize_prior_deviations(
        member_outputs[0], pivot_inverse_matrices[0]
    ).astype(jnp.bfloat16)
    collapsed_aggregate = lax.psum_scatter(
        make_term(former_subdiagonal_tiles, starting_cheap_cholesky),
        "col",
        scatter_dimension=0,
        tiled=True,
    )
    fresh_strip_entries = member_outputs[1:] - jnp.swapaxes(collapsed_aggregate, 0, 1)
    later_narrow_piece = standardize_prior_deviations(
        fresh_strip_entries[0], pivot_inverse_matrices[1]
    ).astype(jnp.bfloat16)
    later_rows = fresh_strip_entries[1:]
    second_sum = lax.psum_scatter(
        make_term(latter_subdiagonal_tiles, later_narrow_piece),
        "col",
        scatter_dimension=0,
        tiled=True,
    )
    trailing = later_rows - jnp.swapaxes(second_sum, 0, 1)
    whitened = jnp.stack([starting_cheap_cholesky, later_narrow_piece])
    members = starting_cheap_cholesky.shape[1] // 2
    partial_value = jnp.einsum(
        "ie,ik->ek",
        starting_cheap_cholesky[:, :members],
        starting_cheap_cholesky,
        preferred_element_type=jnp.float32,
    )
    partial_value = partial_value + jnp.einsum(
        "ie,ik->ek",
        later_narrow_piece[:, :members],
        later_narrow_piece,
        preferred_element_type=jnp.float32,
    )
    projections = lax.psum(partial_value, "col")
    return (whitened, trailing, projections)


def solution(mesh):
    in_specs = (
        P(None, ("row", "col"), None),
        P(None, "col", "row"),
        P(None, "row", "col"),
        P(None, "row", "col"),
    )
    out_specs = (P(None, "col", None), P(None, ("row", "col"), None), P())
    return jax.shard_map(body, mesh=mesh, in_specs=in_specs, out_specs=out_specs, check_vma=False)
```

profile of v0, /device:TPU:1, one launch (start us, length us, event | category | flops | bytes accessed | tf_op | source)
XLA Modules:
  0.0 669.8 jit_solution(6507258605242536984)
XLA Ops:
  7.2 0.0 copy-start
  7.2 0.0 all-reduce.8.cloned.1.call-start
  7.2 0.8 slice.55
  8.0 39.0 %all-gather = bf16[1,512,512]{2,1,0:T(8,128)(2,1)S(1)} all-gather(bf16[1,16,512]{2,1,0:T(8,128)(2,1)S(1)} %slice.55), channel_id=2, replica_groups=mesh['row'=16,'col'=32] {'col'}, dimensions={1}, use_global_device_ids=true | all-gather | bytes 540672 | tf_op jit(solution)/shard_map/all_gather | solution.py:10
  47.0 1.2 fusion.1
  48.3 66.5 %all-reduce.11 = bf16[256,512]{1,0:T(8,128)(2,1)S(1)} all-reduce(f32[256,512]{1,0:T(8,128)S(1)} %fusion.1), channel_id=1, replica_groups=mesh['row'=16,'col'=32] {'row'}, use_global_device_ids=true, to_apply=%region_0.0 | all-reduce | flops 131072 | bytes 786432 | tf_op jit(solution)/shard_map/psum | solution.py:13
  114.8 0.0 copy-done
  114.8 0.5 convolution_bitcast_fusion
  115.3 2.5 copy.13
  117.7 0.0 slice-start
  117.7 0.0 copy-start.1
  117.8 0.0 all-reduce.8.cloned.1.call-update
  117.8 0.0 all-reduce.10.cloned.1.call-start
  117.8 1.3 dynamic-slice
  119.8 0.2 fusion.10
  120.1 216.7 %all-reduce.8.cloned.1.call-done = f32[512,2,512]{2,1,0:T(2,128)} async-done(((f32[512,2,512]{2,1,0:T(2,128)}), f32[512,2,512]{2,1,0:T(2,128)}) %all-reduce.8.cloned.1.call-update) | async-done | bytes 2097168
  336.8 0.0 slice-done
  336.8 0.9 copy_subtract_fusion
  337.7 29.6 %all-gather.1 = bf16[1,512,512]{2,1,0:T(8,128)(2,1)S(1)} all-gather(bf16[1,16,512]{2,1,0:T(8,128)(2,1)S(1)} %copy.14), channel_id=3, replica_groups=mesh['row'=16,'col'=32] {'col'}, dimensions={1}, use_global_device_ids=true | all-gather | bytes 540672 | tf_op jit(solution)/shard_map/all_gather | solution.py:10
  367.3 0.0 copy-done.1
  367.3 0.3 convolution_bitcast_fusion.2
  367.6 66.1 %all-reduce.12 = bf16[256,512]{1,0:T(8,128)(2,1)S(1)} all-reduce(f32[256,512]{1,0:T(8,128)S(1)} %convolution_bitcast_fusion.2), channel_id=1, replica_groups=mesh['row'=16,'col'=32] {'row'}, use_global_device_ids=true, to_apply=%region_2.0 | all-reduce | flops 131072 | bytes 786432 | tf_op jit(solution)/shard_map/psum | solution.py:13
  433.8 1.0 convolution_add_fusion
  434.8 1.3 convolution_bitcast_fusion.1
  436.1 2.0 copy.16
  438.1 0.0 all-reduce.10.cloned.1.call-update
  438.1 0.8 pad_maximum_fusion
  439.0 220.7 %all-reduce.10.cloned.1.call-done = (f32[512,1,512]{2,1,0:T(1,128)}, f32[256,512]{1,0:T(8,128)}) async-done(((f32[512,1,512]{2,1,0:T(1,128)}, f32[256,512]{1,0:T(8,128)}), (f32[512,1,512]{2,1,0:T(1,128)}, f32[256,512]{1,0:T(8,128)})) %all-reduce.10.cloned.1.call-update) | async-done | bytes 1572880
  659.7 0.8 slice_subtract_fusion
  660.5 0.6 copy.17
  661.1 1.9 copy.30
  (2 shorter events, 0.0 us)
Async XLA Ops:
  7.2 107.6 %copy-start = (bf16[2,512,256]{2,1,0:T(8,128)(2,1)S(1)}, bf16[2,512,256]{2,1,0:T(8,128)(2,1)}, u32[]{:S(2)}) copy-start(bf16[2,512,256]{2,1,0:T(8,128)(2,1)} %param.6) | copy-start | bytes 1572868
  7.2 329.6 %all-reduce.8.cloned.1.call-start = ((), (), s32[]{:S(2)}) async-start(), calls=%async_computation | async-start | bytes 4194304
  117.7 219.0 %slice-start = ((f32[3,16,512]{2,1,0:T(8,128)}), f32[2,16,512]{2,1,0:T(8,128)S(1)}, s32[]{:S(2)}) async-start(f32[3,16,512]{2,1,0:T(8,128)} %param.4), calls=%async_computation.2 | async-start | bytes 131072 | tf_op jit(solution)/shard_map/slice | solution.py:32
  117.7 249.6 %copy-start.1 = (bf16[2,256,512]{2,1,0:T(8,128)(2,1)S(1)}, bf16[2,256,512]{2,1,0:T(8,128)(2,1)}, u32[]{:S(2)}) copy-start(bf16[2,256,512]{2,1,0:T(8,128)(2,1)} %param.5) | copy-start | bytes 1572868
  117.8 541.9 %all-reduce.10.cloned.1.call-start = ((), (), s32[]{:S(2)}) async-start(), calls=%async_computation.1 | async-start | bytes 3145728
Sparse Core Ops, SparseCore 0:
  117.9 218.8 all-reduce.7
  438.3 221.3 all-reduce.9
where the time goes:
time: 670 us
  waiting for transfers between devices  437 us (65%)
  blocking collectives  201 us (30%)
  between operations  14.8 us (2%)
  local copies, waits for them, and re-layouts  9.1 us (1%)
    unnamed x4, waiting for transfers between devices  437 us
    psum x2, blocking collectives, standardize_prior_deviations(): return lax.psum(partial_value, 'row')  133 us
    all_gather x2, blocking collectives, standardize_prior_deviations(): lax.all_gather(partition_height.astype(jnp.bfloat16), 'col', axis=0, tile...  68.6 us
  transfers between devices with their start and end apart: 2, of which 2 were waited for; matrix products, arithmetic and copies ran while one was open for 0% of the time, Pallas kernels for 0%

commit v1 on v0

v1 whole, which is shorter than its diff:
```python
import jax
import jax.numpy as jnp
from jax import lax
from jax.sharding import Mesh, PartitionSpec as P

BF = jnp.bfloat16
F32 = jnp.float32
ROW = ("x", "y")


def swap(pieces, axis):
    return lax.all_to_all(pieces, axis, 0, 0)


def spread(piece, axis, count):
    return swap(jnp.broadcast_to(piece[None], (count,) + piece.shape), axis)


def fold(partial, axis, count):
    rows, width = partial.shape
    pieces = partial.astype(BF).reshape(count, rows // count, width)
    return jnp.sum(swap(pieces, axis).astype(F32), axis=0)


def both_cores(block):
    return lax.all_gather(block, "core", axis=0)


def body(outputs, inverses, former, latter):
    core = lax.axis_index("core")
    here = lax.axis_index(ROW)
    half = outputs.shape[2] // 2
    own = outputs.shape[1]

    def mine(pair):
        width = pair.shape[-1] // 2
        return lax.dynamic_slice_in_dim(pair, core * width, width, axis=pair.ndim - 1)

    def whiten(inverse, rows):
        partial = jnp.dot(inverse, rows, preferred_element_type=F32)
        piece = fold(partial, ROW, 16).astype(BF)
        return spread(piece, ROW, 16).reshape(-1, half)

    def panel(tiles, white):
        depth = tiles.shape[2]
        return jnp.dot(tiles[0], white[:depth], preferred_element_type=F32) + jnp.dot(
            tiles[1], white[depth:], preferred_element_type=F32
        )

    pair = mine(both_cores(outputs[:2]))
    height = 2 * own
    first_rows = pair[:, 0].reshape(height, half)
    second_rows = pair[:, 1].reshape(height, half)
    inverse0 = both_cores(inverses[0]).reshape(-1, inverses.shape[2])
    inverse1 = both_cores(inverses[1]).reshape(-1, inverses.shape[2])
    former0 = both_cores(former[0])
    former1 = both_cores(former[1])
    latter0 = both_cores(latter[0])

    gathered = spread(first_rows.astype(BF), "z", 16).reshape(-1, half)
    white0 = whiten(inverse0, gathered)
    update = fold(panel(former0, white0), "z", 16)
    right = (second_rows - update).astype(BF)
    gathered = spread(right, "z", 16).reshape(-1, half)
    white1 = whiten(inverse1, gathered)
    last = panel(former1, white0) + panel(latter0, white1)

    whole0 = both_cores(white0)
    whole1 = both_cores(white1)
    gram = lax.dot_general(whole0[0], white0, (((0,), (0,)), ((), ())), preferred_element_type=F32)
    gram = gram + lax.dot_general(
        whole1[0], white1, (((0,), (0,)), ((), ())), preferred_element_type=F32
    )
    part = half // 16
    slab = lax.dynamic_slice_in_dim(gram, here * part, part, axis=0).astype(BF)

    pieces = jnp.concatenate(
        [
            last.astype(BF).reshape(16, height, half),
            jnp.broadcast_to(slab[None], (16, part, half)),
        ],
        axis=1,
    )
    summed = jnp.sum(swap(pieces, "z").astype(F32), axis=0)
    ends = swap(summed[:height].reshape(2, own, half), "core")
    trailing = outputs[2:] - jnp.concatenate([ends[0], ends[1]], axis=1)[None]
    slabs = spread(summed[height:], ROW, 16).reshape(-1, half)
    halves = both_cores(slabs)
    projections = jnp.concatenate([halves[0], halves[1]], axis=1)

    rows = white0.shape[0] // 2
    stacked = jnp.stack([whole0, whole1])
    blocks = lax.dynamic_slice_in_dim(stacked, core * rows, rows, axis=2)
    whitened = jnp.concatenate([blocks[:, 0], blocks[:, 1]], axis=2)
    return (whitened, trailing, projections)


def solution(mesh):
    grid = Mesh(mesh.devices.reshape(4, 4, 16, 2), ("x", "y", "z", "core"))
    col = ("z", "core")
    every = ("x", "y", "z", "core")
    in_specs = (P(None, every, None), P(None, col, ROW), P(None, ROW, col), P(None, ROW, col))
    out_specs = (P(None, col, None), P(None, every, None), P())
    return jax.shard_map(body, mesh=grid, in_specs=in_specs, out_specs=out_specs, check_vma=False)
```

time: 670 us -> 197 us (0.29)
  waiting for transfers between devices: 437 us -> 57.4 us
  blocking collectives: 201 us -> 76.2 us
  starting transfers between devices: 0.08 us -> 47.8 us
  between operations: 14.8 us -> 0.96 us
    unnamed x4 -> x0, waiting for transfers between devices: 437 us -> none
    psum x2 -> x0, blocking collectives: 133 us -> none  [standardize_prior_deviations(): return lax.psum(partial_value, 'row')]
    all_to_all x0 -> x8, waiting for transfers between devices: none -> 57.4 us  [swap(): return lax.all_to_all(pieces, axis, 0, 0)]
    all_to_all x0 -> x8, starting transfers between devices: none -> 47.8 us  [swap(): return lax.all_to_all(pieces, axis, 0, 0)]
    all_to_all x0 -> x2, blocking collectives: none -> 25.2 us  [swap(): return lax.all_to_all(pieces, axis, 0, 0)]
    all_gather x2 -> x9, blocking collectives: 68.6 us -> 51 us  [both_cores(): return lax.all_gather(block, 'core', axis=0)]
  transfers between devices with their start and end apart: 2 -> 8, of which waited for: 2 -> 6; matrix products, arithmetic and copies ran while one was open for 0% -> 1% of each run, Pallas kernels for 0% -> 0%
where the time goes in v1:
time: 197 us; the launch traced here: 196 us
  blocking collectives  76.2 us (39%)
  waiting for transfers between devices  57.4 us (29%)
  starting transfers between devices  47.8 us (24%)
  local copies, waits for them, and re-layouts  7.27 us (4%)
  other arithmetic  3.34 us (2%)
  matrix products  2.83 us (1%)
    all_to_all x8, waiting for transfers between devices, swap(): return lax.all_to_all(pieces, axis, 0, 0)  57.4 us
    all_gather x9, blocking collectives, both_cores(): return lax.all_gather(block, 'core', axis=0)  51 us
    all_to_all x8, starting transfers between devices, swap(): return lax.all_to_all(pieces, axis, 0, 0)  47.8 us
    all_to_all x2, blocking collectives, swap(): return lax.all_to_all(pieces, axis, 0, 0)  25.2 us
  transfers between devices with their start and end apart: 8, of which 6 were waited for; matrix products, arithmetic and copies ran while one was open for 1% of the time, Pallas kernels for 0%

profile of v1, /device:TPU:1, one launch (start us, length us, event | category | flops | bytes accessed | tf_op | source)
XLA Modules:
  0.0 195.8 jit_solution(5190549378235407549)
XLA Ops:
  0.6 0.8 slice-done
  1.5 8.5 %all-gather = f32[4,16,512]{2,1,0:T(8,128)S(1)} all-gather(f32[2,16,512]{2,1,0:T(8,128)S(1)} %slice-done), channel_id=2, replica_groups=mesh['x'=4,'y'=4,'z'=16,'core'=2] {'core'}, dimensions={0}, use_global_device_ids=true | all-gather | bytes 196608 | tf_op jit(solution)/shard_map/all_gather | solution.py:26
  10.0 0.7 broadcast_in_dim.14
  10.8 9.5 %all-to-all-start = ((bf16[16,32,256]{2,1,0:T(8,128)(2,1)}), bf16[16,32,256]{2,1,0:T(8,128)(2,1)S(1)}, u32[]{:S(2)}, u32[]{:S(2)}) async-start(bf16[16,32,256]{2,1,0:T(8,128)(2,1)} %broadcast_in_dim.14), calls=%async_computation | async-start | bytes 524288 | tf_op jit(solution)/shard_map/all_to_all | solution.py:12
  20.4 2.4 %all_gather.32 = bf16[2,256,512]{2,1,0:T(8,128)(2,1)S(1)} all-gather(bf16[1,256,512]{2,1,0:T(8,128)(2,1)S(1)} %get-tuple-element.10), channel_id=1, replica_groups=mesh['x'=4,'y'=4,'z'=16,'core'=2] {'core'}, dimensions={0}, use_global_device_ids=true | all-gather | bytes 786432 | tf_op jit(solution)/shard_map/all_gather | solution.py:26
  22.8 11.5 %all-to-all-done = bf16[16,32,256]{2,1,0:T(8,128)(2,1)S(1)} async-done(((bf16[16,32,256]{2,1,0:T(8,128)(2,1)}), bf16[16,32,256]{2,1,0:T(8,128)(2,1)S(1)}, u32[]{:S(2)}, u32[]{:S(2)}) %all-to-all-start) | async-done | bytes 262176 | tf_op jit(solution)/shard_map/all_to_all | solution.py:12
  34.8 13.9 %all_to_all.50 = bf16[16,32,256]{2,1,0:T(8,128)(2,1)S(1)} all-to-all(bf16[16,32,256]{2,1,0:T(8,128)(2,1)S(1)} %bitcast.102), channel_id=1, replica_groups=mesh['x'=4,'y'=4,'z'=16,'core'=2] {'x','y'}, dimensions={0} | all-to-all | bytes 524288 | tf_op jit(solution)/shard_map/all_to_all | solution.py:12
  49.5 3.5 %all-to-all-start.2 = ((bf16[16,32,256]{2,1,0:T(8,128)(2,1)}), bf16[16,32,256]{2,1,0:T(8,128)(2,1)S(1)}, u32[]{:S(2)}, u32[]{:S(2)}) async-start(bf16[16,32,256]{2,1,0:T(8,128)(2,1)} %broadcast_in_dim.15), calls=%async_computation.2 | async-start | bytes 524288 | tf_op jit(solution)/shard_map/all_to_all | solution.py:12
  53.1 8.5 %all_gather.34 = bf16[2,512,256]{2,1,0:T(8,128)(2,1)S(1)} all-gather(bf16[1,512,256]{2,1,0:T(8,128)(2,1)S(1)} %get-tuple-element.6), channel_id=1, replica_groups=mesh['x'=4,'y'=4,'z'=16,'core'=2] {'core'}, dimensions={0}, use_global_device_ids=true | all-gather | bytes 786432 | tf_op jit(solution)/shard_map/all_gather | solution.py:26
  62.2 0.8 copy.13
  63.0 9.1 %all-to-all-start.3 = ((bf16[16,32,256]{2,1,0:T(8,128)(2,1)}), bf16[16,32,256]{2,1,0:T(8,128)(2,1)S(1)}, u32[]{:S(2)}, u32[]{:S(2)}) async-start(bf16[16,32,256]{2,1,0:T(8,128)(2,1)} %bitcast.14), calls=%async_computation.3 | async-start | bytes 524288 | tf_op jit(solution)/shard_map/all_to_all | solution.py:12
  72.2 12.8 %all-to-all-done.3 = bf16[16,32,256]{2,1,0:T(8,128)(2,1)S(1)} async-done(((bf16[16,32,256]{2,1,0:T(8,128)(2,1)}), bf16[16,32,256]{2,1,0:T(8,128)(2,1)S(1)}, u32[]{:S(2)}, u32[]{:S(2)}) %all-to-all-start.3) | async-done | bytes 262176 | tf_op jit(solution)/shard_map/all_to_all | solution.py:12
  85.7 9.0 %all-to-all-start.4 = ((bf16[16,32,256]{2,1,0:T(8,128)(2,1)}), bf16[16,32,256]{2,1,0:T(8,128)(2,1)S(1)}, u32[]{:S(2)}, u32[]{:S(2)}) async-start(bf16[16,32,256]{2,1,0:T(8,128)(2,1)} %broadcast_in_dim.16), calls=%async_computation.4 | async-start | bytes 524288 | tf_op jit(solution)/shard_map/all_to_all | solution.py:12
  94.8 5.3 %all_gather.35 = bf16[2,256,512]{2,1,0:T(8,128)(2,1)S(1)} all-gather(bf16[1,256,512]{2,1,0:T(8,128)(2,1)S(1)} %get-tuple-element.9), channel_id=1, replica_groups=mesh['x'=4,'y'=4,'z'=16,'core'=2] {'core'}, dimensions={0}, use_global_device_ids=true | all-gather | bytes 786432 | tf_op jit(solution)/shard_map/all_gather | solution.py:26
  100.0 2.2 %all_gather.38 = bf16[2,512,256]{2,1,0:T(8,128)(2,1)S(1)} all-gather(bf16[1,512,256]{2,1,0:T(8,128)(2,1)S(1)} %copy-done.2), channel_id=1, replica_groups=mesh['x'=4,'y'=4,'z'=16,'core'=2] {'core'}, dimensions={0}, use_global_device_ids=true | all-gather | bytes 786432 | tf_op jit(solution)/shard_map/all_gather | solution.py:26
  102.2 2.2 %all_gather.37 = bf16[2,512,256]{2,1,0:T(8,128)(2,1)S(1)} all-gather(bf16[1,512,256]{2,1,0:T(8,128)(2,1)S(1)} %get-tuple-element.5), channel_id=1, replica_groups=mesh['x'=4,'y'=4,'z'=16,'core'=2] {'core'}, dimensions={0}, use_global_device_ids=true | all-gather | bytes 786432 | tf_op jit(solution)/shard_map/all_gather | solution.py:26
  104.6 2.9 %all-to-all-done.4 = bf16[16,32,256]{2,1,0:T(8,128)(2,1)S(1)} async-done(((bf16[16,32,256]{2,1,0:T(8,128)(2,1)}), bf16[16,32,256]{2,1,0:T(8,128)(2,1)S(1)}, u32[]{:S(2)}, u32[]{:S(2)}) %all-to-all-start.4) | async-done | bytes 262176 | tf_op jit(solution)/shard_map/all_to_all | solution.py:12
  107.9 0.8 copy.14
  108.7 4.0 %all-to-all-start.5 = ((bf16[16,32,256]{2,1,0:T(8,128)(2,1)}), bf16[16,32,256]{2,1,0:T(8,128)(2,1)S(1)}, u32[]{:S(2)}, u32[]{:S(2)}) async-start(bf16[16,32,256]{2,1,0:T(8,128)(2,1)} %bitcast.18), calls=%async_computation.5 | async-start | bytes 524288 | tf_op jit(solution)/shard_map/all_to_all | solution.py:12
  113.0 7.0 %all-to-all-done.5 = bf16[16,32,256]{2,1,0:T(8,128)(2,1)S(1)} async-done(((bf16[16,32,256]{2,1,0:T(8,128)(2,1)}), bf16[16,32,256]{2,1,0:T(8,128)(2,1)S(1)}, u32[]{:S(2)}, u32[]{:S(2)}) %all-to-all-start.5) | async-done | bytes 262176 | tf_op jit(solution)/shard_map/all_to_all | solution.py:12
  120.9 3.5 %all-to-all-start.6 = ((bf16[16,32,256]{2,1,0:T(8,128)(2,1)}), bf16[16,32,256]{2,1,0:T(8,128)(2,1)S(1)}, u32[]{:S(2)}, u32[]{:S(2)}) async-start(bf16[16,32,256]{2,1,0:T(8,128)(2,1)} %broadcast_in_dim.17), calls=%async_computation.6 | async-start | bytes 524288 | tf_op jit(solution)/shard_map/all_to_all | solution.py:12
  124.4 10.1 %all_gather.33 = bf16[2,512,256]{2,1,0:T(8,128)(2,1)S(1)} all-gather(bf16[1,512,256]{2,1,0:T(8,128)(2,1)S(1)} %bitcast.88), channel_id=1, replica_groups=mesh['x'=4,'y'=4,'z'=16,'core'=2] {'core'}, dimensions={0}, use_global_device_ids=true | all-gather | bytes 786432 | tf_op jit(solution)/shard_map/all_gather | solution.py:26
  135.5 8.2 %all_gather.36 = bf16[2,512,256]{2,1,0:T(8,128)(2,1)S(1)} all-gather(bf16[1,512,256]{2,1,0:T(8,128)(2,1)S(1)} %bitcast.90), channel_id=1, replica_groups=mesh['x'=4,'y'=4,'z'=16,'core'=2] {'core'}, dimensions={0}, use_global_device_ids=true | all-gather | bytes 786432 | tf_op jit(solution)/shard_map/all_gather | solution.py:26
  144.0 0.8 pad_maximum_fusion.2
  144.8 5.3 %all-to-all-start.7 = ((bf16[16,48,256]{2,1,0:T(8,128)(2,1)}), bf16[16,48,256]{2,1,0:T(8,128)(2,1)S(1)}, u32[]{:S(2)}, u32[]{:S(2)}) async-start(bf16[16,48,256]{2,1,0:T(8,128)(2,1)} %pad_maximum_fusion.2), calls=%async_computation.7 | async-start | bytes 786432 | tf_op jit(solution)/shard_map/all_to_all | solution.py:12
  150.2 0.8 pad_maximum_fusion
  151.0 16.3 %all-to-all-done.7 = bf16[16,48,256]{2,1,0:T(8,128)(2,1)S(1)} async-done(((bf16[16,48,256]{2,1,0:T(8,128)(2,1)}), bf16[16,48,256]{2,1,0:T(8,128)(2,1)S(1)}, u32[]{:S(2)}, u32[]{:S(2)}) %all-to-all-start.7) | async-done | bytes 393248 | tf_op jit(solution)/shard_map/all_to_all | solution.py:12
  168.0 11.3 %all_to_all.51 = f32[2,16,256]{2,1,0:T(8,128)S(1)} all-to-all(f32[2,16,256]{2,1,0:T(8,128)S(1)} %bitcast.109), channel_id=1, replica_groups=mesh['x'=4,'y'=4,'z'=16,'core'=2] {'core'}, dimensions={0} | all-to-all | bytes 65536 | tf_op jit(solution)/shard_map/all_to_all | solution.py:12
  180.0 3.7 %all-to-all-start.9 = ((f32[16,16,256]{2,1,0:T(8,128)}), f32[16,16,256]{2,1,0:T(8,128)S(1)}, u32[]{:S(2)}, u32[]{:S(2)}) async-start(f32[16,16,256]{2,1,0:T(8,128)} %broadcast_in_dim.20), calls=%async_computation.9 | async-start | bytes 524288 | tf_op jit(solution)/shard_map/all_to_all | solution.py:12
  184.3 6.9 %all-to-all-done.9 = f32[16,16,256]{2,1,0:T(8,128)S(1)} async-done(((f32[16,16,256]{2,1,0:T(8,128)}), f32[16,16,256]{2,1,0:T(8,128)S(1)}, u32[]{:S(2)}, u32[]{:S(2)}) %all-to-all-start.9) | async-done | bytes 262176 | tf_op jit(solution)/shard_map/all_to_all | solution.py:12
  191.3 3.6 %all_gather.39 = f32[2,256,256]{2,1,0:T(8,128)S(1)} all-gather(f32[1,256,256]{2,1,0:T(8,128)S(1)} %bitcast.100), channel_id=1, replica_groups=mesh['x'=4,'y'=4,'z'=16,'core'=2] {'core'}, dimensions={0}, use_global_device_ids=true | all-gather | bytes 786432 | tf_op jit(solution)/shard_map/all_gather | solution.py:26
  194.9 0.9 pad_maximum_fusion.1
  (50 shorter events, 7.7 us)
Async XLA Ops:
  0.6 0.8 slice-start
  1.5 18.8 %copy-start = (bf16[2,256,512]{2,1,0:T(8,128)(2,1)S(1)}, bf16[2,256,512]{2,1,0:T(8,128)(2,1)}, u32[]{:S(2)}) copy-start(bf16[2,256,512]{2,1,0:T(8,128)(2,1)} %param.5) | copy-start | bytes 1572868
  10.8 23.6 %all-to-all-start = ((bf16[16,32,256]{2,1,0:T(8,128)(2,1)}), bf16[16,32,256]{2,1,0:T(8,128)(2,1)S(1)}, u32[]{:S(2)}, u32[]{:S(2)}) async-start(bf16[16,32,256]{2,1,0:T(8,128)(2,1)} %broadcast_in_dim.14), calls=%async_computation | async-start | bytes 524288 | tf_op jit(solution)/shard_map/all_to_all | solution.py:12
  48.7 4.3 %copy-start.1 = (bf16[2,512,256]{2,1,0:T(8,128)(2,1)S(1)}, bf16[2,512,256]{2,1,0:T(8,128)(2,1)}, u32[]{:S(2)}) copy-start(bf16[2,512,256]{2,1,0:T(8,128)(2,1)} %param.6) | copy-start | bytes 1572868
  49.5 12.1 %all-to-all-start.2 = ((bf16[16,32,256]{2,1,0:T(8,128)(2,1)}), bf16[16,32,256]{2,1,0:T(8,128)(2,1)S(1)}, u32[]{:S(2)}, u32[]{:S(2)}) async-start(bf16[16,32,256]{2,1,0:T(8,128)(2,1)} %broadcast_in_dim.15), calls=%async_computation.2 | async-start | bytes 524288 | tf_op jit(solution)/shard_map/all_to_all | solution.py:12
  63.0 21.9 %all-to-all-start.3 = ((bf16[16,32,256]{2,1,0:T(8,128)(2,1)}), bf16[16,32,256]{2,1,0:T(8,128)(2,1)S(1)}, u32[]{:S(2)}, u32[]{:S(2)}) async-start(bf16[16,32,256]{2,1,0:T(8,128)(2,1)} %bitcast.14), calls=%async_computation.3 | async-start | bytes 524288 | tf_op jit(solution)/shard_map/all_to_all | solution.py:12
  85.7 21.8 %all-to-all-start.4 = ((bf16[16,32,256]{2,1,0:T(8,128)(2,1)}), bf16[16,32,256]{2,1,0:T(8,128)(2,1)S(1)}, u32[]{:S(2)}, u32[]{:S(2)}) async-start(bf16[16,32,256]{2,1,0:T(8,128)(2,1)} %broadcast_in_dim.16), calls=%async_computation.4 | async-start | bytes 524288 | tf_op jit(solution)/shard_map/all_to_all | solution.py:12
  94.8 5.3 %copy-start.2 = (bf16[1,512,256]{2,1,0:T(8,128)(2,1)S(1)}, bf16[1,512,256]{2,1,0:T(8,128)(2,1)}, u32[]{:S(2)}) copy-start(bf16[1,512,256]{2,1,0:T(8,128)(2,1)} %param.7) | copy-start | bytes 786436
  108.7 11.4 %all-to-all-start.5 = ((bf16[16,32,256]{2,1,0:T(8,128)(2,1)}), bf16[16,32,256]{2,1,0:T(8,128)(2,1)S(1)}, u32[]{:S(2)}, u32[]{:S(2)}) async-start(bf16[16,32,256]{2,1,0:T(8,128)(2,1)} %bitcast.18), calls=%async_computation.5 | async-start | bytes 524288 | tf_op jit(solution)/shard_map/all_to_all | solution.py:12
  120.9 13.9 %all-to-all-start.6 = ((bf16[16,32,256]{2,1,0:T(8,128)(2,1)}), bf16[16,32,256]{2,1,0:T(8,128)(2,1)S(1)}, u32[]{:S(2)}, u32[]{:S(2)}) async-start(bf16[16,32,256]{2,1,0:T(8,128)(2,1)} %broadcast_in_dim.17), calls=%async_computation.6 | async-start | bytes 524288 | tf_op jit(solution)/shard_map/all_to_all | solution.py:12
  144.8 22.5 %all-to-all-start.7 = ((bf16[16,48,256]{2,1,0:T(8,128)(2,1)}), bf16[16,48,256]{2,1,0:T(8,128)(2,1)S(1)}, u32[]{:S(2)}, u32[]{:S(2)}) async-start(bf16[16,48,256]{2,1,0:T(8,128)(2,1)} %pad_maximum_fusion.2), calls=%async_computation.7 | async-start | bytes 786432 | tf_op jit(solution)/shard_map/all_to_all | solution.py:12
  167.4 0.6 copy-start.4
  168.0 11.3 %slice-start.1 = ((f32[48,256]{1,0:T(8,128)}), f32[16,256]{1,0:T(8,128)S(1)}, s32[]{:S(2)}) async-start(f32[48,256]{1,0:T(8,128)} %copy-done.4), calls=%async_computation.11 | async-start | bytes 32768 | tf_op jit(solution)/shard_map/slice | solution.py:87
  180.0 3.7 %copy-start.3 = (f32[3,16,512]{2,1,0:T(8,128)S(1)}, f32[3,16,512]{2,1,0:T(8,128)}, u32[]{:S(2)}) copy-start(f32[3,16,512]{2,1,0:T(8,128)} %param.4) | copy-start | bytes 294916
  180.0 11.3 %all-to-all-start.9 = ((f32[16,16,256]{2,1,0:T(8,128)}), f32[16,16,256]{2,1,0:T(8,128)S(1)}, u32[]{:S(2)}, u32[]{:S(2)}) async-start(f32[16,16,256]{2,1,0:T(8,128)} %broadcast_in_dim.20), calls=%async_computation.9 | async-start | bytes 524288 | tf_op jit(solution)/shard_map/all_to_all | solution.py:12

commit v2 on v1

v2 whole, which is shorter than its diff:
```python
import jax
import jax.numpy as jnp
from jax import lax
from jax.sharding import Mesh, PartitionSpec as P

BF = jnp.bfloat16
F32 = jnp.float32
ROW = ("x", "y")
COL = ("z", "core")
together = lax.optimization_barrier


def swap(pieces, axis):
    return lax.all_to_all(pieces, axis, 0, 0)


def spread(piece, axis, count):
    return swap(jnp.broadcast_to(piece[None], (count,) + piece.shape), axis)


def cut(partial, count):
    rows, width = partial.shape
    return partial.astype(BF).reshape(count, rows // count, width)


def total(pieces):
    return together(jnp.sum(pieces.astype(F32), axis=0))


def both_cores(block):
    return lax.all_gather(block, "core", axis=0)


def body(outputs, inverses, former, latter):
    core = lax.axis_index("core")
    here = lax.axis_index(ROW)
    half = outputs.shape[2] // 2
    own = outputs.shape[1]
    height = 2 * own

    def whiten(inverse, rows):
        partial = jnp.dot(inverse, rows, preferred_element_type=F32)
        piece = total(swap(cut(partial, 16), ROW)).astype(BF)
        return spread(piece, ROW, 16).reshape(-1, half)

    def panel(tiles, white):
        depth = tiles.shape[2]
        return jnp.dot(tiles[0], white[:depth], preferred_element_type=F32) + jnp.dot(
            tiles[1], white[depth:], preferred_element_type=F32
        )

    def gram(whole, white):
        return lax.dot_general(
            whole[0], white, (((0,), (0,)), ((), ())), preferred_element_type=F32
        )

    def block(whole):
        rows = whole.shape[1] // 2
        mine = lax.dynamic_slice_in_dim(whole, core * rows, rows, axis=1)
        return jnp.concatenate([mine[0], mine[1]], axis=1)

    first = outputs[0].astype(BF)
    first = jnp.stack([first[:, :half], first[:, half:]])
    pieces = jnp.broadcast_to(first[None], (16,) + first.shape).reshape(32, own, half)
    gathered = swap(pieces, COL).reshape(-1, half)
    (gathered, inverse0, inverse1, former0, former1, latter0, pair) = together(
        (
            gathered,
            both_cores(inverses[0]),
            both_cores(inverses[1]),
            both_cores(former[0]),
            both_cores(former[1]),
            both_cores(latter[0]),
            both_cores(outputs[1]),
        )
    )
    second = lax.dynamic_slice_in_dim(pair, core * half, half, axis=2).reshape(height, half)

    white0 = whiten(inverse0.reshape(-1, inverse0.shape[2]), gathered)
    pieces = swap(cut(panel(former0, white0), 16), "z")
    whole0 = both_cores(white0)
    pieces, last, slabs0, block0 = together(
        (pieces, panel(former1, white0), gram(whole0, white0), block(whole0))
    )
    right = (second - total(pieces)).astype(BF)
    gathered = spread(right, "z", 16).reshape(-1, half)
    white1 = whiten(inverse1.reshape(-1, inverse1.shape[2]), gathered)

    whole1 = both_cores(white1)
    last = last + panel(latter0, white1)
    slabs = slabs0 + gram(whole1, white1)
    part = half // 16
    slab = lax.dynamic_slice_in_dim(slabs, here * part, part, axis=0).astype(BF)
    pieces = jnp.concatenate(
        [cut(last, 16), jnp.broadcast_to(slab[None], (16, part, half))], axis=1
    )
    pieces, whole1 = together((swap(pieces, "z"), whole1))
    slab = total(pieces[:, height:])
    ends = total(pieces[:, :height])
    ends = lax.dynamic_slice_in_dim(both_cores(ends), core * own, own, axis=1)
    trailing = outputs[2:] - jnp.concatenate([ends[0], ends[1]], axis=1)[None]
    parts, trailing = together((spread(slab, ROW + ("core",), 32), trailing))
    parts = parts.reshape(16, 2, part, half)
    projections = jnp.concatenate(
        [parts[:, 0].reshape(half, half), parts[:, 1].reshape(half, half)], axis=1
    )
    whitened = jnp.stack([block0, block(whole1)])
    return (whitened, trailing, projections)


def solution(mesh):
    grid = Mesh(mesh.devices.reshape(4, 4, 16, 2), ("x", "y", "z", "core"))
    every = ("x", "y", "z", "core")
    in_specs = (P(None, every, None), P(None, COL, ROW), P(None, ROW, COL), P(None, ROW, COL))
    out_specs = (P(None, COL, None), P(None, every, None), P())
    return jax.shard_map(body, mesh=grid, in_specs=in_specs, out_specs=out_specs, check_vma=False)
```

time: 197 us -> 192 us (0.975)
  starting transfers between devices: 47.8 us -> 44.4 us
  blocking collectives: 76.2 us -> 78.7 us
  local copies, waits for them, and re-layouts: 7.27 us -> 4.92 us
    all_to_all x2 -> x3, blocking collectives: 25.2 us -> 47.6 us  [swap(): return lax.all_to_all(pieces, axis, 0, 0)]
    all_gather x9, blocking collectives: 51 us -> 31.1 us  [both_cores(): return lax.all_gather(block, 'core', axis=0)]
    all_to_all x8 -> x6, starting transfers between devices: 47.8 us -> 44.4 us  [swap(): return lax.all_to_all(pieces, axis, 0, 0)]
    all_to_all x8 -> x6, waiting for transfers between devices: 57.4 us -> 55.5 us  [swap(): return lax.all_to_all(pieces, axis, 0, 0)]
  transfers between devices with their start and end apart: 8 -> 6, of which waited for: 6 -> 6; matrix products, arithmetic and copies ran while one was open for 1% -> 1% of each run, Pallas kernels for 0% -> 0%
where the time goes in v2:
time: 192 us; the launch traced here: 191 us
  blocking collectives  78.7 us (41%)
  waiting for transfers between devices  55.5 us (29%)
  starting transfers between devices  44.4 us (23%)
  local copies, waits for them, and re-layouts  4.92 us (3%)
  other arithmetic  3.34 us (2%)
  matrix products  3.17 us (2%)
    all_to_all x6, waiting for transfers between devices, swap(): return lax.all_to_all(pieces, axis, 0, 0)  55.5 us
    all_to_all x3, blocking collectives, swap(): return lax.all_to_all(pieces, axis, 0, 0)  47.6 us
    all_to_all x6, starting transfers between devices, swap(): return lax.all_to_all(pieces, axis, 0, 0)  44.4 us
    all_gather x9, blocking collectives, both_cores(): return lax.all_gather(block, 'core', axis=0)  31.1 us
  transfers between devices with their start and end apart: 6, of which 6 were waited for; matrix products, arithmetic and copies ran while one was open for 1% of the time, Pallas kernels for 0%

profile of v2, /device:TPU:1, one launch (start us, length us, event | category | flops | bytes accessed | tf_op | source)
XLA Modules:
  0.0 190.9 jit_solution(6897872838893181068)
XLA Ops:
  0.6 0.8 fusion.22
  1.5 0.7 broadcast_in_dim.14
  2.2 16.8 %all-to-all-start = ((bf16[32,16,256]{2,1,0:T(8,128)(2,1)}), bf16[32,16,256]{2,1,0:T(8,128)(2,1)S(1)}, u32[]{:S(2)}, u32[]{:S(2)}) async-start(bf16[32,16,256]{2,1,0:T(8,128)(2,1)} %bitcast.3), calls=%async_computation | async-start | bytes 524288 | tf_op jit(solution)/shard_map/all_to_all | solution.py:14
  19.0 0.7 slice-done
  19.8 1.8 all_gather.35
  21.6 2.2 %all_gather.30 = bf16[2,256,512]{2,1,0:T(8,128)(2,1)S(1)} all-gather(bf16[1,256,512]{2,1,0:T(8,128)(2,1)S(1)} %get-tuple-element.42), channel_id=1, replica_groups=mesh['x'=4,'y'=4,'z'=16,'core'=2] {'core'}, dimensions={0}, use_global_device_ids=true | all-gather | bytes 786432 | tf_op jit(solution)/shard_map/all_gather | solution.py:31
  23.8 2.3 %all_gather.31 = bf16[2,256,512]{2,1,0:T(8,128)(2,1)S(1)} all-gather(bf16[1,256,512]{2,1,0:T(8,128)(2,1)S(1)} %get-tuple-element.41), channel_id=1, replica_groups=mesh['x'=4,'y'=4,'z'=16,'core'=2] {'core'}, dimensions={0}, use_global_device_ids=true | all-gather | bytes 786432 | tf_op jit(solution)/shard_map/all_gather | solution.py:31
  26.1 2.2 %all_gather.32 = bf16[2,512,256]{2,1,0:T(8,128)(2,1)S(1)} all-gather(bf16[1,512,256]{2,1,0:T(8,128)(2,1)S(1)} %get-tuple-element.40), channel_id=1, replica_groups=mesh['x'=4,'y'=4,'z'=16,'core'=2] {'core'}, dimensions={0}, use_global_device_ids=true | all-gather | bytes 786432 | tf_op jit(solution)/shard_map/all_gather | solution.py:31
  28.3 2.3 %all_gather.33 = bf16[2,512,256]{2,1,0:T(8,128)(2,1)S(1)} all-gather(bf16[1,512,256]{2,1,0:T(8,128)(2,1)S(1)} %get-tuple-element.39), channel_id=1, replica_groups=mesh['x'=4,'y'=4,'z'=16,'core'=2] {'core'}, dimensions={0}, use_global_device_ids=true | all-gather | bytes 786432 | tf_op jit(solution)/shard_map/all_gather | solution.py:31
  30.6 2.2 %all_gather.34 = bf16[2,512,256]{2,1,0:T(8,128)(2,1)S(1)} all-gather(bf16[1,512,256]{2,1,0:T(8,128)(2,1)S(1)} %copy-done.2), channel_id=1, replica_groups=mesh['x'=4,'y'=4,'z'=16,'core'=2] {'core'}, dimensions={0}, use_global_device_ids=true | all-gather | bytes 786432 | tf_op jit(solution)/shard_map/all_gather | solution.py:31
  32.8 8.2 %all-to-all-done = bf16[32,16,256]{2,1,0:T(8,128)(2,1)S(1)} async-done(((bf16[32,16,256]{2,1,0:T(8,128)(2,1)}), bf16[32,16,256]{2,1,0:T(8,128)(2,1)S(1)}, u32[]{:S(2)}, u32[]{:S(2)}) %all-to-all-start) | async-done | bytes 262176 | tf_op jit(solution)/shard_map/all_to_all | solution.py:14
  41.3 14.0 %all_to_all.45 = bf16[16,32,256]{2,1,0:T(8,128)(2,1)S(1)} all-to-all(bf16[16,32,256]{2,1,0:T(8,128)(2,1)S(1)} %bitcast.100), channel_id=1, replica_groups=mesh['x'=4,'y'=4,'z'=16,'core'=2] {'x','y'}, dimensions={0} | all-to-all | bytes 524288 | tf_op jit(solution)/shard_map/all_to_all | solution.py:14
  56.1 3.5 %all-to-all-start.2 = ((bf16[16,32,256]{2,1,0:T(8,128)(2,1)}), bf16[16,32,256]{2,1,0:T(8,128)(2,1)S(1)}, u32[]{:S(2)}, u32[]{:S(2)}) async-start(bf16[16,32,256]{2,1,0:T(8,128)(2,1)} %broadcast_in_dim.15), calls=%async_computation.2 | async-start | bytes 524288 | tf_op jit(solution)/shard_map/all_to_all | solution.py:14
  59.6 7.4 %all-to-all-done.2 = bf16[16,32,256]{2,1,0:T(8,128)(2,1)S(1)} async-done(((bf16[16,32,256]{2,1,0:T(8,128)(2,1)}), bf16[16,32,256]{2,1,0:T(8,128)(2,1)S(1)}, u32[]{:S(2)}, u32[]{:S(2)}) %all-to-all-start.2) | async-done | bytes 262176 | tf_op jit(solution)/shard_map/all_to_all | solution.py:14
  67.3 0.9 fusion.2
  68.3 4.0 %all-to-all-start.3 = ((bf16[16,32,256]{2,1,0:T(8,128)(2,1)}), bf16[16,32,256]{2,1,0:T(8,128)(2,1)S(1)}, u32[]{:S(2)}, u32[]{:S(2)}) async-start(bf16[16,32,256]{2,1,0:T(8,128)(2,1)} %bitcast.11), calls=%async_computation.3 | async-start | bytes 524288 | tf_op jit(solution)/shard_map/all_to_all | solution.py:14
  72.2 4.8 %all_gather.36 = bf16[2,512,256]{2,1,0:T(8,128)(2,1)S(1)} all-gather(bf16[1,512,256]{2,1,0:T(8,128)(2,1)S(1)} %bitcast.86), channel_id=1, replica_groups=mesh['x'=4,'y'=4,'z'=16,'core'=2] {'core'}, dimensions={0}, use_global_device_ids=true | all-gather | bytes 786432 | tf_op jit(solution)/shard_map/all_gather | solution.py:31
  77.8 7.2 %all-to-all-done.3 = bf16[16,32,256]{2,1,0:T(8,128)(2,1)S(1)} async-done(((bf16[16,32,256]{2,1,0:T(8,128)(2,1)}), bf16[16,32,256]{2,1,0:T(8,128)(2,1)S(1)}, u32[]{:S(2)}, u32[]{:S(2)}) %all-to-all-start.3) | async-done | bytes 262176 | tf_op jit(solution)/shard_map/all_to_all | solution.py:14
  85.1 22.5 %all_to_all.46 = bf16[16,32,256]{2,1,0:T(8,128)(2,1)S(1)} all-to-all(bf16[16,32,256]{2,1,0:T(8,128)(2,1)S(1)} %broadcast_in_dim.16), channel_id=1, replica_groups=mesh['x'=4,'y'=4,'z'=16,'core'=2] {'z'}, dimensions={0} | all-to-all | bytes 524288 | tf_op jit(solution)/shard_map/all_to_all | solution.py:14
  108.0 11.0 %all_to_all.47 = bf16[16,32,256]{2,1,0:T(8,128)(2,1)S(1)} all-to-all(bf16[16,32,256]{2,1,0:T(8,128)(2,1)S(1)} %bitcast.102), channel_id=1, replica_groups=mesh['x'=4,'y'=4,'z'=16,'core'=2] {'x','y'}, dimensions={0} | all-to-all | bytes 524288 | tf_op jit(solution)/shard_map/all_to_all | solution.py:14
  119.8 3.5 %all-to-all-start.6 = ((bf16[16,32,256]{2,1,0:T(8,128)(2,1)}), bf16[16,32,256]{2,1,0:T(8,128)(2,1)S(1)}, u32[]{:S(2)}, u32[]{:S(2)}) async-start(bf16[16,32,256]{2,1,0:T(8,128)(2,1)} %broadcast_in_dim.17), calls=%async_computation.6 | async-start | bytes 524288 | tf_op jit(solution)/shard_map/all_to_all | solution.py:14
  123.3 7.3 %all-to-all-done.6 = bf16[16,32,256]{2,1,0:T(8,128)(2,1)S(1)} async-done(((bf16[16,32,256]{2,1,0:T(8,128)(2,1)}), bf16[16,32,256]{2,1,0:T(8,128)(2,1)S(1)}, u32[]{:S(2)}, u32[]{:S(2)}) %all-to-all-start.6) | async-done | bytes 262176 | tf_op jit(solution)/shard_map/all_to_all | solution.py:14
  130.6 11.5 %all_gather.37 = bf16[2,512,256]{2,1,0:T(8,128)(2,1)S(1)} all-gather(bf16[1,512,256]{2,1,0:T(8,128)(2,1)S(1)} %bitcast.88), channel_id=1, replica_groups=mesh['x'=4,'y'=4,'z'=16,'core'=2] {'core'}, dimensions={0}, use_global_device_ids=true | all-gather | bytes 786432 | tf_op jit(solution)/shard_map/all_gather | solution.py:31
  142.9 0.8 pad_maximum_fusion.2
  143.6 5.1 %all-to-all-start.7 = ((bf16[16,48,256]{2,1,0:T(8,128)(2,1)}), bf16[16,48,256]{2,1,0:T(8,128)(2,1)S(1)}, u32[]{:S(2)}, u32[]{:S(2)}) async-start(bf16[16,48,256]{2,1,0:T(8,128)(2,1)} %pad_maximum_fusion.2), calls=%async_computation.7 | async-start | bytes 786432 | tf_op jit(solution)/shard_map/all_to_all | solution.py:14
  148.8 17.2 %all-to-all-done.7 = bf16[16,48,256]{2,1,0:T(8,128)(2,1)S(1)} async-done(((bf16[16,48,256]{2,1,0:T(8,128)(2,1)}), bf16[16,48,256]{2,1,0:T(8,128)(2,1)S(1)}, u32[]{:S(2)}, u32[]{:S(2)}) %all-to-all-start.7) | async-done | bytes 393248 | tf_op jit(solution)/shard_map/all_to_all | solution.py:14
  166.1 0.9 broadcast_in_dim.19
  166.9 11.5 %all-to-all-start.8 = ((f32[32,16,256]{2,1,0:T(8,128)}), f32[32,16,256]{2,1,0:T(8,128)S(1)}, u32[]{:S(2)}, u32[]{:S(2)}) async-start(f32[32,16,256]{2,1,0:T(8,128)} %broadcast_in_dim.19), calls=%async_computation.8 | async-start | bytes 1048576 | tf_op jit(solution)/shard_map/all_to_all | solution.py:14
  178.4 1.9 all-gather
  180.3 0.8 pad_maximum_fusion
  181.8 8.2 %all-to-all-done.8 = f32[32,16,256]{2,1,0:T(8,128)S(1)} async-done(((f32[32,16,256]{2,1,0:T(8,128)}), f32[32,16,256]{2,1,0:T(8,128)S(1)}, u32[]{:S(2)}, u32[]{:S(2)}) %all-to-all-start.8) | async-done | bytes 524320 | tf_op jit(solution)/shard_map/all_to_all | solution.py:14
  190.1 0.9 pad_maximum_fusion.1
  (43 shorter events, 4.9 us)
Async XLA Ops:
  0.6 18.3 %copy-start = (bf16[2,256,512]{2,1,0:T(8,128)(2,1)S(1)}, bf16[2,256,512]{2,1,0:T(8,128)(2,1)}, u32[]{:S(2)}) copy-start(bf16[2,256,512]{2,1,0:T(8,128)(2,1)} %param.5) | copy-start | bytes 1572868
  2.2 38.8 %all-to-all-start = ((bf16[32,16,256]{2,1,0:T(8,128)(2,1)}), bf16[32,16,256]{2,1,0:T(8,128)(2,1)S(1)}, u32[]{:S(2)}, u32[]{:S(2)}) async-start(bf16[32,16,256]{2,1,0:T(8,128)(2,1)} %bitcast.3), calls=%async_computation | async-start | bytes 524288 | tf_op jit(solution)/shard_map/all_to_all | solution.py:14
  19.0 0.8 slice-start
  23.8 2.3 %copy-start.1 = (bf16[2,512,256]{2,1,0:T(8,128)(2,1)S(1)}, bf16[2,512,256]{2,1,0:T(8,128)(2,1)}, u32[]{:S(2)}) copy-start(bf16[2,512,256]{2,1,0:T(8,128)(2,1)} %param.6) | copy-start | bytes 1572868
  28.3 2.3 %copy-start.2 = (bf16[1,512,256]{2,1,0:T(8,128)(2,1)S(1)}, bf16[1,512,256]{2,1,0:T(8,128)(2,1)}, u32[]{:S(2)}) copy-start(bf16[1,512,256]{2,1,0:T(8,128)(2,1)} %param.7) | copy-start | bytes 786436
  56.1 11.0 %all-to-all-start.2 = ((bf16[16,32,256]{2,1,0:T(8,128)(2,1)}), bf16[16,32,256]{2,1,0:T(8,128)(2,1)S(1)}, u32[]{:S(2)}, u32[]{:S(2)}) async-start(bf16[16,32,256]{2,1,0:T(8,128)(2,1)} %broadcast_in_dim.15), calls=%async_computation.2 | async-start | bytes 524288 | tf_op jit(solution)/shard_map/all_to_all | solution.py:14
  68.3 16.8 %all-to-all-start.3 = ((bf16[16,32,256]{2,1,0:T(8,128)(2,1)}), bf16[16,32,256]{2,1,0:T(8,128)(2,1)S(1)}, u32[]{:S(2)}, u32[]{:S(2)}) async-start(bf16[16,32,256]{2,1,0:T(8,128)(2,1)} %bitcast.11), calls=%async_computation.3 | async-start | bytes 524288 | tf_op jit(solution)/shard_map/all_to_all | solution.py:14
  119.8 10.8 %all-to-all-start.6 = ((bf16[16,32,256]{2,1,0:T(8,128)(2,1)}), bf16[16,32,256]{2,1,0:T(8,128)(2,1)S(1)}, u32[]{:S(2)}, u32[]{:S(2)}) async-start(bf16[16,32,256]{2,1,0:T(8,128)(2,1)} %broadcast_in_dim.17), calls=%async_computation.6 | async-start | bytes 524288 | tf_op jit(solution)/shard_map/all_to_all | solution.py:14
  143.6 22.3 %all-to-all-start.7 = ((bf16[16,48,256]{2,1,0:T(8,128)(2,1)}), bf16[16,48,256]{2,1,0:T(8,128)(2,1)S(1)}, u32[]{:S(2)}, u32[]{:S(2)}) async-start(bf16[16,48,256]{2,1,0:T(8,128)(2,1)} %pad_maximum_fusion.2), calls=%async_computation.7 | async-start | bytes 786432 | tf_op jit(solution)/shard_map/all_to_all | solution.py:14
  166.9 23.1 %all-to-all-start.8 = ((f32[32,16,256]{2,1,0:T(8,128)}), f32[32,16,256]{2,1,0:T(8,128)S(1)}, u32[]{:S(2)}, u32[]{:S(2)}) async-start(f32[32,16,256]{2,1,0:T(8,128)} %broadcast_in_dim.19), calls=%async_computation.8 | async-start | bytes 1048576 | tf_op jit(solution)/shard_map/all_to_all | solution.py:14
  180.3 0.9 copy-start.3

commit v3 on v2

v3 whole, which is shorter than its diff:
```python
import jax
import jax.numpy as jnp
from jax import lax
from jax.sharding import Mesh, PartitionSpec as P

BF = jnp.bfloat16
F32 = jnp.float32
ROW = ("x", "y")
QUAD = ("pair", "core")
together = lax.optimization_barrier


def dot(a, b):
    return jnp.dot(a, b, preferred_element_type=F32)


def swap(pieces, axis):
    return lax.all_to_all(pieces, axis, 0, 0)


def spread(piece, axis, count):
    return swap(jnp.broadcast_to(piece[None], (count,) + piece.shape), axis)


def cut(partial, count):
    rows, width = partial.shape
    return partial.astype(BF).reshape(count, rows // count, width)


def total(pieces):
    return together(jnp.sum(pieces.astype(F32), axis=0))


def both_cores(block):
    return lax.all_gather(block, "core", axis=0)


def trade(block):
    return lax.ppermute(block, "pair", [(0, 1), (1, 0)])


def body(outputs, inverses, former, latter):
    core = lax.axis_index("core")
    side = lax.axis_index("pair")
    here = lax.axis_index(ROW)
    own = outputs.shape[1]
    half = outputs.shape[2] // 2
    quarter = half // 2
    tall = 2 * inverses.shape[1]

    def near(rows):
        depth = rows.shape[0] // 2
        return lax.dynamic_slice_in_dim(rows, side * depth, depth, axis=0)

    def far(rows):
        depth = rows.shape[0] // 2
        return lax.dynamic_slice_in_dim(rows, (1 - side) * depth, depth, axis=0)

    def beside(kept, got):
        return jnp.where(
            side == 0,
            jnp.concatenate([kept, got], axis=1),
            jnp.concatenate([got, kept], axis=1),
        )

    def panel(tiles, rows):
        depth = tiles.shape[2]
        return dot(tiles[0], rows[:depth]) + dot(tiles[1], rows[depth:])

    def panels(kept, got, white):
        return panel(kept, near(white)) + panel(got, far(white))

    def upright(pieces):
        return pieces.reshape(16, 2, -1, quarter).swapaxes(0, 1).reshape(2 * tall, quarter)

    def columns(whole):
        rows = whole.shape[1] // 2
        mine = lax.dynamic_slice_in_dim(whole, core * rows, rows, axis=1)
        return jnp.concatenate([mine[0], mine[1]], axis=1)

    first = both_cores(outputs[0].astype(BF))
    first = lax.dynamic_slice_in_dim(first, core * half, half, axis=2).reshape(2 * own, half)
    gathered = spread(first, ("eight", "pair"), 16).reshape(-1, half)
    given = trade(outputs[1])
    given = jnp.where(side == 0, jnp.stack([outputs[1], given]), jnp.stack([given, outputs[1]]))
    given = lax.dynamic_slice_in_dim(
        both_cores(given), core * half + side * quarter, quarter, axis=3
    )
    second = given.swapaxes(0, 1).reshape(4 * own, quarter)
    gathered, inverse0, second, former0, inverse1 = together(
        (gathered, both_cores(inverses[0]), second, former[0], inverses[1])
    )

    partial = dot(inverse0.reshape(tall, -1), gathered)
    pieces = swap(cut(partial, 16), ROW)
    pieces, former0_near, former0_got, inverse1_got, former1, latter0 = together(
        (pieces, both_cores(former0), trade(former0), trade(inverse1), former[1], latter[0])
    )
    piece = total(pieces).astype(BF)
    piece = jnp.stack([piece[:, :quarter], piece[:, quarter:]])
    pieces = jnp.broadcast_to(piece[None], (16,) + piece.shape)
    pieces = swap(pieces.reshape((32,) + piece.shape[1:]), ROW + ("pair",))
    pieces, former0_far, inverse1_near, former1_got, latter0_got = together(
        (
            pieces,
            both_cores(former0_got),
            both_cores(inverse1),
            trade(former1),
            trade(latter0),
        )
    )
    white0 = upright(pieces)

    pieces = swap(cut(panels(former0_near, former0_far, white0), 8), "eight")
    last = panels(both_cores(former1), both_cores(former1_got), white0)
    pieces, last, inverse1_far = together((pieces, last, both_cores(inverse1_got)))
    right = (second - total(pieces)).astype(BF)
    gathered = spread(right, "eight", 8).reshape(-1, quarter)
    gathered, latter0_near, latter0_far = together(
        (gathered, both_cores(latter0), both_cores(latter0_got))
    )

    pieces = jnp.concatenate(
        [
            cut(dot(inverse1_near.reshape(tall, -1), gathered), 16),
            cut(dot(inverse1_far.reshape(tall, -1), gathered), 16),
        ],
        axis=1,
    )
    pieces, got0 = together((swap(pieces, ROW), trade(far(white0))))
    piece = total(pieces).astype(BF).reshape(2, -1, quarter)
    piece = jnp.where(side == 0, piece, piece[::-1]).reshape(-1, quarter)
    pieces, block0 = together(
        (spread(piece, ROW, 16), columns(both_cores(beside(near(white0), got0))))
    )
    white1 = upright(pieces)

    part = half // 16
    member = (here % 8) * part + lax.broadcasted_iota(jnp.int32, (part, quarter), 0)
    picked = lax.broadcasted_iota(jnp.int32, (part, quarter), 1) == member
    pick = jnp.where(picked & (side == here // 8), 1.0, 0.0).astype(BF)
    slices = jnp.concatenate(
        [
            lax.dot_general(pick, white, (((1,), (1,)), ((), ())), preferred_element_type=F32)
            for white in (white0, white1)
        ],
        axis=1,
    ).astype(BF)
    slices = spread(slices, QUAD, 4)
    last = last + panels(latter0_near, latter0_far, white1)
    slices = slices[0] + slices[2]
    slab = dot(slices[:, : 2 * tall], white0) + dot(slices[:, 2 * tall :], white1)

    pieces = jnp.concatenate(
        [cut(last, 8), jnp.broadcast_to(slab.astype(BF)[None], (8, part, quarter))], axis=1
    )
    got1 = trade(far(white1))
    pieces, block1 = together(
        (swap(pieces, "eight"), columns(both_cores(beside(near(white1), got1))))
    )
    height = 4 * own
    slab = total(pieces[:, height:]).astype(BF)
    ends = total(pieces[:, :height])
    ends = both_cores(beside(near(ends), trade(far(ends))))
    trailing = outputs[2:] - columns(ends)[None]
    parts, trailing = together((spread(slab, ROW + QUAD, 64), trailing))
    parts = parts.astype(F32).reshape(16, 4, part, quarter)
    projections = jnp.concatenate(
        [parts[:, place].reshape(half, quarter) for place in (0, 2, 1, 3)], axis=1
    )
    return (jnp.stack([block0, block1]), trailing, projections)


def solution(mesh):
    axes = ("x", "y", "eight", "pair", "core")
    grid = Mesh(mesh.devices.reshape(4, 4, 8, 2, 2), axes)
    col = axes[2:]
    in_specs = (P(None, axes, None), P(None, col, ROW), P(None, ROW, col), P(None, ROW, col))
    out_specs = (P(None, col, None), P(None, axes, None), P())
    return jax.shard_map(body, mesh=grid, in_specs=in_specs, out_specs=out_specs, check_vma=False)
```

time: 192 us -> 211 us (1.099)
  starting transfers between devices: 44.4 us -> 91.1 us
  blocking collectives: 78.7 us -> 54 us
  waiting for transfers between devices: 55.5 us -> 45.4 us
  local copies, waits for them, and re-layouts: 4.92 us -> 7.75 us
  matrix products: 3.17 us -> 5.65 us
    all_to_all x3 -> x0, blocking collectives: 47.6 us -> none  [swap(): return lax.all_to_all(pieces, axis, 0, 0)]
    ppermute x0 -> x8, starting transfers between devices: none -> 24.8 us  [trade(): return lax.ppermute(block, 'pair', [(0, 1), (1, 0)])]
    all_gather x9 -> x14, blocking collectives: 31.1 us -> 54 us  [both_cores(): return lax.all_gather(block, 'core', axis=0)]
    all_to_all x6 -> x10, starting transfers between devices: 44.4 us -> 66.3 us  [swap(): return lax.all_to_all(pieces, axis, 0, 0)]
    all_to_all x6 -> x10, waiting for transfers between devices: 55.5 us -> 33.8 us  [swap(): return lax.all_to_all(pieces, axis, 0, 0)]
    ppermute x0 -> x8, waiting for transfers between devices: none -> 11.6 us  [trade(): return lax.ppermute(block, 'pair', [(0, 1), (1, 0)])]
    dot_general x10 -> x19, matrix products: 3.17 us -> 5.65 us  [the longest x17 5.26 us: dot(): return jnp.dot(a, b, preferred_element_type=F32)]
  transfers between devices with their start and end apart: 6 -> 18, of which waited for: 6 -> 12; matrix products, arithmetic and copies ran while one was open for 1% -> 4% of each run, Pallas kernels for 0% -> 0%
where the time goes in v3:
time: 211 us; the launch traced here: 210 us
  starting transfers between devices  91.1 us (43%)
  blocking collectives  54 us (26%)
  waiting for transfers between devices  45.4 us (22%)
  local copies, waits for them, and re-layouts  7.75 us (4%)
  matrix products  5.65 us (3%)
  other arithmetic  4.87 us (2%)
    all_to_all x10, starting transfers between devices, swap(): return lax.all_to_all(pieces, axis, 0, 0)  66.3 us
    all_gather x14, blocking collectives, both_cores(): return lax.all_gather(block, 'core', axis=0)  54 us
    all_to_all x10, waiting for transfers between devices, swap(): return lax.all_to_all(pieces, axis, 0, 0)  33.8 us
    ppermute x8, starting transfers between devices, trade(): return lax.ppermute(block, 'pair', [(0, 1), (1, 0)])  24.8 us
    ppermute x8, waiting for transfers between devices, trade(): return lax.ppermute(block, 'pair', [(0, 1), (1, 0)])  11.6 us
    dot_general x17, matrix products, dot(): return jnp.dot(a, b, preferred_element_type=F32)  5.26 us
  transfers between devices with their start and end apart: 18, of which 12 were waited for; matrix products, arithmetic and copies ran while one was open for 4% of the time, Pallas kernels for 0%

profile of v3, /device:TPU:1, one launch (start us, length us, event | category | flops | bytes accessed | tf_op | source)
XLA Modules:
  0.0 209.9 jit_solution(4910753641158777276)
XLA Ops:
  1.5 8.4 %all_gather.71 = bf16[2,16,512]{2,1,0:T(8,128)(2,1)S(1)} all-gather(bf16[1,16,512]{2,1,0:T(8,128)(2,1)S(1)} %slice.265), channel_id=1, replica_groups=mesh['x'=4,'y'=4,'eight'=8,'pair'=2,'core'=2] {'core'}, dimensions={0}, use_global_device_ids=true | all-gather | bytes 49152 | tf_op jit(solution)/shard_map/all_gather | solution.py:35
  10.6 9.5 %all-to-all-start = ((bf16[16,32,256]{2,1,0:T(8,128)(2,1)}), bf16[16,32,256]{2,1,0:T(8,128)(2,1)S(1)}, u32[]{:S(2)}, u32[]{:S(2)}) async-start(bf16[16,32,256]{2,1,0:T(8,128)(2,1)} %broadcast_in_dim.29), calls=%async_computation | async-start | bytes 524288 | tf_op jit(solution)/shard_map/all_to_all | solution.py:18
  20.9 3.4 %collective-permute-start = (f32[16,512]{1,0:T(8,128)S(1)}, f32[16,512]{1,0:T(8,128)S(1)}, u32[]{:S(2)}, u32[]{:S(2)}) collective-permute-start(f32[16,512]{1,0:T(8,128)S(1)} %get-tuple-element.80), channel_id=1, source_target_pairs={{0,2},{2,0},{1,3},{3,1},{4,6},{6,4},{5,7},{7,5},{8,10},{10,8},{9,1... | collective-permute-start | bytes 98312 | tf_op jit(solution)/shard_map/ppermute | solution.py:39
  24.4 3.0 %all_gather.72 = bf16[2,256,512]{2,1,0:T(8,128)(2,1)S(1)} all-gather(bf16[1,256,512]{2,1,0:T(8,128)(2,1)S(1)} %get-tuple-element.70), channel_id=1, replica_groups=mesh['x'=4,'y'=4,'eight'=8,'pair'=2,'core'=2] {'core'}, dimensions={0}, use_global_device_ids=true | all-gather | bytes 786432 | tf_op jit(solution)/shard_map/all_gather | solution.py:35
  27.4 5.0 %collective-permute-done = f32[16,512]{1,0:T(8,128)S(1)} collective-permute-done((f32[16,512]{1,0:T(8,128)S(1)}, f32[16,512]{1,0:T(8,128)S(1)}, u32[]{:S(2)}, u32[]{:S(2)}) %collective-permute-start) | collective-permute-done | bytes 32800 | tf_op jit(solution)/shard_map/ppermute | solution.py:39
  32.4 3.7 %all_gather.73 = f32[2,2,16,512]{3,2,0,1:T(8,128)S(1)} all-gather(f32[1,2,16,512]{3,2,0,1:T(8,128)S(1)} %maximum_select_fusion.2), channel_id=1, replica_groups=mesh['x'=4,'y'=4,'eight'=8,'pair'=2,'core'=2] {'core'}, dimensions={0}, use_global_device_ids=true | all-gather | bytes 196608 | tf_op jit(solution)/shard_map/all_gather | solution.py:35
  36.1 5.5 %collective-permute-start.1 = (bf16[512,256]{1,0:T(8,128)(2,1)S(1)}, bf16[512,256]{1,0:T(8,128)(2,1)S(1)}, u32[]{:S(2)}, u32[]{:S(2)}) collective-permute-start(bf16[512,256]{1,0:T(8,128)(2,1)S(1)} %get-tuple-element.35), channel_id=1, source_target_pairs={{0,2},{2,0},{1,3},{3,1},{4,6},{6,4},{5,7},{7,5},{8,10},{10,8},{9,1... | collective-permute-start | bytes 786440 | tf_op jit(solution)/shard_map/ppermute | solution.py:39
  44.6 6.8 %all-to-all-start.1 = ((bf16[16,32,256]{2,1,0:T(8,128)(2,1)}), bf16[16,32,256]{2,1,0:T(8,128)(2,1)S(1)}, u32[]{:S(2)}, u32[]{:S(2)}) async-start(bf16[16,32,256]{2,1,0:T(8,128)(2,1)} %bitcast.10), calls=%async_computation.1 | async-start | bytes 524288 | tf_op jit(solution)/shard_map/all_to_all | solution.py:18
  51.3 3.9 %all-gather = bf16[1024,256]{1,0:T(8,128)(2,1)S(1)} all-gather(bf16[512,256]{1,0:T(8,128)(2,1)S(1)} %get-tuple-element.35), channel_id=2, replica_groups=mesh['x'=4,'y'=4,'eight'=8,'pair'=2,'core'=2] {'core'}, dimensions={0}, use_global_device_ids=true | all-gather | bytes 786432 | tf_op jit(solution)/shard_map/all_gather | solution.py:35
  55.2 3.5 %all-to-all-done.1 = bf16[16,32,256]{2,1,0:T(8,128)(2,1)S(1)} async-done(((bf16[16,32,256]{2,1,0:T(8,128)(2,1)}), bf16[16,32,256]{2,1,0:T(8,128)(2,1)S(1)}, u32[]{:S(2)}, u32[]{:S(2)}) %all-to-all-start.1) | async-done | bytes 262176 | tf_op jit(solution)/shard_map/all_to_all | solution.py:18
  59.6 5.2 %all-to-all-start.2 = ((bf16[32,32,128]{2,1,0:T(8,128)(2,1)}), bf16[32,32,128]{2,1,0:T(8,128)(2,1)S(1)}, u32[]{:S(2)}, u32[]{:S(2)}) async-start(bf16[32,32,128]{2,1,0:T(8,128)(2,1)} %bitcast.16), calls=%async_computation.2 | async-start | bytes 524288 | tf_op jit(solution)/shard_map/all_to_all | solution.py:18
  64.8 5.3 %all-gather.2 = bf16[512,512]{1,0:T(8,128)(2,1)S(1)} all-gather(bf16[256,512]{1,0:T(8,128)(2,1)S(1)} %get-tuple-element.36), channel_id=4, replica_groups=mesh['x'=4,'y'=4,'eight'=8,'pair'=2,'core'=2] {'core'}, dimensions={0}, use_global_device_ids=true | all-gather | bytes 786432 | tf_op jit(solution)/shard_map/all_gather | solution.py:35
  70.2 3.5 %collective-permute-start.3 = (bf16[512,256]{1,0:T(8,128)(2,1)S(1)}, bf16[512,256]{1,0:T(8,128)(2,1)S(1)}, u32[]{:S(2)}, u32[]{:S(2)}) collective-permute-start(bf16[512,256]{1,0:T(8,128)(2,1)S(1)} %get-tuple-element.39), channel_id=1, source_target_pairs={{0,2},{2,0},{1,3},{3,1},{4,6},{6,4},{5,7},{7,5},{8,10},{10,8},{9,1... | collective-permute-start | bytes 786440 | tf_op jit(solution)/shard_map/ppermute | solution.py:39
  75.7 2.7 %all-gather.3 = bf16[1024,256]{1,0:T(8,128)(2,1)S(1)} all-gather(bf16[512,256]{1,0:T(8,128)(2,1)S(1)} %get-tuple-element.39), channel_id=5, replica_groups=mesh['x'=4,'y'=4,'eight'=8,'pair'=2,'core'=2] {'core'}, dimensions={0}, use_global_device_ids=true | all-gather | bytes 786432 | tf_op jit(solution)/shard_map/all_gather | solution.py:35
  87.2 7.4 %all-to-all-start.3 = ((bf16[8,64,128]{2,1,0:T(8,128)(2,1)}), bf16[8,64,128]{2,1,0:T(8,128)(2,1)S(1)}, u32[]{:S(2)}, u32[]{:S(2)}) async-start(bf16[8,64,128]{2,1,0:T(8,128)(2,1)} %bitcast.27), calls=%async_computation.3 | async-start | bytes 262144 | tf_op jit(solution)/shard_map/all_to_all | solution.py:18
  95.7 3.2 %all-gather.4 = bf16[1024,256]{1,0:T(8,128)(2,1)S(1)} all-gather(bf16[512,256]{1,0:T(8,128)(2,1)S(1)} %copy-done.9), channel_id=6, replica_groups=mesh['x'=4,'y'=4,'eight'=8,'pair'=2,'core'=2] {'core'}, dimensions={0}, use_global_device_ids=true | all-gather | bytes 786432 | tf_op jit(solution)/shard_map/all_gather | solution.py:35
  99.4 8.5 %all-to-all-done.3 = bf16[8,64,128]{2,1,0:T(8,128)(2,1)S(1)} async-done(((bf16[8,64,128]{2,1,0:T(8,128)(2,1)}), bf16[8,64,128]{2,1,0:T(8,128)(2,1)S(1)}, u32[]{:S(2)}, u32[]{:S(2)}) %all-to-all-start.3) | async-done | bytes 131104 | tf_op jit(solution)/shard_map/all_to_all | solution.py:18
  108.6 4.4 %all-to-all-start.4 = ((bf16[8,64,128]{2,1,0:T(8,128)(2,1)}), bf16[8,64,128]{2,1,0:T(8,128)(2,1)S(1)}, u32[]{:S(2)}, u32[]{:S(2)}) async-start(bf16[8,64,128]{2,1,0:T(8,128)(2,1)} %broadcast_in_dim.58), calls=%async_computation.4 | async-start | bytes 262144 | tf_op jit(solution)/shard_map/all_to_all | solution.py:18
  112.9 5.0 %all-gather.6 = bf16[1024,256]{1,0:T(8,128)(2,1)S(1)} all-gather(bf16[512,256]{1,0:T(8,128)(2,1)S(1)} %bitcast.159), channel_id=8, replica_groups=mesh['x'=4,'y'=4,'eight'=8,'pair'=2,'core'=2] {'core'}, dimensions={0}, use_global_device_ids=true | all-gather | bytes 786432 | tf_op jit(solution)/shard_map/all_gather | solution.py:35
  120.3 7.4 %all-to-all-done.4 = bf16[8,64,128]{2,1,0:T(8,128)(2,1)S(1)} async-done(((bf16[8,64,128]{2,1,0:T(8,128)(2,1)}), bf16[8,64,128]{2,1,0:T(8,128)(2,1)S(1)}, u32[]{:S(2)}, u32[]{:S(2)}) %all-to-all-start.4) | async-done | bytes 131104 | tf_op jit(solution)/shard_map/all_to_all | solution.py:18
  129.1 6.4 %all-to-all-start.5 = ((bf16[16,64,128]{2,1,0:T(8,128)(2,1)}), bf16[16,64,128]{2,1,0:T(8,128)(2,1)S(1)}, u32[]{:S(2)}, u32[]{:S(2)}) async-start(bf16[16,64,128]{2,1,0:T(8,128)(2,1)} %pad_maximum_fusion.2), calls=%async_computation.5 | async-start | bytes 524288 | tf_op jit(solution)/shard_map/all_to_all | solution.py:18
  137.7 3.6 %collective-permute-done.5 = bf16[512,128]{1,0:T(8,128)(2,1)S(1)} collective-permute-done((bf16[512,128]{1,0:T(8,128)(2,1)S(1)}, bf16[512,128]{1,0:T(8,128)(2,1)S(1)}, u32[]{:S(2)}, u32[]{:S(2)}) %collective-permute-start.5) | collective-permute-done | bytes 131104 | tf_op jit(solution)/shard_map/ppermute | solution.py:39
  143.7 5.4 %all-to-all-start.6 = ((bf16[16,64,128]{2,1,0:T(8,128)(2,1)}), bf16[16,64,128]{2,1,0:T(8,128)(2,1)S(1)}, u32[]{:S(2)}, u32[]{:S(2)}) async-start(bf16[16,64,128]{2,1,0:T(8,128)(2,1)} %broadcast_in_dim.60), calls=%async_computation.6 | async-start | bytes 524288 | tf_op jit(solution)/shard_map/all_to_all | solution.py:18
  149.1 6.3 %all_gather.90 = bf16[2,512,256]{2,1,0:T(8,128)(2,1)S(1)} all-gather(bf16[1,512,256]{2,1,0:T(8,128)(2,1)S(1)} %maximum_select_fusion), channel_id=1, replica_groups=mesh['x'=4,'y'=4,'eight'=8,'pair'=2,'core'=2] {'core'}, dimensions={0}, use_global_device_ids=true | all-gather | bytes 786432 | tf_op jit(solution)/shard_map/all_gather | solution.py:35
  157.3 9.0 %all-to-all-start.7 = ((bf16[4,16,2048]{2,1,0:T(8,128)(2,1)}), bf16[4,16,2048]{2,1,0:T(8,128)(2,1)S(1)}, u32[]{:S(2)}, u32[]{:S(2)}) async-start(bf16[4,16,2048]{2,1,0:T(8,128)(2,1)} %broadcast_in_dim.63), calls=%async_computation.7 | async-start | bytes 524288 | tf_op jit(solution)/shard_map/all_to_all | solution.py:18
  166.6 3.3 %collective-permute-start.6 = (bf16[512,128]{1,0:T(8,128)(2,1)S(1)}, bf16[512,128]{1,0:T(8,128)(2,1)S(1)}, u32[]{:S(2)}, u32[]{:S(2)}) collective-permute-start(bf16[512,128]{1,0:T(8,128)(2,1)S(1)} %get-tuple-element.76), channel_id=1, source_target_pairs={{0,2},{2,0},{1,3},{3,1},{4,6},{6,4},{5,7},{7,5},{8,10},{10,8},{9,1... | collective-permute-start | bytes 393224 | tf_op jit(solution)/shard_map/ppermute | solution.py:39
  172.6 3.4 %all-to-all-start.8 = ((bf16[8,80,128]{2,1,0:T(8,128)(2,1)}), bf16[8,80,128]{2,1,0:T(8,128)(2,1)S(1)}, u32[]{:S(2)}, u32[]{:S(2)}) async-start(bf16[8,80,128]{2,1,0:T(8,128)(2,1)} %pad_maximum_fusion.5), calls=%async_computation.8 | async-start | bytes 327680 | tf_op jit(solution)/shard_map/all_to_all | solution.py:18
  176.0 3.2 %all_gather.91 = bf16[2,512,256]{2,1,0:T(8,128)(2,1)S(1)} all-gather(bf16[1,512,256]{2,1,0:T(8,128)(2,1)S(1)} %maximum_select_fusion.1), channel_id=1, replica_groups=mesh['x'=4,'y'=4,'eight'=8,'pair'=2,'core'=2] {'core'}, dimensions={0}, use_global_device_ids=true | all-gather | bytes 786432 | tf_op jit(solution)/shard_map/all_gather | solution.py:35
  179.2 10.0 %all-to-all-done.8 = bf16[8,80,128]{2,1,0:T(8,128)(2,1)S(1)} async-done(((bf16[8,80,128]{2,1,0:T(8,128)(2,1)}), bf16[8,80,128]{2,1,0:T(8,128)(2,1)S(1)}, u32[]{:S(2)}, u32[]{:S(2)}) %all-to-all-start.8) | async-done | bytes 163872 | tf_op jit(solution)/shard_map/all_to_all | solution.py:18
  190.0 8.8 %all-to-all-start.9 = ((bf16[64,16,128]{2,1,0:T(8,128)(2,1)}), bf16[64,16,128]{2,1,0:T(8,128)(2,1)S(1)}, u32[]{:S(2)}, u32[]{:S(2)}) async-start(bf16[64,16,128]{2,1,0:T(8,128)(2,1)} %broadcast_in_dim.65), calls=%async_computation.9 | async-start | bytes 524288 | tf_op jit(solution)/shard_map/all_to_all | solution.py:18
  198.9 3.3 %collective-permute-start.7 = (f32[32,128]{1,0:T(8,128)S(1)}, f32[32,128]{1,0:T(8,128)S(1)}, u32[]{:S(2)}, u32[]{:S(2)}) collective-permute-start(f32[32,128]{1,0:T(8,128)S(1)} %get-tuple-element.84), channel_id=1, source_target_pairs={{0,2},{2,0},{1,3},{3,1},{4,6},{6,4},{5,7},{7,5},{8,10},{10,8},{9,1... | collective-permute-start | bytes 49160 | tf_op jit(solution)/shard_map/ppermute | solution.py:39
  204.0 2.5 %all_gather.92 = f32[2,32,256]{2,1,0:T(8,128)S(1)} all-gather(f32[1,32,256]{2,1,0:T(8,128)S(1)} %maximum_select_fusion.3), channel_id=1, replica_groups=mesh['x'=4,'y'=4,'eight'=8,'pair'=2,'core'=2] {'core'}, dimensions={0}, use_global_device_ids=true | all-gather | bytes 98304 | tf_op jit(solution)/shard_map/all_gather | solution.py:35
  (102 shorter events, 38.3 us)
Async XLA Ops:
  0.6 23.6 %copy-start = (bf16[2,256,512]{2,1,0:T(8,128)(2,1)S(1)}, bf16[2,256,512]{2,1,0:T(8,128)(2,1)}, u32[]{:S(2)}) copy-start(bf16[2,256,512]{2,1,0:T(8,128)(2,1)} %param.5) | copy-start | bytes 1572868
  10.6 25.6 %all-to-all-start = ((bf16[16,32,256]{2,1,0:T(8,128)(2,1)}), bf16[16,32,256]{2,1,0:T(8,128)(2,1)S(1)}, u32[]{:S(2)}, u32[]{:S(2)}) async-start(bf16[16,32,256]{2,1,0:T(8,128)(2,1)} %broadcast_in_dim.29), calls=%async_computation | async-start | bytes 524288 | tf_op jit(solution)/shard_map/all_to_all | solution.py:18
  20.9 3.5 %copy-start.1 = (bf16[2,512,256]{2,1,0:T(8,128)(2,1)S(1)}, bf16[2,512,256]{2,1,0:T(8,128)(2,1)}, u32[]{:S(2)}) copy-start(bf16[2,512,256]{2,1,0:T(8,128)(2,1)} %param.6) | copy-start | bytes 1572868
  20.9 11.5 %collective-permute-start = (f32[16,512]{1,0:T(8,128)S(1)}, f32[16,512]{1,0:T(8,128)S(1)}, u32[]{:S(2)}, u32[]{:S(2)}) collective-permute-start(f32[16,512]{1,0:T(8,128)S(1)} %get-tuple-element.80), channel_id=1, source_target_pairs={{0,2},{2,0},{1,3},{3,1},{4,6},{6,4},{5,7},{7,5},{8,10},{10,8},{9,1... | collective-permute-start | bytes 98312 | tf_op jit(solution)/shard_map/ppermute | solution.py:39
  36.1 22.6 %collective-permute-start.1 = (bf16[512,256]{1,0:T(8,128)(2,1)S(1)}, bf16[512,256]{1,0:T(8,128)(2,1)S(1)}, u32[]{:S(2)}, u32[]{:S(2)}) collective-permute-start(bf16[512,256]{1,0:T(8,128)(2,1)S(1)} %get-tuple-element.35), channel_id=1, source_target_pairs={{0,2},{2,0},{1,3},{3,1},{4,6},{6,4},{5,7},{7,5},{8,10},{10,8},{9,1... | collective-permute-start | bytes 786440 | tf_op jit(solution)/shard_map/ppermute | solution.py:39
  41.7 17.1 %collective-permute-start.2 = (bf16[256,512]{1,0:T(8,128)(2,1)S(1)}, bf16[256,512]{1,0:T(8,128)(2,1)S(1)}, u32[]{:S(2)}, u32[]{:S(2)}) collective-permute-start(bf16[256,512]{1,0:T(8,128)(2,1)S(1)} %get-tuple-element.36), channel_id=1, source_target_pairs={{0,2},{2,0},{1,3},{3,1},{4,6},{6,4},{5,7},{7,5},{8,10},{10,8},{9,1... | collective-permute-start | bytes 786440 | tf_op jit(solution)/shard_map/ppermute | solution.py:39
  44.6 14.1 %all-to-all-start.1 = ((bf16[16,32,256]{2,1,0:T(8,128)(2,1)}), bf16[16,32,256]{2,1,0:T(8,128)(2,1)S(1)}, u32[]{:S(2)}, u32[]{:S(2)}) async-start(bf16[16,32,256]{2,1,0:T(8,128)(2,1)} %bitcast.10), calls=%async_computation.1 | async-start | bytes 524288 | tf_op jit(solution)/shard_map/all_to_all | solution.py:18
  58.7 0.9 copy-start.4
  58.7 0.9 copy-start.6
  59.6 26.0 %all-to-all-start.2 = ((bf16[32,32,128]{2,1,0:T(8,128)(2,1)}), bf16[32,32,128]{2,1,0:T(8,128)(2,1)S(1)}, u32[]{:S(2)}, u32[]{:S(2)}) async-start(bf16[32,32,128]{2,1,0:T(8,128)(2,1)} %bitcast.16), calls=%async_computation.2 | async-start | bytes 524288 | tf_op jit(solution)/shard_map/all_to_all | solution.py:18
  64.8 8.9 %copy-start.2 = (bf16[1,512,256]{2,1,0:T(8,128)(2,1)S(1)}, bf16[1,512,256]{2,1,0:T(8,128)(2,1)}, u32[]{:S(2)}) copy-start(bf16[1,512,256]{2,1,0:T(8,128)(2,1)} %param.7) | copy-start | bytes 786436
  70.2 8.2 %copy-start.5 = (bf16[512,256]{1,0:T(8,128)(2,1)S(1)}, bf16[512,256]{1,0:T(8,128)(2,1)}, u32[]{:S(2)}) copy-start(bf16[512,256]{1,0:T(8,128)(2,1)} %copy-done.4) | copy-start | bytes 786436
  70.2 12.7 %collective-permute-start.3 = (bf16[512,256]{1,0:T(8,128)(2,1)S(1)}, bf16[512,256]{1,0:T(8,128)(2,1)S(1)}, u32[]{:S(2)}, u32[]{:S(2)}) collective-permute-start(bf16[512,256]{1,0:T(8,128)(2,1)S(1)} %get-tuple-element.39), channel_id=1, source_target_pairs={{0,2},{2,0},{1,3},{3,1},{4,6},{6,4},{5,7},{7,5},{8,10},{10,8},{9,1... | collective-permute-start | bytes 786440 | tf_op jit(solution)/shard_map/ppermute | solution.py:39
  73.7 11.8 %collective-permute-start.4 = (bf16[512,256]{1,0:T(8,128)(2,1)S(1)}, bf16[512,256]{1,0:T(8,128)(2,1)}, u32[]{:S(2)}, u32[]{:S(2)}) collective-permute-start(bf16[512,256]{1,0:T(8,128)(2,1)S(1)} %bitcast.158), channel_id=1, source_target_pairs={{0,2},{2,0},{1,3},{3,1},{4,6},{6,4},{5,7},{7,5},{8,10},{10,8},{9,1... | collective-permute-start | bytes 786440 | tf_op jit(solution)/shard_map/ppermute | solution.py:39
  78.3 2.3 %copy-start.7 = (bf16[256,512]{1,0:T(8,128)(2,1)S(1)}, bf16[256,512]{1,0:T(8,128)(2,1)}, u32[]{:S(2)}) copy-start(bf16[256,512]{1,0:T(8,128)(2,1)} %copy-done.6) | copy-start | bytes 786436
  82.8 0.7 copy-start.8
  87.2 20.7 %all-to-all-start.3 = ((bf16[8,64,128]{2,1,0:T(8,128)(2,1)}), bf16[8,64,128]{2,1,0:T(8,128)(2,1)S(1)}, u32[]{:S(2)}, u32[]{:S(2)}) async-start(bf16[8,64,128]{2,1,0:T(8,128)(2,1)} %bitcast.27), calls=%async_computation.3 | async-start | bytes 262144 | tf_op jit(solution)/shard_map/all_to_all | solution.py:18
  94.8 1.0 copy-start.9
  107.9 5.1 %copy-start.3 = (bf16[1,512,256]{2,1,0:T(8,128)(2,1)S(1)}, bf16[1,512,256]{2,1,0:T(8,128)(2,1)}, u32[]{:S(2)}) copy-start(bf16[1,512,256]{2,1,0:T(8,128)(2,1)} %param.7) | copy-start | bytes 786436
  108.6 19.2 %all-to-all-start.4 = ((bf16[8,64,128]{2,1,0:T(8,128)(2,1)}), bf16[8,64,128]{2,1,0:T(8,128)(2,1)S(1)}, u32[]{:S(2)}, u32[]{:S(2)}) async-start(bf16[8,64,128]{2,1,0:T(8,128)(2,1)} %broadcast_in_dim.58), calls=%async_computation.4 | async-start | bytes 262144 | tf_op jit(solution)/shard_map/all_to_all | solution.py:18
  129.1 13.8 %all-to-all-start.5 = ((bf16[16,64,128]{2,1,0:T(8,128)(2,1)}), bf16[16,64,128]{2,1,0:T(8,128)(2,1)S(1)}, u32[]{:S(2)}, u32[]{:S(2)}) async-start(bf16[16,64,128]{2,1,0:T(8,128)(2,1)} %pad_maximum_fusion.2), calls=%async_computation.5 | async-start | bytes 524288 | tf_op jit(solution)/shard_map/all_to_all | solution.py:18
  135.6 5.7 %collective-permute-start.5 = (bf16[512,128]{1,0:T(8,128)(2,1)S(1)}, bf16[512,128]{1,0:T(8,128)(2,1)S(1)}, u32[]{:S(2)}, u32[]{:S(2)}) collective-permute-start(bf16[512,128]{1,0:T(8,128)(2,1)S(1)} %get-tuple-element.78), channel_id=1, source_target_pairs={{0,2},{2,0},{1,3},{3,1},{4,6},{6,4},{5,7},{7,5},{8,10},{10,8},{9,1... | collective-permute-start | bytes 393224 | tf_op jit(solution)/shard_map/ppermute | solution.py:39
  143.7 12.7 %all-to-all-start.6 = ((bf16[16,64,128]{2,1,0:T(8,128)(2,1)}), bf16[16,64,128]{2,1,0:T(8,128)(2,1)S(1)}, u32[]{:S(2)}, u32[]{:S(2)}) async-start(bf16[16,64,128]{2,1,0:T(8,128)(2,1)} %broadcast_in_dim.60), calls=%async_computation.6 | async-start | bytes 524288 | tf_op jit(solution)/shard_map/all_to_all | solution.py:18
  157.3 14.2 %all-to-all-start.7 = ((bf16[4,16,2048]{2,1,0:T(8,128)(2,1)}), bf16[4,16,2048]{2,1,0:T(8,128)(2,1)S(1)}, u32[]{:S(2)}, u32[]{:S(2)}) async-start(bf16[4,16,2048]{2,1,0:T(8,128)(2,1)} %broadcast_in_dim.63), calls=%async_computation.7 | async-start | bytes 524288 | tf_op jit(solution)/shard_map/all_to_all | solution.py:18
  166.6 9.3 %collective-permute-start.6 = (bf16[512,128]{1,0:T(8,128)(2,1)S(1)}, bf16[512,128]{1,0:T(8,128)(2,1)S(1)}, u32[]{:S(2)}, u32[]{:S(2)}) collective-permute-start(bf16[512,128]{1,0:T(8,128)(2,1)S(1)} %get-tuple-element.76), channel_id=1, source_target_pairs={{0,2},{2,0},{1,3},{3,1},{4,6},{6,4},{5,7},{7,5},{8,10},{10,8},{9,1... | collective-permute-start | bytes 393224 | tf_op jit(solution)/shard_map/ppermute | solution.py:39
  172.6 16.7 %all-to-all-start.8 = ((bf16[8,80,128]{2,1,0:T(8,128)(2,1)}), bf16[8,80,128]{2,1,0:T(8,128)(2,1)S(1)}, u32[]{:S(2)}, u32[]{:S(2)}) async-start(bf16[8,80,128]{2,1,0:T(8,128)(2,1)} %pad_maximum_fusion.5), calls=%async_computation.8 | async-start | bytes 327680 | tf_op jit(solution)/shard_map/all_to_all | solution.py:18
  190.0 19.0 %all-to-all-start.9 = ((bf16[64,16,128]{2,1,0:T(8,128)(2,1)}), bf16[64,16,128]{2,1,0:T(8,128)(2,1)S(1)}, u32[]{:S(2)}, u32[]{:S(2)}) async-start(bf16[64,16,128]{2,1,0:T(8,128)(2,1)} %broadcast_in_dim.65), calls=%async_computation.9 | async-start | bytes 524288 | tf_op jit(solution)/shard_map/all_to_all | solution.py:18
  198.9 5.1 %collective-permute-start.7 = (f32[32,128]{1,0:T(8,128)S(1)}, f32[32,128]{1,0:T(8,128)S(1)}, u32[]{:S(2)}, u32[]{:S(2)}) collective-permute-start(f32[32,128]{1,0:T(8,128)S(1)} %get-tuple-element.84), channel_id=1, source_target_pairs={{0,2},{2,0},{1,3},{3,1},{4,6},{6,4},{5,7},{7,5},{8,10},{10,8},{9,1... | collective-permute-start | bytes 49160 | tf_op jit(solution)/shard_map/ppermute | solution.py:39

commit v4 on v2

v4 whole, which is shorter than its diff:
```python
import jax
import jax.numpy as jnp
from jax import lax
from jax.sharding import Mesh, PartitionSpec as P

BF = jnp.bfloat16
F32 = jnp.float32
ROW = ("x", "y")
COL = ("z", "core")
together = lax.optimization_barrier


def swap(pieces, axis):
    return lax.all_to_all(pieces, axis, 0, 0)


def spread(piece, axis, count):
    return swap(jnp.broadcast_to(piece[None], (count,) + piece.shape), axis)


def cut(partial, count):
    rows, width = partial.shape
    return partial.astype(BF).reshape(count, rows // count, width)


def total(pieces):
    return together(jnp.sum(pieces.astype(F32), axis=0))


def both_cores(block):
    return lax.all_gather(block, "core", axis=0)


def body(outputs, inverses, former, latter):
    core = lax.axis_index("core").astype(jnp.uint32)
    place = lax.axis_index(ROW).astype(jnp.uint32) * 16
    half = outputs.shape[2] // 2
    own = outputs.shape[1]
    height = 2 * own

    def whiten(inverse, rows):
        partial = jnp.dot(inverse, rows, preferred_element_type=F32)
        piece = total(swap(cut(partial, 16), ROW)).astype(BF)
        return spread(piece, ROW, 16).reshape(-1, half)

    def panel(tiles, white):
        depth = tiles.shape[2]
        return jnp.dot(tiles[0], white[:depth], preferred_element_type=F32) + jnp.dot(
            tiles[1], white[depth:], preferred_element_type=F32
        )

    def gram(whole, white):
        return lax.dot_general(
            whole[0], white, (((0,), (0,)), ((), ())), preferred_element_type=F32
        )

    def window(array, start, size, axis):
        starts = [jnp.uint32(0)] * array.ndim
        starts[axis] = start
        sizes = array.shape[:axis] + (size,) + array.shape[axis + 1 :]
        return lax.dynamic_slice(array, starts, sizes)

    def block(whole, start):
        sizes = (1, whole.shape[1] // 2, half)
        zero, one = jnp.uint32(0), jnp.uint32(1)
        left = lax.dynamic_slice(whole, (zero, start, zero), sizes)
        right = lax.dynamic_slice(whole, (one, start, zero), sizes)
        return jnp.concatenate([left[0], right[0]], axis=1)

    first = both_cores(outputs[0].astype(BF))
    first = window(first, core * half, half, 2).reshape(height, half)
    gathered = spread(first, "z", 16).reshape(-1, half)
    second = window(both_cores(outputs[1]), core * half, half, 2)
    rows = inverses.shape[1]
    gathered, inverse0, former0, second, block_start, end_start, slab_start = together(
        (
            gathered,
            both_cores(inverses[0]),
            both_cores(former[0]),
            second.reshape(height, half),
            core * rows,
            core * own,
            place,
        )
    )
    white0 = whiten(inverse0.reshape(-1, inverse0.shape[2]), gathered)

    pieces = cut(panel(former0, white0), 16)
    pieces, white0, former1, inverse1, latter0 = together(
        (pieces, white0, former[1], inverses[1], latter[0])
    )
    pieces = swap(pieces, "z")
    whole0 = both_cores(white0)
    last = panel(both_cores(former1), white0)
    pieces, last, slabs0, block0, inverse1, latter0 = together(
        (
            pieces,
            last,
            gram(whole0, white0),
            block(whole0, block_start),
            both_cores(inverse1),
            both_cores(latter0),
        )
    )
    right = (second - total(pieces)).astype(BF)
    gathered = spread(right, "z", 16).reshape(-1, half)
    white1 = whiten(inverse1.reshape(-1, inverse1.shape[2]), gathered)

    whole1 = both_cores(white1)
    last = last + panel(latter0, white1)
    slabs = slabs0 + gram(whole1, white1)
    part = half // 16
    slab = window(slabs, slab_start, part, 0).astype(BF)
    pieces = jnp.concatenate(
        [cut(last, 16), jnp.broadcast_to(slab[None], (16, part, half))], axis=1
    )
    pieces, whole1 = together((swap(pieces, "z"), whole1))
    slab = total(pieces[:, height:]).astype(BF)
    ends = total(pieces[:, :height])
    pieces, ends = together((jnp.broadcast_to(slab[None], (32,) + slab.shape), ends))
    trailing = outputs[2:] - block(both_cores(ends), end_start)[None]
    parts, trailing = together((swap(pieces, ROW + ("core",)), trailing))
    parts = parts.astype(F32).reshape(16, 2, part, half)
    projections = jnp.concatenate(
        [parts[:, 0].reshape(half, half), parts[:, 1].reshape(half, half)], axis=1
    )
    whitened = jnp.stack([block0, block(whole1, block_start)])
    return (whitened, trailing, projections)


def solution(mesh):
    grid = Mesh(mesh.devices.reshape(4, 4, 16, 2), ("x", "y", "z", "core"))
    every = ("x", "y", "z", "core")
    in_specs = (P(None, every, None), P(None, COL, ROW), P(None, ROW, COL), P(None, ROW, COL))
    out_specs = (P(None, COL, None), P(None, every, None), P())
    return jax.shard_map(body, mesh=grid, in_specs=in_specs, out_specs=out_specs, check_vma=False)
```

time: 192 us -> 188 us (0.979)
  blocking collectives: 78.7 us -> 132 us
  waiting for transfers between devices: 55.5 us -> 12.2 us
  starting transfers between devices: 44.4 us -> 31.5 us
    all_to_all x3 -> x6, blocking collectives: 47.6 us -> 93.7 us  [swap(): return lax.all_to_all(pieces, axis, 0, 0)]
    all_to_all x6 -> x3, waiting for transfers between devices: 55.5 us -> 12.2 us  [swap(): return lax.all_to_all(pieces, axis, 0, 0)]
    all_to_all x6 -> x3, starting transfers between devices: 44.4 us -> 31.5 us  [swap(): return lax.all_to_all(pieces, axis, 0, 0)]
    all_gather x9 -> x10, blocking collectives: 31.1 us -> 38.4 us  [both_cores(): return lax.all_gather(block, 'core', axis=0)]
  transfers between devices with their start and end apart: 6 -> 3, of which waited for: 6 -> 2; matrix products, arithmetic and copies ran while one was open for 1% -> 1% of each run, Pallas kernels for 0% -> 0%
where the time goes in v4:
time: 188 us; the launch traced here: 187 us
  blocking collectives  132 us (70%)
  starting transfers between devices  31.5 us (17%)
  waiting for transfers between devices  12.2 us (6%)
  local copies, waits for them, and re-layouts  4.3 us (2%)
  matrix products  3.16 us (2%)
  other arithmetic  2.6 us (1%)
    all_to_all x6, blocking collectives, swap(): return lax.all_to_all(pieces, axis, 0, 0)  93.7 us
    all_gather x10, blocking collectives, both_cores(): return lax.all_gather(block, 'core', axis=0)  38.4 us
    all_to_all x3, starting transfers between devices, swap(): return lax.all_to_all(pieces, axis, 0, 0)  31.5 us
    all_to_all x3, waiting for transfers between devices, swap(): return lax.all_to_all(pieces, axis, 0, 0)  12.2 us
  transfers between devices with their start and end apart: 3, of which 2 were waited for; matrix products, arithmetic and copies ran while one was open for 1% of the time, Pallas kernels for 0%

profile of v4, /device:TPU:1, one launch (start us, length us, event | category | flops | bytes accessed | tf_op | source)
XLA Modules:
  0.0 186.7 jit_solution(17181956596486307127)
XLA Ops:
  0.6 0.8 slice.165
  1.4 8.4 %all_gather.46 = bf16[2,16,512]{2,1,0:T(8,128)(2,1)S(1)} all-gather(bf16[1,16,512]{2,1,0:T(8,128)(2,1)S(1)} %slice.165), channel_id=1, replica_groups=mesh['x'=4,'y'=4,'z'=16,'core'=2] {'core'}, dimensions={0}, use_global_device_ids=true | all-gather | bytes 49152 | tf_op jit(solution)/shard_map/all_gather | solution.py:31
  9.8 0.7 broadcast_in_dim.17
  10.5 9.5 %all-to-all-start = ((bf16[16,32,256]{2,1,0:T(8,128)(2,1)}), bf16[16,32,256]{2,1,0:T(8,128)(2,1)S(1)}, u32[]{:S(2)}, u32[]{:S(2)}) async-start(bf16[16,32,256]{2,1,0:T(8,128)(2,1)} %broadcast_in_dim.17), calls=%async_computation | async-start | bytes 524288 | tf_op jit(solution)/shard_map/all_to_all | solution.py:14
  20.1 0.7 slice-done
  20.8 2.1 %all_gather.49 = f32[2,16,512]{2,1,0:T(8,128)S(1)} all-gather(f32[1,16,512]{2,1,0:T(8,128)S(1)} %slice-done), channel_id=1, replica_groups=mesh['x'=4,'y'=4,'z'=16,'core'=2] {'core'}, dimensions={0}, use_global_device_ids=true | all-gather | bytes 98304 | tf_op jit(solution)/shard_map/all_gather | solution.py:31
  23.0 2.3 %all_gather.47 = bf16[2,256,512]{2,1,0:T(8,128)(2,1)S(1)} all-gather(bf16[1,256,512]{2,1,0:T(8,128)(2,1)S(1)} %get-tuple-element.56), channel_id=1, replica_groups=mesh['x'=4,'y'=4,'z'=16,'core'=2] {'core'}, dimensions={0}, use_global_device_ids=true | all-gather | bytes 786432 | tf_op jit(solution)/shard_map/all_gather | solution.py:31
  25.3 2.2 %all_gather.48 = bf16[2,512,256]{2,1,0:T(8,128)(2,1)S(1)} all-gather(bf16[1,512,256]{2,1,0:T(8,128)(2,1)S(1)} %get-tuple-element.58), channel_id=1, replica_groups=mesh['x'=4,'y'=4,'z'=16,'core'=2] {'core'}, dimensions={0}, use_global_device_ids=true | all-gather | bytes 786432 | tf_op jit(solution)/shard_map/all_gather | solution.py:31
  27.5 6.6 %all-to-all-done = bf16[16,32,256]{2,1,0:T(8,128)(2,1)S(1)} async-done(((bf16[16,32,256]{2,1,0:T(8,128)(2,1)}), bf16[16,32,256]{2,1,0:T(8,128)(2,1)S(1)}, u32[]{:S(2)}, u32[]{:S(2)}) %all-to-all-start) | async-done | bytes 262176 | tf_op jit(solution)/shard_map/all_to_all | solution.py:14
  34.1 0.3 convolution_convert_fusion.1
  34.4 13.9 %all_to_all.45 = bf16[16,32,256]{2,1,0:T(8,128)(2,1)S(1)} all-to-all(bf16[16,32,256]{2,1,0:T(8,128)(2,1)S(1)} %bitcast.88), channel_id=1, replica_groups=mesh['x'=4,'y'=4,'z'=16,'core'=2] {'x','y'}, dimensions={0} | all-to-all | bytes 524288 | tf_op jit(solution)/shard_map/all_to_all | solution.py:14
  48.3 10.5 %all_to_all.46 = bf16[16,32,256]{2,1,0:T(8,128)(2,1)S(1)} all-to-all(bf16[16,32,256]{2,1,0:T(8,128)(2,1)S(1)} %broadcast_in_dim.18), channel_id=1, replica_groups=mesh['x'=4,'y'=4,'z'=16,'core'=2] {'x','y'}, dimensions={0} | all-to-all | bytes 524288 | tf_op jit(solution)/shard_map/all_to_all | solution.py:14
  59.1 0.9 fusion.2
  60.0 10.5 %all-to-all-start.3 = ((bf16[16,32,256]{2,1,0:T(8,128)(2,1)}), bf16[16,32,256]{2,1,0:T(8,128)(2,1)S(1)}, u32[]{:S(2)}, u32[]{:S(2)}) async-start(bf16[16,32,256]{2,1,0:T(8,128)(2,1)} %bitcast.9), calls=%async_computation.3 | async-start | bytes 524288 | tf_op jit(solution)/shard_map/all_to_all | solution.py:14
  70.5 5.3 %all-gather = bf16[1024,256]{1,0:T(8,128)(2,1)S(1)} all-gather(bf16[512,256]{1,0:T(8,128)(2,1)S(1)} %get-tuple-element.31), channel_id=2, replica_groups=mesh['x'=4,'y'=4,'z'=16,'core'=2] {'core'}, dimensions={0}, use_global_device_ids=true | all-gather | bytes 786432 | tf_op jit(solution)/shard_map/all_gather | solution.py:31
  75.8 2.2 %all-gather.1 = bf16[1024,256]{1,0:T(8,128)(2,1)S(1)} all-gather(bf16[512,256]{1,0:T(8,128)(2,1)S(1)} %bitcast.74), channel_id=3, replica_groups=mesh['x'=4,'y'=4,'z'=16,'core'=2] {'core'}, dimensions={0}, use_global_device_ids=true | all-gather | bytes 786432 | tf_op jit(solution)/shard_map/all_gather | solution.py:31
  78.0 2.2 %all-gather.2 = bf16[512,512]{1,0:T(8,128)(2,1)S(1)} all-gather(bf16[256,512]{1,0:T(8,128)(2,1)S(1)} %get-tuple-element.34), channel_id=4, replica_groups=mesh['x'=4,'y'=4,'z'=16,'core'=2] {'core'}, dimensions={0}, use_global_device_ids=true | all-gather | bytes 786432 | tf_op jit(solution)/shard_map/all_gather | solution.py:31
  80.3 0.9 copy-done.2
  81.2 2.2 %all-gather.3 = bf16[1024,256]{1,0:T(8,128)(2,1)S(1)} all-gather(bf16[512,256]{1,0:T(8,128)(2,1)S(1)} %bitcast.97), channel_id=5, replica_groups=mesh['x'=4,'y'=4,'z'=16,'core'=2] {'core'}, dimensions={0}, use_global_device_ids=true | all-gather | bytes 786432 | tf_op jit(solution)/shard_map/all_gather | solution.py:31
  84.2 25.5 %all_to_all.47 = bf16[16,32,256]{2,1,0:T(8,128)(2,1)S(1)} all-to-all(bf16[16,32,256]{2,1,0:T(8,128)(2,1)S(1)} %broadcast_in_dim.19), channel_id=1, replica_groups=mesh['x'=4,'y'=4,'z'=16,'core'=2] {'z'}, dimensions={0} | all-to-all | bytes 524288 | tf_op jit(solution)/shard_map/all_to_all | solution.py:14
  109.7 0.3 convolution_convert_fusion
  110.0 10.5 %all_to_all.48 = bf16[16,32,256]{2,1,0:T(8,128)(2,1)S(1)} all-to-all(bf16[16,32,256]{2,1,0:T(8,128)(2,1)S(1)} %bitcast.90), channel_id=1, replica_groups=mesh['x'=4,'y'=4,'z'=16,'core'=2] {'x','y'}, dimensions={0} | all-to-all | bytes 524288 | tf_op jit(solution)/shard_map/all_to_all | solution.py:14
  120.6 10.5 %all_to_all.49 = bf16[16,32,256]{2,1,0:T(8,128)(2,1)S(1)} all-to-all(bf16[16,32,256]{2,1,0:T(8,128)(2,1)S(1)} %broadcast_in_dim.20), channel_id=1, replica_groups=mesh['x'=4,'y'=4,'z'=16,'core'=2] {'x','y'}, dimensions={0} | all-to-all | bytes 524288 | tf_op jit(solution)/shard_map/all_to_all | solution.py:14
  131.1 9.8 %all_gather.58 = bf16[2,512,256]{2,1,0:T(8,128)(2,1)S(1)} all-gather(bf16[1,512,256]{2,1,0:T(8,128)(2,1)S(1)} %bitcast.78), channel_id=1, replica_groups=mesh['x'=4,'y'=4,'z'=16,'core'=2] {'core'}, dimensions={0}, use_global_device_ids=true | all-gather | bytes 786432 | tf_op jit(solution)/shard_map/all_gather | solution.py:31
  141.8 22.7 %all_to_all.50 = bf16[16,48,256]{2,1,0:T(8,128)(2,1)S(1)} all-to-all(bf16[16,48,256]{2,1,0:T(8,128)(2,1)S(1)} %pad_maximum_fusion.2), channel_id=1, replica_groups=mesh['x'=4,'y'=4,'z'=16,'core'=2] {'z'}, dimensions={0} | all-to-all | bytes 786432 | tf_op jit(solution)/shard_map/all_to_all | solution.py:14
  164.6 0.7 broadcast_in_dim.22
  165.4 11.5 %all-to-all-start.8 = ((bf16[32,16,256]{2,1,0:T(8,128)(2,1)}), bf16[32,16,256]{2,1,0:T(8,128)(2,1)S(1)}, u32[]{:S(2)}, u32[]{:S(2)}) async-start(bf16[32,16,256]{2,1,0:T(8,128)(2,1)} %broadcast_in_dim.22), calls=%async_computation.8 | async-start | bytes 524288 | tf_op jit(solution)/shard_map/all_to_all | solution.py:14
  176.8 1.9 all-gather.4
  178.7 0.8 pad_maximum_fusion
  179.6 0.6 fusion.21
  180.2 5.6 %all-to-all-done.8 = bf16[32,16,256]{2,1,0:T(8,128)(2,1)S(1)} async-done(((bf16[32,16,256]{2,1,0:T(8,128)(2,1)}), bf16[32,16,256]{2,1,0:T(8,128)(2,1)S(1)}, u32[]{:S(2)}, u32[]{:S(2)}) %all-to-all-start.8) | async-done | bytes 262176 | tf_op jit(solution)/shard_map/all_to_all | solution.py:14
  185.9 0.9 pad_maximum_fusion.1
  (40 shorter events, 2.3 us)
Async XLA Ops:
  9.8 13.2 %copy-start = (bf16[2,256,512]{2,1,0:T(8,128)(2,1)S(1)}, bf16[2,256,512]{2,1,0:T(8,128)(2,1)}, u32[]{:S(2)}) copy-start(bf16[2,256,512]{2,1,0:T(8,128)(2,1)} %param.5) | copy-start | bytes 1572868
  10.5 23.6 %all-to-all-start = ((bf16[16,32,256]{2,1,0:T(8,128)(2,1)}), bf16[16,32,256]{2,1,0:T(8,128)(2,1)S(1)}, u32[]{:S(2)}, u32[]{:S(2)}) async-start(bf16[16,32,256]{2,1,0:T(8,128)(2,1)} %broadcast_in_dim.17), calls=%async_computation | async-start | bytes 524288 | tf_op jit(solution)/shard_map/all_to_all | solution.py:14
  20.0 0.8 slice-start
  23.0 2.3 %copy-start.1 = (bf16[2,512,256]{2,1,0:T(8,128)(2,1)S(1)}, bf16[2,512,256]{2,1,0:T(8,128)(2,1)}, u32[]{:S(2)}) copy-start(bf16[2,512,256]{2,1,0:T(8,128)(2,1)} %param.6) | copy-start | bytes 1572868
  60.0 24.1 %all-to-all-start.3 = ((bf16[16,32,256]{2,1,0:T(8,128)(2,1)}), bf16[16,32,256]{2,1,0:T(8,128)(2,1)S(1)}, u32[]{:S(2)}, u32[]{:S(2)}) async-start(bf16[16,32,256]{2,1,0:T(8,128)(2,1)} %bitcast.9), calls=%async_computation.3 | async-start | bytes 524288 | tf_op jit(solution)/shard_map/all_to_all | solution.py:14
  80.2 1.0 copy-start.2
  165.4 20.5 %all-to-all-start.8 = ((bf16[32,16,256]{2,1,0:T(8,128)(2,1)}), bf16[32,16,256]{2,1,0:T(8,128)(2,1)S(1)}, u32[]{:S(2)}, u32[]{:S(2)}) async-start(bf16[32,16,256]{2,1,0:T(8,128)(2,1)} %broadcast_in_dim.22), calls=%async_computation.8 | async-start | bytes 524288 | tf_op jit(solution)/shard_map/all_to_all | solution.py:14
  178.7 0.9 copy-start.3

commit v5 on v4

--- a/solution.py
+++ b/solution.py
@@ -72,33 +72,33 @@
     gathered = spread(first, "z", 16).reshape(-1, half)
     second = window(both_cores(outputs[1]), core * half, half, 2)
     rows = inverses.shape[1]
-    gathered, inverse0, former0, second, block_start, end_start, slab_start = together(
+    gathered, inverse0, former0, second, inverse1, former1, *starts = together(
         (
             gathered,
             both_cores(inverses[0]),
             both_cores(former[0]),
             second.reshape(height, half),
+            both_cores(inverses[1]),
+            both_cores(former[1]),
             core * rows,
             core * own,
             place,
         )
     )
+    block_start, end_start, slab_start = starts
     white0 = whiten(inverse0.reshape(-1, inverse0.shape[2]), gathered)
 
     pieces = cut(panel(former0, white0), 16)
-    pieces, white0, former1, inverse1, latter0 = together(
-        (pieces, white0, former[1], inverses[1], latter[0])
-    )
+    pieces, white0 = together((pieces, white0))
     pieces = swap(pieces, "z")
+    last, white0, latter0 = together((panel(former1, white0), white0, latter[0]))
     whole0 = both_cores(white0)
-    last = panel(both_cores(former1), white0)
-    pieces, last, slabs0, block0, inverse1, latter0 = together(
+    pieces, last, slabs0, block0, latter0 = together(
         (
             pieces,
             last,
             gram(whole0, white0),
             block(whole0, block_start),
-            both_cores(inverse1),
             both_cores(latter0),
         )
     )
@@ -117,14 +117,15 @@
     pieces, whole1 = together((swap(pieces, "z"), whole1))
     slab = total(pieces[:, height:]).astype(BF)
     ends = total(pieces[:, :height])
-    pieces, ends = together((jnp.broadcast_to(slab[None], (32,) + slab.shape), ends))
+    pieces, ends, whole1 = together((jnp.broadcast_to(slab[None], (32,) + slab.shape), ends, whole1))
+    block1, ends = together((block(whole1, block_start), ends))
     trailing = outputs[2:] - block(both_cores(ends), end_start)[None]
     parts, trailing = together((swap(pieces, ROW + ("core",)), trailing))
     parts = parts.astype(F32).reshape(16, 2, part, half)
     projections = jnp.concatenate(
         [parts[:, 0].reshape(half, half), parts[:, 1].reshape(half, half)], axis=1
     )
-    whitened = jnp.stack([block0, block(whole1, block_start)])
+    whitened = jnp.stack([block0, block1])
     return (whitened, trailing, projections)
 
 

time: 188 us -> 185 us (0.984)
  blocking collectives: 132 us -> 130 us
    all_to_all x6, blocking collectives: 93.7 us -> 89.9 us  [swap(): return lax.all_to_all(pieces, axis, 0, 0)]
  transfers between devices with their start and end apart: 3 -> 3, of which waited for: 2 -> 3; matrix products, arithmetic and copies ran while one was open for 1% -> 1% of each run, Pallas kernels for 0% -> 0%
where the time goes in v5:
time: 185 us; the launch traced here: 184 us
  blocking collectives  130 us (70%)
  starting transfers between devices  31.6 us (17%)
  waiting for transfers between devices  11.4 us (6%)
  local copies, waits for them, and re-layouts  4.29 us (2%)
  matrix products  3.18 us (2%)
  other arithmetic  2.6 us (1%)
    all_to_all x6, blocking collectives, swap(): return lax.all_to_all(pieces, axis, 0, 0)  89.9 us
    all_gather x10, blocking collectives, both_cores(): return lax.all_gather(block, 'core', axis=0)  40 us
    all_to_all x3, starting transfers between devices, swap(): return lax.all_to_all(pieces, axis, 0, 0)  31.6 us
    all_to_all x3, waiting for transfers between devices, swap(): return lax.all_to_all(pieces, axis, 0, 0)  11.4 us
  transfers between devices with their start and end apart: 3, of which 3 were waited for; matrix products, arithmetic and copies ran while one was open for 1% of the time, Pallas kernels for 0%

profile of v5, /device:TPU:1, one launch (start us, length us, event | category | flops | bytes accessed | tf_op | source)
XLA Modules:
  0.0 183.9 jit_solution(10541915320185177460)
XLA Ops:
  0.6 0.8 slice.163
  1.4 8.4 %all_gather.40 = bf16[2,16,512]{2,1,0:T(8,128)(2,1)S(1)} all-gather(bf16[1,16,512]{2,1,0:T(8,128)(2,1)S(1)} %slice.163), channel_id=1, replica_groups=mesh['x'=4,'y'=4,'z'=16,'core'=2] {'core'}, dimensions={0}, use_global_device_ids=true | all-gather | bytes 49152 | tf_op jit(solution)/shard_map/all_gather | solution.py:31
  9.8 0.7 broadcast_in_dim.17
  10.5 9.5 %all-to-all-start = ((bf16[16,32,256]{2,1,0:T(8,128)(2,1)}), bf16[16,32,256]{2,1,0:T(8,128)(2,1)S(1)}, u32[]{:S(2)}, u32[]{:S(2)}) async-start(bf16[16,32,256]{2,1,0:T(8,128)(2,1)} %broadcast_in_dim.17), calls=%async_computation | async-start | bytes 524288 | tf_op jit(solution)/shard_map/all_to_all | solution.py:14
  20.1 0.7 slice-done
  20.8 2.1 %all_gather.43 = f32[2,16,512]{2,1,0:T(8,128)S(1)} all-gather(f32[1,16,512]{2,1,0:T(8,128)S(1)} %slice-done), channel_id=1, replica_groups=mesh['x'=4,'y'=4,'z'=16,'core'=2] {'core'}, dimensions={0}, use_global_device_ids=true | all-gather | bytes 98304 | tf_op jit(solution)/shard_map/all_gather | solution.py:31
  23.0 2.2 %all_gather.44 = bf16[2,256,512]{2,1,0:T(8,128)(2,1)S(1)} all-gather(bf16[1,256,512]{2,1,0:T(8,128)(2,1)S(1)} %get-tuple-element.65), channel_id=1, replica_groups=mesh['x'=4,'y'=4,'z'=16,'core'=2] {'core'}, dimensions={0}, use_global_device_ids=true | all-gather | bytes 786432 | tf_op jit(solution)/shard_map/all_gather | solution.py:31
  25.1 2.3 %all_gather.41 = bf16[2,256,512]{2,1,0:T(8,128)(2,1)S(1)} all-gather(bf16[1,256,512]{2,1,0:T(8,128)(2,1)S(1)} %get-tuple-element.66), channel_id=1, replica_groups=mesh['x'=4,'y'=4,'z'=16,'core'=2] {'core'}, dimensions={0}, use_global_device_ids=true | all-gather | bytes 786432 | tf_op jit(solution)/shard_map/all_gather | solution.py:31
  27.5 2.2 %all_gather.45 = bf16[2,512,256]{2,1,0:T(8,128)(2,1)S(1)} all-gather(bf16[1,512,256]{2,1,0:T(8,128)(2,1)S(1)} %get-tuple-element.63), channel_id=1, replica_groups=mesh['x'=4,'y'=4,'z'=16,'core'=2] {'core'}, dimensions={0}, use_global_device_ids=true | all-gather | bytes 786432 | tf_op jit(solution)/shard_map/all_gather | solution.py:31
  29.7 2.2 %all_gather.42 = bf16[2,512,256]{2,1,0:T(8,128)(2,1)S(1)} all-gather(bf16[1,512,256]{2,1,0:T(8,128)(2,1)S(1)} %get-tuple-element.64), channel_id=1, replica_groups=mesh['x'=4,'y'=4,'z'=16,'core'=2] {'core'}, dimensions={0}, use_global_device_ids=true | all-gather | bytes 786432 | tf_op jit(solution)/shard_map/all_gather | solution.py:31
  31.8 2.2 %all-to-all-done = bf16[16,32,256]{2,1,0:T(8,128)(2,1)S(1)} async-done(((bf16[16,32,256]{2,1,0:T(8,128)(2,1)}), bf16[16,32,256]{2,1,0:T(8,128)(2,1)S(1)}, u32[]{:S(2)}, u32[]{:S(2)}) %all-to-all-start) | async-done | bytes 262176 | tf_op jit(solution)/shard_map/all_to_all | solution.py:14
  34.1 0.3 convolution_convert_fusion.1
  34.4 13.9 %all_to_all.45 = bf16[16,32,256]{2,1,0:T(8,128)(2,1)S(1)} all-to-all(bf16[16,32,256]{2,1,0:T(8,128)(2,1)S(1)} %bitcast.90), channel_id=1, replica_groups=mesh['x'=4,'y'=4,'z'=16,'core'=2] {'x','y'}, dimensions={0} | all-to-all | bytes 524288 | tf_op jit(solution)/shard_map/all_to_all | solution.py:14
  48.3 10.5 %all_to_all.46 = bf16[16,32,256]{2,1,0:T(8,128)(2,1)S(1)} all-to-all(bf16[16,32,256]{2,1,0:T(8,128)(2,1)S(1)} %broadcast_in_dim.18), channel_id=1, replica_groups=mesh['x'=4,'y'=4,'z'=16,'core'=2] {'x','y'}, dimensions={0} | all-to-all | bytes 524288 | tf_op jit(solution)/shard_map/all_to_all | solution.py:14
  59.1 0.9 fusion.2
  60.0 10.5 %all-to-all-start.3 = ((bf16[16,32,256]{2,1,0:T(8,128)(2,1)}), bf16[16,32,256]{2,1,0:T(8,128)(2,1)S(1)}, u32[]{:S(2)}, u32[]{:S(2)}) async-start(bf16[16,32,256]{2,1,0:T(8,128)(2,1)} %bitcast.9), calls=%async_computation.3 | async-start | bytes 524288 | tf_op jit(solution)/shard_map/all_to_all | solution.py:14
  71.0 5.3 %all-gather = bf16[1024,256]{1,0:T(8,128)(2,1)S(1)} all-gather(bf16[512,256]{1,0:T(8,128)(2,1)S(1)} %bitcast.76), channel_id=2, replica_groups=mesh['x'=4,'y'=4,'z'=16,'core'=2] {'core'}, dimensions={0}, use_global_device_ids=true | all-gather | bytes 786432 | tf_op jit(solution)/shard_map/all_gather | solution.py:31
  76.4 0.9 copy-done.2
  77.3 2.2 %all-gather.1 = bf16[1024,256]{1,0:T(8,128)(2,1)S(1)} all-gather(bf16[512,256]{1,0:T(8,128)(2,1)S(1)} %bitcast.99), channel_id=3, replica_groups=mesh['x'=4,'y'=4,'z'=16,'core'=2] {'core'}, dimensions={0}, use_global_device_ids=true | all-gather | bytes 786432 | tf_op jit(solution)/shard_map/all_gather | solution.py:31
  79.8 3.6 %all-to-all-done.3 = bf16[16,32,256]{2,1,0:T(8,128)(2,1)S(1)} async-done(((bf16[16,32,256]{2,1,0:T(8,128)(2,1)}), bf16[16,32,256]{2,1,0:T(8,128)(2,1)S(1)}, u32[]{:S(2)}, u32[]{:S(2)}) %all-to-all-start.3) | async-done | bytes 262176 | tf_op jit(solution)/shard_map/all_to_all | solution.py:14
  83.4 21.6 %all_to_all.47 = bf16[16,32,256]{2,1,0:T(8,128)(2,1)S(1)} all-to-all(bf16[16,32,256]{2,1,0:T(8,128)(2,1)S(1)} %broadcast_in_dim.19), channel_id=1, replica_groups=mesh['x'=4,'y'=4,'z'=16,'core'=2] {'z'}, dimensions={0} | all-to-all | bytes 524288 | tf_op jit(solution)/shard_map/all_to_all | solution.py:14
  105.3 11.2 %all_to_all.48 = bf16[16,32,256]{2,1,0:T(8,128)(2,1)S(1)} all-to-all(bf16[16,32,256]{2,1,0:T(8,128)(2,1)S(1)} %bitcast.92), channel_id=1, replica_groups=mesh['x'=4,'y'=4,'z'=16,'core'=2] {'x','y'}, dimensions={0} | all-to-all | bytes 524288 | tf_op jit(solution)/shard_map/all_to_all | solution.py:14
  116.5 10.5 %all_to_all.49 = bf16[16,32,256]{2,1,0:T(8,128)(2,1)S(1)} all-to-all(bf16[16,32,256]{2,1,0:T(8,128)(2,1)S(1)} %broadcast_in_dim.20), channel_id=1, replica_groups=mesh['x'=4,'y'=4,'z'=16,'core'=2] {'x','y'}, dimensions={0} | all-to-all | bytes 524288 | tf_op jit(solution)/shard_map/all_to_all | solution.py:14
  127.0 11.4 %all_gather.50 = bf16[2,512,256]{2,1,0:T(8,128)(2,1)S(1)} all-gather(bf16[1,512,256]{2,1,0:T(8,128)(2,1)S(1)} %bitcast.78), channel_id=1, replica_groups=mesh['x'=4,'y'=4,'z'=16,'core'=2] {'core'}, dimensions={0}, use_global_device_ids=true | all-gather | bytes 786432 | tf_op jit(solution)/shard_map/all_gather | solution.py:31
  139.3 22.2 %all_to_all.50 = bf16[16,48,256]{2,1,0:T(8,128)(2,1)S(1)} all-to-all(bf16[16,48,256]{2,1,0:T(8,128)(2,1)S(1)} %pad_maximum_fusion.2), channel_id=1, replica_groups=mesh['x'=4,'y'=4,'z'=16,'core'=2] {'z'}, dimensions={0} | all-to-all | bytes 786432 | tf_op jit(solution)/shard_map/all_to_all | solution.py:14
  161.6 0.7 broadcast_in_dim.22
  162.4 11.6 %all-to-all-start.8 = ((bf16[32,16,256]{2,1,0:T(8,128)(2,1)}), bf16[32,16,256]{2,1,0:T(8,128)(2,1)S(1)}, u32[]{:S(2)}, u32[]{:S(2)}) async-start(bf16[32,16,256]{2,1,0:T(8,128)(2,1)} %broadcast_in_dim.22), calls=%async_computation.8 | async-start | bytes 524288 | tf_op jit(solution)/shard_map/all_to_all | solution.py:14
  174.0 1.9 %all-gather.2 = f32[64,256]{1,0:T(8,128)S(1)} all-gather(f32[32,256]{1,0:T(8,128)S(1)} %convert_reduce_fusion), channel_id=4, replica_groups=mesh['x'=4,'y'=4,'z'=16,'core'=2] {'core'}, dimensions={0}, use_global_device_ids=true | all-gather | bytes 98304 | tf_op jit(solution)/shard_map/all_gather | solution.py:31
  175.8 0.8 pad_maximum_fusion
  176.7 0.6 fusion.23
  177.3 5.6 %all-to-all-done.8 = bf16[32,16,256]{2,1,0:T(8,128)(2,1)S(1)} async-done(((bf16[32,16,256]{2,1,0:T(8,128)(2,1)}), bf16[32,16,256]{2,1,0:T(8,128)(2,1)S(1)}, u32[]{:S(2)}, u32[]{:S(2)}) %all-to-all-start.8) | async-done | bytes 262176 | tf_op jit(solution)/shard_map/all_to_all | solution.py:14
  183.0 0.9 pad_maximum_fusion.1
  (40 shorter events, 2.7 us)
Async XLA Ops:
  9.8 13.2 %copy-start = (bf16[2,256,512]{2,1,0:T(8,128)(2,1)S(1)}, bf16[2,256,512]{2,1,0:T(8,128)(2,1)}, u32[]{:S(2)}) copy-start(bf16[2,256,512]{2,1,0:T(8,128)(2,1)} %param.5) | copy-start | bytes 1572868
  10.5 23.6 %all-to-all-start = ((bf16[16,32,256]{2,1,0:T(8,128)(2,1)}), bf16[16,32,256]{2,1,0:T(8,128)(2,1)S(1)}, u32[]{:S(2)}, u32[]{:S(2)}) async-start(bf16[16,32,256]{2,1,0:T(8,128)(2,1)} %broadcast_in_dim.17), calls=%async_computation | async-start | bytes 524288 | tf_op jit(solution)/shard_map/all_to_all | solution.py:14
  20.0 0.8 slice-start
  25.1 2.3 %copy-start.1 = (bf16[2,512,256]{2,1,0:T(8,128)(2,1)S(1)}, bf16[2,512,256]{2,1,0:T(8,128)(2,1)}, u32[]{:S(2)}) copy-start(bf16[2,512,256]{2,1,0:T(8,128)(2,1)} %param.6) | copy-start | bytes 1572868
  60.0 23.3 %all-to-all-start.3 = ((bf16[16,32,256]{2,1,0:T(8,128)(2,1)}), bf16[16,32,256]{2,1,0:T(8,128)(2,1)S(1)}, u32[]{:S(2)}, u32[]{:S(2)}) async-start(bf16[16,32,256]{2,1,0:T(8,128)(2,1)} %bitcast.9), calls=%async_computation.3 | async-start | bytes 524288 | tf_op jit(solution)/shard_map/all_to_all | solution.py:14
  76.4 1.0 copy-start.2
  162.4 20.6 %all-to-all-start.8 = ((bf16[32,16,256]{2,1,0:T(8,128)(2,1)}), bf16[32,16,256]{2,1,0:T(8,128)(2,1)S(1)}, u32[]{:S(2)}, u32[]{:S(2)}) async-start(bf16[32,16,256]{2,1,0:T(8,128)(2,1)} %broadcast_in_dim.22), calls=%async_computation.8 | async-start | bytes 524288 | tf_op jit(solution)/shard_map/all_to_all | solution.py:14
  175.8 0.9 copy-start.3

commit v6 on v5

--- a/solution.py
+++ b/solution.py
@@ -67,10 +67,10 @@
         right = lax.dynamic_slice(whole, (one, start, zero), sizes)
         return jnp.concatenate([left[0], right[0]], axis=1)
 
-    first = both_cores(outputs[0].astype(BF))
-    first = window(first, core * half, half, 2).reshape(height, half)
+    given = window(both_cores(outputs), core * half, half, 3)
+    first = given[:, 0].astype(BF).reshape(height, half)
     gathered = spread(first, "z", 16).reshape(-1, half)
-    second = window(both_cores(outputs[1]), core * half, half, 2)
+    second = given[:, 1]
     rows = inverses.shape[1]
     gathered, inverse0, former0, second, inverse1, former1, *starts = together(
         (

time: 185 us -> 184 us (level)
  blocking collectives: 130 us -> 128 us
  waiting for transfers between devices: 11.4 us -> 13.3 us
    all_gather x10 -> x9, blocking collectives: 40 us -> 38.5 us  [both_cores(): return lax.all_gather(block, 'core', axis=0)]
  transfers between devices with their start and end apart: 3 -> 3, of which waited for: 3 -> 3; matrix products, arithmetic and copies ran while one was open for 1% -> 2% of each run, Pallas kernels for 0% -> 0%
where the time goes in v6:
time: 184 us; the launch traced here: 183 us
  blocking collectives  128 us (70%)
  starting transfers between devices  31.7 us (17%)
  waiting for transfers between devices  13.3 us (7%)
  other arithmetic  3.36 us (2%)
  matrix products  3.17 us (2%)
  local copies, waits for them, and re-layouts  2.75 us (1%)
    all_to_all x6, blocking collectives, swap(): return lax.all_to_all(pieces, axis, 0, 0)  89.9 us
    all_gather x9, blocking collectives, both_cores(): return lax.all_gather(block, 'core', axis=0)  38.5 us
    all_to_all x3, starting transfers between devices, swap(): return lax.all_to_all(pieces, axis, 0, 0)  31.7 us
    all_to_all x3, waiting for transfers between devices, swap(): return lax.all_to_all(pieces, axis, 0, 0)  13.3 us
  transfers between devices with their start and end apart: 3, of which 3 were waited for; matrix products, arithmetic and copies ran while one was open for 2% of the time, Pallas kernels for 0%

profile of v6, /device:TPU:1, one launch (start us, length us, event | category | flops | bytes accessed | tf_op | source)
XLA Modules:
  0.0 183.4 jit_solution(9914047538180917438)
XLA Ops:
  0.6 8.7 %all-gather = f32[6,16,512]{2,1,0:T(8,128)S(1)} all-gather(f32[3,16,512]{2,1,0:T(8,128)} %param.4), channel_id=2, replica_groups=mesh['x'=4,'y'=4,'z'=16,'core'=2] {'core'}, dimensions={0}, use_global_device_ids=true | all-gather | bytes 294912 | tf_op jit(solution)/shard_map/all_gather | solution.py:31
  9.3 0.7 broadcast_in_dim.14
  10.1 9.5 %all-to-all-start = ((bf16[16,32,256]{2,1,0:T(8,128)(2,1)}), bf16[16,32,256]{2,1,0:T(8,128)(2,1)S(1)}, u32[]{:S(2)}, u32[]{:S(2)}) async-start(bf16[16,32,256]{2,1,0:T(8,128)(2,1)} %broadcast_in_dim.14), calls=%async_computation | async-start | bytes 524288 | tf_op jit(solution)/shard_map/all_to_all | solution.py:14
  19.7 2.4 %all_gather.43 = bf16[2,256,512]{2,1,0:T(8,128)(2,1)S(1)} all-gather(bf16[1,256,512]{2,1,0:T(8,128)(2,1)S(1)} %get-tuple-element.65), channel_id=1, replica_groups=mesh['x'=4,'y'=4,'z'=16,'core'=2] {'core'}, dimensions={0}, use_global_device_ids=true | all-gather | bytes 786432 | tf_op jit(solution)/shard_map/all_gather | solution.py:31
  22.1 2.3 %all_gather.41 = bf16[2,256,512]{2,1,0:T(8,128)(2,1)S(1)} all-gather(bf16[1,256,512]{2,1,0:T(8,128)(2,1)S(1)} %get-tuple-element.66), channel_id=1, replica_groups=mesh['x'=4,'y'=4,'z'=16,'core'=2] {'core'}, dimensions={0}, use_global_device_ids=true | all-gather | bytes 786432 | tf_op jit(solution)/shard_map/all_gather | solution.py:31
  24.5 2.2 %all_gather.44 = bf16[2,512,256]{2,1,0:T(8,128)(2,1)S(1)} all-gather(bf16[1,512,256]{2,1,0:T(8,128)(2,1)S(1)} %get-tuple-element.63), channel_id=1, replica_groups=mesh['x'=4,'y'=4,'z'=16,'core'=2] {'core'}, dimensions={0}, use_global_device_ids=true | all-gather | bytes 786432 | tf_op jit(solution)/shard_map/all_gather | solution.py:31
  26.7 2.2 %all_gather.42 = bf16[2,512,256]{2,1,0:T(8,128)(2,1)S(1)} all-gather(bf16[1,512,256]{2,1,0:T(8,128)(2,1)S(1)} %get-tuple-element.64), channel_id=1, replica_groups=mesh['x'=4,'y'=4,'z'=16,'core'=2] {'core'}, dimensions={0}, use_global_device_ids=true | all-gather | bytes 786432 | tf_op jit(solution)/shard_map/all_gather | solution.py:31
  28.8 4.8 %all-to-all-done = bf16[16,32,256]{2,1,0:T(8,128)(2,1)S(1)} async-done(((bf16[16,32,256]{2,1,0:T(8,128)(2,1)}), bf16[16,32,256]{2,1,0:T(8,128)(2,1)S(1)}, u32[]{:S(2)}, u32[]{:S(2)}) %all-to-all-start) | async-done | bytes 262176 | tf_op jit(solution)/shard_map/all_to_all | solution.py:14
  33.6 0.3 convolution_convert_fusion.1
  33.9 13.9 %all_to_all.45 = bf16[16,32,256]{2,1,0:T(8,128)(2,1)S(1)} all-to-all(bf16[16,32,256]{2,1,0:T(8,128)(2,1)S(1)} %bitcast.91), channel_id=1, replica_groups=mesh['x'=4,'y'=4,'z'=16,'core'=2] {'x','y'}, dimensions={0} | all-to-all | bytes 524288 | tf_op jit(solution)/shard_map/all_to_all | solution.py:14
  47.9 10.5 %all_to_all.46 = bf16[16,32,256]{2,1,0:T(8,128)(2,1)S(1)} all-to-all(bf16[16,32,256]{2,1,0:T(8,128)(2,1)S(1)} %broadcast_in_dim.15), channel_id=1, replica_groups=mesh['x'=4,'y'=4,'z'=16,'core'=2] {'x','y'}, dimensions={0} | all-to-all | bytes 524288 | tf_op jit(solution)/shard_map/all_to_all | solution.py:14
  58.6 0.9 fusion.2
  59.6 10.5 %all-to-all-start.3 = ((bf16[16,32,256]{2,1,0:T(8,128)(2,1)}), bf16[16,32,256]{2,1,0:T(8,128)(2,1)S(1)}, u32[]{:S(2)}, u32[]{:S(2)}) async-start(bf16[16,32,256]{2,1,0:T(8,128)(2,1)} %bitcast.10), calls=%async_computation.3 | async-start | bytes 524288 | tf_op jit(solution)/shard_map/all_to_all | solution.py:14
  70.6 5.3 %all-gather.1 = bf16[1024,256]{1,0:T(8,128)(2,1)S(1)} all-gather(bf16[512,256]{1,0:T(8,128)(2,1)S(1)} %bitcast.77), channel_id=3, replica_groups=mesh['x'=4,'y'=4,'z'=16,'core'=2] {'core'}, dimensions={0}, use_global_device_ids=true | all-gather | bytes 786432 | tf_op jit(solution)/shard_map/all_gather | solution.py:31
  76.0 0.9 copy-done.2
  76.9 2.2 %all-gather.2 = bf16[1024,256]{1,0:T(8,128)(2,1)S(1)} all-gather(bf16[512,256]{1,0:T(8,128)(2,1)S(1)} %bitcast.102), channel_id=4, replica_groups=mesh['x'=4,'y'=4,'z'=16,'core'=2] {'core'}, dimensions={0}, use_global_device_ids=true | all-gather | bytes 786432 | tf_op jit(solution)/shard_map/all_gather | solution.py:31
  79.0 0.3 fusion.4
  79.3 3.6 %all-to-all-done.3 = bf16[16,32,256]{2,1,0:T(8,128)(2,1)S(1)} async-done(((bf16[16,32,256]{2,1,0:T(8,128)(2,1)}), bf16[16,32,256]{2,1,0:T(8,128)(2,1)S(1)}, u32[]{:S(2)}, u32[]{:S(2)}) %all-to-all-start.3) | async-done | bytes 262176 | tf_op jit(solution)/shard_map/all_to_all | solution.py:14
  83.0 21.6 %all_to_all.47 = bf16[16,32,256]{2,1,0:T(8,128)(2,1)S(1)} all-to-all(bf16[16,32,256]{2,1,0:T(8,128)(2,1)S(1)} %broadcast_in_dim.16), channel_id=1, replica_groups=mesh['x'=4,'y'=4,'z'=16,'core'=2] {'z'}, dimensions={0} | all-to-all | bytes 524288 | tf_op jit(solution)/shard_map/all_to_all | solution.py:14
  104.6 0.3 convolution_convert_fusion
  104.9 11.2 %all_to_all.48 = bf16[16,32,256]{2,1,0:T(8,128)(2,1)S(1)} all-to-all(bf16[16,32,256]{2,1,0:T(8,128)(2,1)S(1)} %bitcast.93), channel_id=1, replica_groups=mesh['x'=4,'y'=4,'z'=16,'core'=2] {'x','y'}, dimensions={0} | all-to-all | bytes 524288 | tf_op jit(solution)/shard_map/all_to_all | solution.py:14
  116.1 10.5 %all_to_all.49 = bf16[16,32,256]{2,1,0:T(8,128)(2,1)S(1)} all-to-all(bf16[16,32,256]{2,1,0:T(8,128)(2,1)S(1)} %broadcast_in_dim.17), channel_id=1, replica_groups=mesh['x'=4,'y'=4,'z'=16,'core'=2] {'x','y'}, dimensions={0} | all-to-all | bytes 524288 | tf_op jit(solution)/shard_map/all_to_all | solution.py:14
  126.6 11.4 %all_gather.49 = bf16[2,512,256]{2,1,0:T(8,128)(2,1)S(1)} all-gather(bf16[1,512,256]{2,1,0:T(8,128)(2,1)S(1)} %bitcast.79), channel_id=1, replica_groups=mesh['x'=4,'y'=4,'z'=16,'core'=2] {'core'}, dimensions={0}, use_global_device_ids=true | all-gather | bytes 786432 | tf_op jit(solution)/shard_map/all_gather | solution.py:31
  138.2 0.3 fusion.3
  138.8 22.2 %all_to_all.50 = bf16[16,48,256]{2,1,0:T(8,128)(2,1)S(1)} all-to-all(bf16[16,48,256]{2,1,0:T(8,128)(2,1)S(1)} %pad_maximum_fusion.2), channel_id=1, replica_groups=mesh['x'=4,'y'=4,'z'=16,'core'=2] {'z'}, dimensions={0} | all-to-all | bytes 786432 | tf_op jit(solution)/shard_map/all_to_all | solution.py:14
  161.1 0.7 broadcast_in_dim.19
  161.9 11.6 %all-to-all-start.8 = ((bf16[32,16,256]{2,1,0:T(8,128)(2,1)}), bf16[32,16,256]{2,1,0:T(8,128)(2,1)S(1)}, u32[]{:S(2)}, u32[]{:S(2)}) async-start(bf16[32,16,256]{2,1,0:T(8,128)(2,1)} %broadcast_in_dim.19), calls=%async_computation.8 | async-start | bytes 524288 | tf_op jit(solution)/shard_map/all_to_all | solution.py:14
  173.5 1.9 %all-gather.3 = f32[64,256]{1,0:T(8,128)S(1)} all-gather(f32[32,256]{1,0:T(8,128)S(1)} %convert_reduce_fusion), channel_id=5, replica_groups=mesh['x'=4,'y'=4,'z'=16,'core'=2] {'core'}, dimensions={0}, use_global_device_ids=true | all-gather | bytes 98304 | tf_op jit(solution)/shard_map/all_gather | solution.py:31
  175.4 0.8 pad_maximum_fusion
  176.2 1.4 fusion.23
  177.6 4.9 %all-to-all-done.8 = bf16[32,16,256]{2,1,0:T(8,128)(2,1)S(1)} async-done(((bf16[32,16,256]{2,1,0:T(8,128)(2,1)}), bf16[32,16,256]{2,1,0:T(8,128)(2,1)S(1)}, u32[]{:S(2)}, u32[]{:S(2)}) %all-to-all-start.8) | async-done | bytes 262176 | tf_op jit(solution)/shard_map/all_to_all | solution.py:14
  182.6 0.9 pad_maximum_fusion.1
  (34 shorter events, 1.8 us)
Async XLA Ops:
  9.3 10.3 %copy-start = (bf16[2,256,512]{2,1,0:T(8,128)(2,1)S(1)}, bf16[2,256,512]{2,1,0:T(8,128)(2,1)}, u32[]{:S(2)}) copy-start(bf16[2,256,512]{2,1,0:T(8,128)(2,1)} %param.5) | copy-start | bytes 1572868
  10.1 23.6 %all-to-all-start = ((bf16[16,32,256]{2,1,0:T(8,128)(2,1)}), bf16[16,32,256]{2,1,0:T(8,128)(2,1)S(1)}, u32[]{:S(2)}, u32[]{:S(2)}) async-start(bf16[16,32,256]{2,1,0:T(8,128)(2,1)} %broadcast_in_dim.14), calls=%async_computation | async-start | bytes 524288 | tf_op jit(solution)/shard_map/all_to_all | solution.py:14
  22.1 2.3 %copy-start.1 = (bf16[2,512,256]{2,1,0:T(8,128)(2,1)S(1)}, bf16[2,512,256]{2,1,0:T(8,128)(2,1)}, u32[]{:S(2)}) copy-start(bf16[2,512,256]{2,1,0:T(8,128)(2,1)} %param.6) | copy-start | bytes 1572868
  59.6 23.3 %all-to-all-start.3 = ((bf16[16,32,256]{2,1,0:T(8,128)(2,1)}), bf16[16,32,256]{2,1,0:T(8,128)(2,1)S(1)}, u32[]{:S(2)}, u32[]{:S(2)}) async-start(bf16[16,32,256]{2,1,0:T(8,128)(2,1)} %bitcast.10), calls=%async_computation.3 | async-start | bytes 524288 | tf_op jit(solution)/shard_map/all_to_all | solution.py:14
  75.9 1.0 copy-start.2
  161.9 20.6 %all-to-all-start.8 = ((bf16[32,16,256]{2,1,0:T(8,128)(2,1)}), bf16[32,16,256]{2,1,0:T(8,128)(2,1)S(1)}, u32[]{:S(2)}, u32[]{:S(2)}) async-start(bf16[32,16,256]{2,1,0:T(8,128)(2,1)} %broadcast_in_dim.19), calls=%async_computation.8 | async-start | bytes 524288 | tf_op jit(solution)/shard_map/all_to_all | solution.py:14

commit v7 on v6

--- a/solution.py
+++ b/solution.py
@@ -6,7 +6,8 @@
 BF = jnp.bfloat16
 F32 = jnp.float32
 ROW = ("x", "y")
-COL = ("z", "core")
+Z = ("eight", "pair")
+COL = Z + ("core",)
 together = lax.optimization_barrier
 
 
@@ -69,7 +70,7 @@
 
     given = window(both_cores(outputs), core * half, half, 3)
     first = given[:, 0].astype(BF).reshape(height, half)
-    gathered = spread(first, "z", 16).reshape(-1, half)
+    gathered = spread(first, Z, 16).reshape(-1, half)
     second = given[:, 1]
     rows = inverses.shape[1]
     gathered, inverse0, former0, second, inverse1, former1, *starts = together(
@@ -90,7 +91,7 @@
 
     pieces = cut(panel(former0, white0), 16)
     pieces, white0 = together((pieces, white0))
-    pieces = swap(pieces, "z")
+    pieces = swap(pieces, Z)
     last, white0, latter0 = together((panel(former1, white0), white0, latter[0]))
     whole0 = both_cores(white0)
     pieces, last, slabs0, block0, latter0 = together(
@@ -103,7 +104,7 @@
         )
     )
     right = (second - total(pieces)).astype(BF)
-    gathered = spread(right, "z", 16).reshape(-1, half)
+    gathered = spread(right, Z, 16).reshape(-1, half)
     white1 = whiten(inverse1.reshape(-1, inverse1.shape[2]), gathered)
 
     whole1 = both_cores(white1)
@@ -111,10 +112,23 @@
     slabs = slabs0 + gram(whole1, white1)
     part = half // 16
     slab = window(slabs, slab_start, part, 0).astype(BF)
+    steps = last.astype(BF).reshape(8, 2, height, half).swapaxes(0, 1)
     pieces = jnp.concatenate(
-        [cut(last, 16), jnp.broadcast_to(slab[None], (16, part, half))], axis=1
+        [
+            steps.reshape(2, 8 * height, half),
+            jnp.broadcast_to(slab[None], (2, part, half)),
+        ],
+        axis=1,
     )
-    pieces, whole1 = together((swap(pieces, "z"), whole1))
+    summed = total(swap(pieces, "pair")).astype(BF)
+    pieces = jnp.concatenate(
+        [
+            summed[: 8 * height].reshape(8, height, half),
+            jnp.broadcast_to(summed[None, 8 * height :], (8, part, half)),
+        ],
+        axis=1,
+    )
+    pieces, whole1 = together((swap(pieces, "eight"), whole1))
     slab = total(pieces[:, height:]).astype(BF)
     ends = total(pieces[:, :height])
     pieces, ends, whole1 = together((jnp.broadcast_to(slab[None], (32,) + slab.shape), ends, whole1))
@@ -130,8 +144,8 @@
 
 
 def solution(mesh):
-    grid = Mesh(mesh.devices.reshape(4, 4, 16, 2), ("x", "y", "z", "core"))
-    every = ("x", "y", "z", "core")
+    every = ROW + COL
+    grid = Mesh(mesh.devices.reshape(4, 4, 8, 2, 2), every)
     in_specs = (P(None, every, None), P(None, COL, ROW), P(None, ROW, COL), P(None, ROW, COL))
     out_specs = (P(None, COL, None), P(None, every, None), P())
     return jax.shard_map(body, mesh=grid, in_specs=in_specs, out_specs=out_specs, check_vma=False)

time: 184 us -> 186 us (1.011)
  blocking collectives: 128 us -> 134 us
  starting transfers between devices: 31.7 us -> 28 us
    all_to_all x6 -> x7, blocking collectives: 89.9 us -> 95.2 us  [swap(): return lax.all_to_all(pieces, axis, 0, 0)]
    all_to_all x3, starting transfers between devices: 31.7 us -> 28 us  [swap(): return lax.all_to_all(pieces, axis, 0, 0)]
where the time goes in v7:
time: 186 us; the launch traced here: 185 us
  blocking collectives  134 us (72%)
  starting transfers between devices  28 us (15%)
  waiting for transfers between devices  13.3 us (7%)
  other arithmetic  3.37 us (2%)
  matrix products  3.16 us (2%)
  local copies, waits for them, and re-layouts  2.79 us (2%)
    all_to_all x7, blocking collectives, swap(): return lax.all_to_all(pieces, axis, 0, 0)  95.2 us
    all_gather x9, blocking collectives, both_cores(): return lax.all_gather(block, 'core', axis=0)  38.5 us
    all_to_all x3, starting transfers between devices, swap(): return lax.all_to_all(pieces, axis, 0, 0)  28 us
    all_to_all x3, waiting for transfers between devices, swap(): return lax.all_to_all(pieces, axis, 0, 0)  13.3 us
  transfers between devices with their start and end apart: 3, of which 3 were waited for; matrix products, arithmetic and copies ran while one was open for 2% of the time, Pallas kernels for 0%

profile of v7, /device:TPU:1, one launch (start us, length us, event | category | flops | bytes accessed | tf_op | source)
XLA Modules:
  0.0 185.2 jit_solution(3004855332754162324)
XLA Ops:
  0.6 8.7 %all-gather = f32[6,16,512]{2,1,0:T(8,128)S(1)} all-gather(f32[3,16,512]{2,1,0:T(8,128)} %param.4), channel_id=2, replica_groups=mesh['x'=4,'y'=4,'eight'=8,'pair'=2,'core'=2] {'core'}, dimensions={0}, use_global_device_ids=true | all-gather | bytes 294912 | tf_op jit(solution)/shard_map/all_gather | solution.py:32
  9.3 0.7 broadcast_in_dim.16
  10.1 9.5 %all-to-all-start = ((bf16[16,32,256]{2,1,0:T(8,128)(2,1)}), bf16[16,32,256]{2,1,0:T(8,128)(2,1)S(1)}, u32[]{:S(2)}, u32[]{:S(2)}) async-start(bf16[16,32,256]{2,1,0:T(8,128)(2,1)} %broadcast_in_dim.16), calls=%async_computation | async-start | bytes 524288 | tf_op jit(solution)/shard_map/all_to_all | solution.py:15
  19.7 2.4 %all_gather.43 = bf16[2,256,512]{2,1,0:T(8,128)(2,1)S(1)} all-gather(bf16[1,256,512]{2,1,0:T(8,128)(2,1)S(1)} %get-tuple-element.65), channel_id=1, replica_groups=mesh['x'=4,'y'=4,'eight'=8,'pair'=2,'core'=2] {'core'}, dimensions={0}, use_global_device_ids=true | all-gather | bytes 786432 | tf_op jit(solution)/shard_map/all_gather | solution.py:32
  22.1 2.3 %all_gather.41 = bf16[2,256,512]{2,1,0:T(8,128)(2,1)S(1)} all-gather(bf16[1,256,512]{2,1,0:T(8,128)(2,1)S(1)} %get-tuple-element.66), channel_id=1, replica_groups=mesh['x'=4,'y'=4,'eight'=8,'pair'=2,'core'=2] {'core'}, dimensions={0}, use_global_device_ids=true | all-gather | bytes 786432 | tf_op jit(solution)/shard_map/all_gather | solution.py:32
  24.5 2.2 %all_gather.44 = bf16[2,512,256]{2,1,0:T(8,128)(2,1)S(1)} all-gather(bf16[1,512,256]{2,1,0:T(8,128)(2,1)S(1)} %get-tuple-element.63), channel_id=1, replica_groups=mesh['x'=4,'y'=4,'eight'=8,'pair'=2,'core'=2] {'core'}, dimensions={0}, use_global_device_ids=true | all-gather | bytes 786432 | tf_op jit(solution)/shard_map/all_gather | solution.py:32
  26.7 2.2 %all_gather.42 = bf16[2,512,256]{2,1,0:T(8,128)(2,1)S(1)} all-gather(bf16[1,512,256]{2,1,0:T(8,128)(2,1)S(1)} %get-tuple-element.64), channel_id=1, replica_groups=mesh['x'=4,'y'=4,'eight'=8,'pair'=2,'core'=2] {'core'}, dimensions={0}, use_global_device_ids=true | all-gather | bytes 786432 | tf_op jit(solution)/shard_map/all_gather | solution.py:32
  28.8 4.8 %all-to-all-done = bf16[16,32,256]{2,1,0:T(8,128)(2,1)S(1)} async-done(((bf16[16,32,256]{2,1,0:T(8,128)(2,1)}), bf16[16,32,256]{2,1,0:T(8,128)(2,1)S(1)}, u32[]{:S(2)}, u32[]{:S(2)}) %all-to-all-start) | async-done | bytes 262176 | tf_op jit(solution)/shard_map/all_to_all | solution.py:15
  33.6 0.3 convolution_convert_fusion.1
  33.9 13.9 %all_to_all.50 = bf16[16,32,256]{2,1,0:T(8,128)(2,1)S(1)} all-to-all(bf16[16,32,256]{2,1,0:T(8,128)(2,1)S(1)} %bitcast.96), channel_id=1, replica_groups=mesh['x'=4,'y'=4,'eight'=8,'pair'=2,'core'=2] {'x','y'}, dimensions={0} | all-to-all | bytes 524288 | tf_op jit(solution)/shard_map/all_to_all | solution.py:15
  47.9 10.5 %all_to_all.51 = bf16[16,32,256]{2,1,0:T(8,128)(2,1)S(1)} all-to-all(bf16[16,32,256]{2,1,0:T(8,128)(2,1)S(1)} %broadcast_in_dim.17), channel_id=1, replica_groups=mesh['x'=4,'y'=4,'eight'=8,'pair'=2,'core'=2] {'x','y'}, dimensions={0} | all-to-all | bytes 524288 | tf_op jit(solution)/shard_map/all_to_all | solution.py:15
  58.6 0.9 fusion.2
  59.6 10.5 %all-to-all-start.3 = ((bf16[16,32,256]{2,1,0:T(8,128)(2,1)}), bf16[16,32,256]{2,1,0:T(8,128)(2,1)S(1)}, u32[]{:S(2)}, u32[]{:S(2)}) async-start(bf16[16,32,256]{2,1,0:T(8,128)(2,1)} %bitcast.10), calls=%async_computation.3 | async-start | bytes 524288 | tf_op jit(solution)/shard_map/all_to_all | solution.py:15
  70.6 5.3 %all-gather.1 = bf16[1024,256]{1,0:T(8,128)(2,1)S(1)} all-gather(bf16[512,256]{1,0:T(8,128)(2,1)S(1)} %bitcast.81), channel_id=3, replica_groups=mesh['x'=4,'y'=4,'eight'=8,'pair'=2,'core'=2] {'core'}, dimensions={0}, use_global_device_ids=true | all-gather | bytes 786432 | tf_op jit(solution)/shard_map/all_gather | solution.py:32
  76.0 0.9 copy-done.2
  76.9 2.2 %all-gather.2 = bf16[1024,256]{1,0:T(8,128)(2,1)S(1)} all-gather(bf16[512,256]{1,0:T(8,128)(2,1)S(1)} %bitcast.108), channel_id=4, replica_groups=mesh['x'=4,'y'=4,'eight'=8,'pair'=2,'core'=2] {'core'}, dimensions={0}, use_global_device_ids=true | all-gather | bytes 786432 | tf_op jit(solution)/shard_map/all_gather | solution.py:32
  79.0 0.3 fusion.4
  79.3 3.6 %all-to-all-done.3 = bf16[16,32,256]{2,1,0:T(8,128)(2,1)S(1)} async-done(((bf16[16,32,256]{2,1,0:T(8,128)(2,1)}), bf16[16,32,256]{2,1,0:T(8,128)(2,1)S(1)}, u32[]{:S(2)}, u32[]{:S(2)}) %all-to-all-start.3) | async-done | bytes 262176 | tf_op jit(solution)/shard_map/all_to_all | solution.py:15
  83.0 21.6 %all_to_all.52 = bf16[16,32,256]{2,1,0:T(8,128)(2,1)S(1)} all-to-all(bf16[16,32,256]{2,1,0:T(8,128)(2,1)S(1)} %broadcast_in_dim.18), channel_id=1, replica_groups=mesh['x'=4,'y'=4,'eight'=8,'pair'=2,'core'=2] {'eight','pair'}, dimensions={0} | all-to-all | bytes 524288 | tf_op jit(solution)/shard_map/all_to_all | solution.py:15
  104.6 0.3 convolution_convert_fusion
  104.9 11.2 %all_to_all.53 = bf16[16,32,256]{2,1,0:T(8,128)(2,1)S(1)} all-to-all(bf16[16,32,256]{2,1,0:T(8,128)(2,1)S(1)} %bitcast.98), channel_id=1, replica_groups=mesh['x'=4,'y'=4,'eight'=8,'pair'=2,'core'=2] {'x','y'}, dimensions={0} | all-to-all | bytes 524288 | tf_op jit(solution)/shard_map/all_to_all | solution.py:15
  116.1 10.5 %all_to_all.54 = bf16[16,32,256]{2,1,0:T(8,128)(2,1)S(1)} all-to-all(bf16[16,32,256]{2,1,0:T(8,128)(2,1)S(1)} %broadcast_in_dim.19), channel_id=1, replica_groups=mesh['x'=4,'y'=4,'eight'=8,'pair'=2,'core'=2] {'x','y'}, dimensions={0} | all-to-all | bytes 524288 | tf_op jit(solution)/shard_map/all_to_all | solution.py:15
  127.1 11.4 %all_gather.49 = bf16[2,512,256]{2,1,0:T(8,128)(2,1)S(1)} all-gather(bf16[1,512,256]{2,1,0:T(8,128)(2,1)S(1)} %bitcast.83), channel_id=1, replica_groups=mesh['x'=4,'y'=4,'eight'=8,'pair'=2,'core'=2] {'core'}, dimensions={0}, use_global_device_ids=true | all-gather | bytes 786432 | tf_op jit(solution)/shard_map/all_gather | solution.py:32
  138.9 8.1 %all_to_all.55 = bf16[2,272,256]{2,1,0:T(8,128)(2,1)S(1)} all-to-all(bf16[2,272,256]{2,1,0:T(8,128)(2,1)S(1)} %pad_maximum_fusion.2), channel_id=1, replica_groups=mesh['x'=4,'y'=4,'eight'=8,'pair'=2,'core'=2] {'pair'}, dimensions={0} | all-to-all | bytes 557056 | tf_op jit(solution)/shard_map/all_to_all | solution.py:15
  147.1 19.4 %all_to_all.56 = bf16[8,48,256]{2,1,0:T(8,128)(2,1)S(1)} all-to-all(bf16[8,48,256]{2,1,0:T(8,128)(2,1)S(1)} %pad_maximum_fusion.5), channel_id=1, replica_groups=mesh['x'=4,'y'=4,'eight'=8,'pair'=2,'core'=2] {'eight'}, dimensions={0} | all-to-all | bytes 393216 | tf_op jit(solution)/shard_map/all_to_all | solution.py:15
  166.5 0.7 broadcast_in_dim.22
  167.4 7.9 %all-to-all-start.9 = ((bf16[32,16,256]{2,1,0:T(8,128)(2,1)}), bf16[32,16,256]{2,1,0:T(8,128)(2,1)S(1)}, u32[]{:S(2)}, u32[]{:S(2)}) async-start(bf16[32,16,256]{2,1,0:T(8,128)(2,1)} %broadcast_in_dim.22), calls=%async_computation.9 | async-start | bytes 524288 | tf_op jit(solution)/shard_map/all_to_all | solution.py:15
  175.3 1.9 %all-gather.3 = f32[64,256]{1,0:T(8,128)S(1)} all-gather(f32[32,256]{1,0:T(8,128)S(1)} %convert_reduce_fusion.4), channel_id=5, replica_groups=mesh['x'=4,'y'=4,'eight'=8,'pair'=2,'core'=2] {'core'}, dimensions={0}, use_global_device_ids=true | all-gather | bytes 98304 | tf_op jit(solution)/shard_map/all_gather | solution.py:32
  177.1 0.8 pad_maximum_fusion
  178.0 1.4 fusion.23
  179.3 4.9 %all-to-all-done.9 = bf16[32,16,256]{2,1,0:T(8,128)(2,1)S(1)} async-done(((bf16[32,16,256]{2,1,0:T(8,128)(2,1)}), bf16[32,16,256]{2,1,0:T(8,128)(2,1)S(1)}, u32[]{:S(2)}, u32[]{:S(2)}) %all-to-all-start.9) | async-done | bytes 262176 | tf_op jit(solution)/shard_map/all_to_all | solution.py:15
  184.3 0.9 pad_maximum_fusion.1
  (41 shorter events, 2.1 us)
Async XLA Ops:
  9.3 10.3 %copy-start = (bf16[2,256,512]{2,1,0:T(8,128)(2,1)S(1)}, bf16[2,256,512]{2,1,0:T(8,128)(2,1)}, u32[]{:S(2)}) copy-start(bf16[2,256,512]{2,1,0:T(8,128)(2,1)} %param.5) | copy-start | bytes 1572868
  10.1 23.6 %all-to-all-start = ((bf16[16,32,256]{2,1,0:T(8,128)(2,1)}), bf16[16,32,256]{2,1,0:T(8,128)(2,1)S(1)}, u32[]{:S(2)}, u32[]{:S(2)}) async-start(bf16[16,32,256]{2,1,0:T(8,128)(2,1)} %broadcast_in_dim.16), calls=%async_computation | async-start | bytes 524288 | tf_op jit(solution)/shard_map/all_to_all | solution.py:15
  22.1 2.3 %copy-start.1 = (bf16[2,512,256]{2,1,0:T(8,128)(2,1)S(1)}, bf16[2,512,256]{2,1,0:T(8,128)(2,1)}, u32[]{:S(2)}) copy-start(bf16[2,512,256]{2,1,0:T(8,128)(2,1)} %param.6) | copy-start | bytes 1572868
  59.6 23.3 %all-to-all-start.3 = ((bf16[16,32,256]{2,1,0:T(8,128)(2,1)}), bf16[16,32,256]{2,1,0:T(8,128)(2,1)S(1)}, u32[]{:S(2)}, u32[]{:S(2)}) async-start(bf16[16,32,256]{2,1,0:T(8,128)(2,1)} %bitcast.10), calls=%async_computation.3 | async-start | bytes 524288 | tf_op jit(solution)/shard_map/all_to_all | solution.py:15
  75.9 1.0 copy-start.2
  167.4 16.9 %all-to-all-start.9 = ((bf16[32,16,256]{2,1,0:T(8,128)(2,1)}), bf16[32,16,256]{2,1,0:T(8,128)(2,1)S(1)}, u32[]{:S(2)}, u32[]{:S(2)}) async-start(bf16[32,16,256]{2,1,0:T(8,128)(2,1)} %broadcast_in_dim.22), calls=%async_computation.9 | async-start | bytes 524288 | tf_op jit(solution)/shard_map/all_to_all | solution.py:15

commit v8 on v6

--- a/solution.py
+++ b/solution.py
@@ -5,22 +5,31 @@
 
 BF = jnp.bfloat16
 F32 = jnp.float32
-ROW = ("x", "y")
+ROW = "row"
 COL = ("z", "core")
+PLANE = ("row", "core")
+FIRST = {"z": 8, ROW: 10, PLANE: 20}
 together = lax.optimization_barrier
 
 
 def swap(pieces, axis):
-    return lax.all_to_all(pieces, axis, 0, 0)
+    count, first = pieces.shape[0], FIRST[axis]
+    order = [(first + place) % count for place in range(count)]
+    return lax.all_to_all(pieces, axis, 0, 0, axis_index_groups=[order])
+
+
+def turn(pieces, by):
+    return jnp.concatenate([pieces[by:], pieces[:by]], axis=0)
 
 
 def spread(piece, axis, count):
-    return swap(jnp.broadcast_to(piece[None], (count,) + piece.shape), axis)
+    pieces = swap(jnp.broadcast_to(piece[None], (count,) + piece.shape), axis)
+    return turn(pieces, count - FIRST[axis])
 
 
-def cut(partial, count):
+def cut(partial, axis):
     rows, width = partial.shape
-    return partial.astype(BF).reshape(count, rows // count, width)
+    return turn(partial.astype(BF).reshape(16, rows // 16, width), FIRST[axis])
 
 
 def total(pieces):
@@ -40,7 +49,7 @@
 
     def whiten(inverse, rows):
         partial = jnp.dot(inverse, rows, preferred_element_type=F32)
-        piece = total(swap(cut(partial, 16), ROW)).astype(BF)
+        piece = total(swap(cut(partial, ROW), ROW)).astype(BF)
         return spread(piece, ROW, 16).reshape(-1, half)
 
     def panel(tiles, white):
@@ -88,7 +97,7 @@
     block_start, end_start, slab_start = starts
     white0 = whiten(inverse0.reshape(-1, inverse0.shape[2]), gathered)
 
-    pieces = cut(panel(former0, white0), 16)
+    pieces = cut(panel(former0, white0), "z")
     pieces, white0 = together((pieces, white0))
     pieces = swap(pieces, "z")
     last, white0, latter0 = together((panel(former1, white0), white0, latter[0]))
@@ -112,16 +121,17 @@
     part = half // 16
     slab = window(slabs, slab_start, part, 0).astype(BF)
     pieces = jnp.concatenate(
-        [cut(last, 16), jnp.broadcast_to(slab[None], (16, part, half))], axis=1
+        [cut(last, "z"), jnp.broadcast_to(slab[None], (16, part, half))], axis=1
     )
     pieces, whole1 = together((swap(pieces, "z"), whole1))
     slab = total(pieces[:, height:]).astype(BF)
     ends = total(pieces[:, :height])
-    pieces, ends, whole1 = together((jnp.broadcast_to(slab[None], (32,) + slab.shape), ends, whole1))
+    pieces = jnp.broadcast_to(slab[None], (32,) + slab.shape)
+    pieces, ends, whole1 = together((pieces, ends, whole1))
     block1, ends = together((block(whole1, block_start), ends))
     trailing = outputs[2:] - block(both_cores(ends), end_start)[None]
-    parts, trailing = together((swap(pieces, ROW + ("core",)), trailing))
-    parts = parts.astype(F32).reshape(16, 2, part, half)
+    parts, trailing = together((swap(pieces, PLANE), trailing))
+    parts = turn(parts, 32 - FIRST[PLANE]).astype(F32).reshape(16, 2, part, half)
     projections = jnp.concatenate(
         [parts[:, 0].reshape(half, half), parts[:, 1].reshape(half, half)], axis=1
     )
@@ -130,8 +140,8 @@
 
 
 def solution(mesh):
-    grid = Mesh(mesh.devices.reshape(4, 4, 16, 2), ("x", "y", "z", "core"))
-    every = ("x", "y", "z", "core")
+    grid = Mesh(mesh.devices.reshape(16, 16, 2), ("row", "z", "core"))
+    every = ("row", "z", "core")
     in_specs = (P(None, every, None), P(None, COL, ROW), P(None, ROW, COL), P(None, ROW, COL))
     out_specs = (P(None, COL, None), P(None, every, None), P())
     return jax.shard_map(body, mesh=grid, in_specs=in_specs, out_specs=out_specs, check_vma=False)

time: 184 us -> 179 us (0.973)
  waiting for transfers between devices: 13.3 us -> 4.34 us
  blocking collectives: 128 us -> 130 us
    all_to_all x3, waiting for transfers between devices: 13.3 us -> 4.34 us  [swap(): return lax.all_to_all(pieces, axis, 0, 0, axis_index_groups=[order])]
    all_to_all x6, blocking collectives: 89.9 us -> 96.5 us  [swap(): return lax.all_to_all(pieces, axis, 0, 0, axis_index_groups=[order])]
    all_gather x9, blocking collectives: 38.5 us -> 33.5 us  [both_cores(): return lax.all_gather(block, 'core', axis=0)]
  transfers between devices with their start and end apart: 3 -> 3, of which waited for: 3 -> 2; matrix products, arithmetic and copies ran while one was open for 2% -> 2% of each run, Pallas kernels for 0% -> 0%
where the time goes in v8:
time: 179 us; the launch traced here: 178 us
  blocking collectives  130 us (73%)
  starting transfers between devices  33 us (18%)
  waiting for transfers between devices  4.34 us (2%)
  other arithmetic  4.3 us (2%)
  local copies, waits for them, and re-layouts  2.91 us (2%)
  matrix products  2.48 us (1%)
    all_to_all x6, blocking collectives, swap(): return lax.all_to_all(pieces, axis, 0, 0, axis_index_groups=[order])  96.5 us
    all_gather x9, blocking collectives, both_cores(): return lax.all_gather(block, 'core', axis=0)  33.5 us
    all_to_all x3, starting transfers between devices, swap(): return lax.all_to_all(pieces, axis, 0, 0, axis_index_groups=[order])  33 us
    all_to_all x3, waiting for transfers between devices, swap(): return lax.all_to_all(pieces, axis, 0, 0, axis_index_groups=[order])  4.34 us
  transfers between devices with their start and end apart: 3, of which 2 were waited for; matrix products, arithmetic and copies ran while one was open for 2% of the time, Pallas kernels for 0%

profile of v8, /device:TPU:1, one launch (start us, length us, event | category | flops | bytes accessed | tf_op | source)
XLA Modules:
  0.0 178.1 jit_solution(1516003828203648959)
XLA Ops:
  0.6 8.7 %all-gather = f32[6,16,512]{2,1,0:T(8,128)S(1)} all-gather(f32[3,16,512]{2,1,0:T(8,128)} %param.4), channel_id=2, replica_groups=mesh['row'=16,'z'=16,'core'=2] {'core'}, dimensions={0}, use_global_device_ids=true | all-gather | bytes 294912 | tf_op jit(solution)/shard_map/all_gather | solution.py:40
  9.3 0.7 broadcast_in_dim.14
  10.1 12.9 %all-to-all-start = ((bf16[16,32,256]{2,1,0:T(8,128)(2,1)}), bf16[16,32,256]{2,1,0:T(8,128)(2,1)S(1)}, u32[]{:S(2)}, u32[]{:S(2)}) async-start(bf16[16,32,256]{2,1,0:T(8,128)(2,1)} %broadcast_in_dim.14), calls=%async_computation | async-start | bytes 524288 | tf_op jit(solution)/shard_map/all_to_all | solution.py:18
  23.0 2.7 %all_gather.43 = bf16[2,256,512]{2,1,0:T(8,128)(2,1)S(1)} all-gather(bf16[1,256,512]{2,1,0:T(8,128)(2,1)S(1)} %get-tuple-element.65), channel_id=1, replica_groups=mesh['row'=16,'z'=16,'core'=2] {'core'}, dimensions={0}, use_global_device_ids=true | all-gather | bytes 786432 | tf_op jit(solution)/shard_map/all_gather | solution.py:40
  25.8 2.3 %all_gather.41 = bf16[2,256,512]{2,1,0:T(8,128)(2,1)S(1)} all-gather(bf16[1,256,512]{2,1,0:T(8,128)(2,1)S(1)} %get-tuple-element.66), channel_id=1, replica_groups=mesh['row'=16,'z'=16,'core'=2] {'core'}, dimensions={0}, use_global_device_ids=true | all-gather | bytes 786432 | tf_op jit(solution)/shard_map/all_gather | solution.py:40
  28.1 2.2 %all_gather.44 = bf16[2,512,256]{2,1,0:T(8,128)(2,1)S(1)} all-gather(bf16[1,512,256]{2,1,0:T(8,128)(2,1)S(1)} %get-tuple-element.63), channel_id=1, replica_groups=mesh['row'=16,'z'=16,'core'=2] {'core'}, dimensions={0}, use_global_device_ids=true | all-gather | bytes 786432 | tf_op jit(solution)/shard_map/all_gather | solution.py:40
  30.3 2.2 %all_gather.42 = bf16[2,512,256]{2,1,0:T(8,128)(2,1)S(1)} all-gather(bf16[1,512,256]{2,1,0:T(8,128)(2,1)S(1)} %get-tuple-element.64), channel_id=1, replica_groups=mesh['row'=16,'z'=16,'core'=2] {'core'}, dimensions={0}, use_global_device_ids=true | all-gather | bytes 786432 | tf_op jit(solution)/shard_map/all_gather | solution.py:40
  32.5 3.2 %all-to-all-done = bf16[16,32,256]{2,1,0:T(8,128)(2,1)S(1)} async-done(((bf16[16,32,256]{2,1,0:T(8,128)(2,1)}), bf16[16,32,256]{2,1,0:T(8,128)(2,1)S(1)}, u32[]{:S(2)}, u32[]{:S(2)}) %all-to-all-start) | async-done | bytes 262176 | tf_op jit(solution)/shard_map/all_to_all | solution.py:18
  35.7 0.3 convolution_convert_fusion.1
  36.1 11.2 %all_to_all.45 = bf16[16,32,256]{2,1,0:T(8,128)(2,1)S(1)} all-to-all(bf16[16,32,256]{2,1,0:T(8,128)(2,1)S(1)} %pad_maximum_fusion.6), channel_id=1, replica_groups={{320,352,384,416,448,480,0,32,64,96,128,160,192,224,256,288},{321,353,3..., dimensions={0} | all-to-all | bytes 524288 | tf_op jit(solution)/shard_map/all_to_all | solution.py:18
  47.4 10.4 %all_to_all.46 = bf16[16,32,256]{2,1,0:T(8,128)(2,1)S(1)} all-to-all(bf16[16,32,256]{2,1,0:T(8,128)(2,1)S(1)} %broadcast_in_dim.15), channel_id=1, replica_groups={{320,352,384,416,448,480,0,32,64,96,128,160,192,224,256,288},{321,353,3..., dimensions={0} | all-to-all | bytes 524288 | tf_op jit(solution)/shard_map/all_to_all | solution.py:18
  58.2 0.2 fusion.2
  58.5 0.7 pad_maximum_fusion.7
  59.2 11.5 %all-to-all-start.3 = ((bf16[16,32,256]{2,1,0:T(8,128)(2,1)}), bf16[16,32,256]{2,1,0:T(8,128)(2,1)S(1)}, u32[]{:S(2)}, u32[]{:S(2)}) async-start(bf16[16,32,256]{2,1,0:T(8,128)(2,1)} %pad_maximum_fusion.7), calls=%async_computation.3 | async-start | bytes 524288 | tf_op jit(solution)/shard_map/all_to_all | solution.py:18
  71.1 5.1 %all-gather.1 = bf16[1024,256]{1,0:T(8,128)(2,1)S(1)} all-gather(bf16[512,256]{1,0:T(8,128)(2,1)S(1)} %bitcast.81), channel_id=3, replica_groups=mesh['row'=16,'z'=16,'core'=2] {'core'}, dimensions={0}, use_global_device_ids=true | all-gather | bytes 786432 | tf_op jit(solution)/shard_map/all_gather | solution.py:40
  76.4 0.9 copy-done.2
  77.3 2.2 %all-gather.2 = bf16[1024,256]{1,0:T(8,128)(2,1)S(1)} all-gather(bf16[512,256]{1,0:T(8,128)(2,1)S(1)} %bitcast.111), channel_id=4, replica_groups=mesh['row'=16,'z'=16,'core'=2] {'core'}, dimensions={0}, use_global_device_ids=true | all-gather | bytes 786432 | tf_op jit(solution)/shard_map/all_gather | solution.py:40
  79.4 0.3 fusion.4
  79.7 1.1 all-to-all-done.3
  80.9 22.7 %all_to_all.47 = bf16[16,32,256]{2,1,0:T(8,128)(2,1)S(1)} all-to-all(bf16[16,32,256]{2,1,0:T(8,128)(2,1)S(1)} %broadcast_in_dim.16), channel_id=1, replica_groups={{16,18,20,22,24,26,28,30,0,2,4,6,8,10,12,14},{17,19,21,23,25,27,29,31,1..., dimensions={0} | all-to-all | bytes 524288 | tf_op jit(solution)/shard_map/all_to_all | solution.py:18
  103.7 0.3 convolution_convert_fusion
  104.1 11.9 %all_to_all.48 = bf16[16,32,256]{2,1,0:T(8,128)(2,1)S(1)} all-to-all(bf16[16,32,256]{2,1,0:T(8,128)(2,1)S(1)} %pad_maximum_fusion.10), channel_id=1, replica_groups={{320,352,384,416,448,480,0,32,64,96,128,160,192,224,256,288},{321,353,3..., dimensions={0} | all-to-all | bytes 524288 | tf_op jit(solution)/shard_map/all_to_all | solution.py:18
  116.1 10.5 %all_to_all.49 = bf16[16,32,256]{2,1,0:T(8,128)(2,1)S(1)} all-to-all(bf16[16,32,256]{2,1,0:T(8,128)(2,1)S(1)} %broadcast_in_dim.17), channel_id=1, replica_groups={{320,352,384,416,448,480,0,32,64,96,128,160,192,224,256,288},{321,353,3..., dimensions={0} | all-to-all | bytes 524288 | tf_op jit(solution)/shard_map/all_to_all | solution.py:18
  127.1 6.3 %all_gather.49 = bf16[2,512,256]{2,1,0:T(8,128)(2,1)S(1)} all-gather(bf16[1,512,256]{2,1,0:T(8,128)(2,1)S(1)} %bitcast.83), channel_id=1, replica_groups=mesh['row'=16,'z'=16,'core'=2] {'core'}, dimensions={0}, use_global_device_ids=true | all-gather | bytes 786432 | tf_op jit(solution)/shard_map/all_gather | solution.py:40
  133.4 0.3 fusion.3
  133.8 29.7 %all_to_all.50 = bf16[16,48,256]{2,1,0:T(8,128)(2,1)S(1)} all-to-all(bf16[16,48,256]{2,1,0:T(8,128)(2,1)S(1)} %pad_maximum_fusion.2), channel_id=1, replica_groups={{16,18,20,22,24,26,28,30,0,2,4,6,8,10,12,14},{17,19,21,23,25,27,29,31,1..., dimensions={0} | all-to-all | bytes 786432 | tf_op jit(solution)/shard_map/all_to_all | solution.py:18
  163.5 0.7 broadcast_in_dim.19
  164.3 8.7 %all-to-all-start.8 = ((bf16[32,16,256]{2,1,0:T(8,128)(2,1)}), bf16[32,16,256]{2,1,0:T(8,128)(2,1)S(1)}, u32[]{:S(2)}, u32[]{:S(2)}) async-start(bf16[32,16,256]{2,1,0:T(8,128)(2,1)} %broadcast_in_dim.19), calls=%async_computation.8 | async-start | bytes 524288 | tf_op jit(solution)/shard_map/all_to_all | solution.py:18
  173.0 1.9 %all-gather.3 = f32[64,256]{1,0:T(8,128)S(1)} all-gather(f32[32,256]{1,0:T(8,128)S(1)} %convert_reduce_fusion), channel_id=5, replica_groups=mesh['row'=16,'z'=16,'core'=2] {'core'}, dimensions={0}, use_global_device_ids=true | all-gather | bytes 98304 | tf_op jit(solution)/shard_map/all_gather | solution.py:40
  174.9 0.8 pad_maximum_fusion
  175.7 1.4 fusion.25
  177.2 0.9 pad_maximum_fusion.1
  (58 shorter events, 2.2 us)
Async XLA Ops:
  9.3 13.7 %copy-start = (bf16[2,256,512]{2,1,0:T(8,128)(2,1)S(1)}, bf16[2,256,512]{2,1,0:T(8,128)(2,1)}, u32[]{:S(2)}) copy-start(bf16[2,256,512]{2,1,0:T(8,128)(2,1)} %param.5) | copy-start | bytes 1572868
  10.1 25.6 %all-to-all-start = ((bf16[16,32,256]{2,1,0:T(8,128)(2,1)}), bf16[16,32,256]{2,1,0:T(8,128)(2,1)S(1)}, u32[]{:S(2)}, u32[]{:S(2)}) async-start(bf16[16,32,256]{2,1,0:T(8,128)(2,1)} %broadcast_in_dim.14), calls=%async_computation | async-start | bytes 524288 | tf_op jit(solution)/shard_map/all_to_all | solution.py:18
  25.8 2.3 %copy-start.1 = (bf16[2,512,256]{2,1,0:T(8,128)(2,1)S(1)}, bf16[2,512,256]{2,1,0:T(8,128)(2,1)}, u32[]{:S(2)}) copy-start(bf16[2,512,256]{2,1,0:T(8,128)(2,1)} %param.6) | copy-start | bytes 1572868
  59.2 21.6 %all-to-all-start.3 = ((bf16[16,32,256]{2,1,0:T(8,128)(2,1)}), bf16[16,32,256]{2,1,0:T(8,128)(2,1)S(1)}, u32[]{:S(2)}, u32[]{:S(2)}) async-start(bf16[16,32,256]{2,1,0:T(8,128)(2,1)} %pad_maximum_fusion.7), calls=%async_computation.3 | async-start | bytes 524288 | tf_op jit(solution)/shard_map/all_to_all | solution.py:18
  76.3 1.0 copy-start.2
  164.3 12.8 %all-to-all-start.8 = ((bf16[32,16,256]{2,1,0:T(8,128)(2,1)}), bf16[32,16,256]{2,1,0:T(8,128)(2,1)S(1)}, u32[]{:S(2)}, u32[]{:S(2)}) async-start(bf16[32,16,256]{2,1,0:T(8,128)(2,1)} %broadcast_in_dim.19), calls=%async_computation.8 | async-start | bytes 524288 | tf_op jit(solution)/shard_map/all_to_all | solution.py:18

commit v9 on v7

--- a/solution.py
+++ b/solution.py
@@ -5,23 +5,33 @@
 
 BF = jnp.bfloat16
 F32 = jnp.float32
-ROW = ("x", "y")
+ROW = "row"
 Z = ("eight", "pair")
-COL = Z + ("core",)
+COL = ("eight", "pair", "core")
+PLANE = ("row", "core")
+WIDE = ("row", "pair", "core")
+FIRST = {Z: 8, ROW: 10, PLANE: 20, "eight": 4, "pair": 0, WIDE: 40}
 together = lax.optimization_barrier
 
 
 def swap(pieces, axis):
-    return lax.all_to_all(pieces, axis, 0, 0)
+    count, first = pieces.shape[0], FIRST[axis]
+    order = [(first + place) % count for place in range(count)]
+    return lax.all_to_all(pieces, axis, 0, 0, axis_index_groups=[order])
+
+
+def turn(pieces, by):
+    return jnp.concatenate([pieces[by:], pieces[:by]], axis=0)
 
 
 def spread(piece, axis, count):
-    return swap(jnp.broadcast_to(piece[None], (count,) + piece.shape), axis)
+    pieces = swap(jnp.broadcast_to(piece[None], (count,) + piece.shape), axis)
+    return turn(pieces, count - FIRST[axis])
 
 
-def cut(partial, count):
+def cut(partial, axis):
     rows, width = partial.shape
-    return partial.astype(BF).reshape(count, rows // count, width)
+    return turn(partial.astype(BF).reshape(16, rows // 16, width), FIRST[axis])
 
 
 def total(pieces):
@@ -34,15 +44,17 @@
 
 def body(outputs, inverses, former, latter):
     core = lax.axis_index("core").astype(jnp.uint32)
-    place = lax.axis_index(ROW).astype(jnp.uint32) * 16
+    place = (lax.axis_index(ROW).astype(jnp.uint32) + 16 - FIRST[ROW]) % 16 * 16
     half = outputs.shape[2] // 2
     own = outputs.shape[1]
     height = 2 * own
 
     def whiten(inverse, rows):
         partial = jnp.dot(inverse, rows, preferred_element_type=F32)
-        piece = total(swap(cut(partial, 16), ROW)).astype(BF)
-        return spread(piece, ROW, 16).reshape(-1, half)
+        partial = partial.astype(BF).reshape(16, -1, half)
+        piece = total(swap(partial, ROW)).astype(BF)
+        pieces = jnp.broadcast_to(piece[None], (16,) + piece.shape)
+        return swap(pieces, ROW).reshape(-1, half)
 
     def panel(tiles, white):
         depth = tiles.shape[2]
@@ -89,7 +101,7 @@
     block_start, end_start, slab_start = starts
     white0 = whiten(inverse0.reshape(-1, inverse0.shape[2]), gathered)
 
-    pieces = cut(panel(former0, white0), 16)
+    pieces = cut(panel(former0, white0), Z)
     pieces, white0 = together((pieces, white0))
     pieces = swap(pieces, Z)
     last, white0, latter0 = together((panel(former1, white0), white0, latter[0]))
@@ -112,7 +124,8 @@
     slabs = slabs0 + gram(whole1, white1)
     part = half // 16
     slab = window(slabs, slab_start, part, 0).astype(BF)
-    steps = last.astype(BF).reshape(8, 2, height, half).swapaxes(0, 1)
+    steps = last.astype(BF).reshape(8, 2, height, half)
+    steps = turn(steps, FIRST["eight"]).swapaxes(0, 1)
     pieces = jnp.concatenate(
         [
             steps.reshape(2, 8 * height, half),
@@ -131,10 +144,11 @@
     pieces, whole1 = together((swap(pieces, "eight"), whole1))
     slab = total(pieces[:, height:]).astype(BF)
     ends = total(pieces[:, :height])
-    pieces, ends, whole1 = together((jnp.broadcast_to(slab[None], (32,) + slab.shape), ends, whole1))
+    pieces = jnp.broadcast_to(slab[None], (32,) + slab.shape)
+    pieces, ends, whole1 = together((pieces, ends, whole1))
     block1, ends = together((block(whole1, block_start), ends))
     trailing = outputs[2:] - block(both_cores(ends), end_start)[None]
-    parts, trailing = together((swap(pieces, ROW + ("core",)), trailing))
+    parts, trailing = together((swap(pieces, PLANE), trailing))
     parts = parts.astype(F32).reshape(16, 2, part, half)
     projections = jnp.concatenate(
         [parts[:, 0].reshape(half, half), parts[:, 1].reshape(half, half)], axis=1
@@ -144,8 +158,8 @@
 
 
 def solution(mesh):
-    every = ROW + COL
-    grid = Mesh(mesh.devices.reshape(4, 4, 8, 2, 2), every)
+    grid = Mesh(mesh.devices.reshape(16, 8, 2, 2), ("row", "eight", "pair", "core"))
+    every = ("row",) + COL
     in_specs = (P(None, every, None), P(None, COL, ROW), P(None, ROW, COL), P(None, ROW, COL))
     out_specs = (P(None, COL, None), P(None, every, None), P())
     return jax.shard_map(body, mesh=grid, in_specs=in_specs, out_specs=out_specs, check_vma=False)

time: 186 us -> 177 us (0.952)
  waiting for transfers between devices: 13.3 us -> 3.9 us
  blocking collectives: 134 us -> 129 us
  starting transfers between devices: 28 us -> 33 us
    all_to_all x3, waiting for transfers between devices: 13.3 us -> 3.9 us  [swap(): return lax.all_to_all(pieces, axis, 0, 0, axis_index_groups=[order])]
    all_to_all x3, starting transfers between devices: 28 us -> 33 us  [swap(): return lax.all_to_all(pieces, axis, 0, 0, axis_index_groups=[order])]
    all_gather x9, blocking collectives: 38.5 us -> 33.5 us  [both_cores(): return lax.all_gather(block, 'core', axis=0)]
  transfers between devices with their start and end apart: 3 -> 3, of which waited for: 3 -> 2; matrix products, arithmetic and copies ran while one was open for 2% -> 2% of each run, Pallas kernels for 0% -> 0%
where the time goes in v9:
time: 177 us
  blocking collectives  129 us (73%)
  starting transfers between devices  33 us (19%)
  other arithmetic  4.18 us (2%)
  waiting for transfers between devices  3.9 us (2%)
  local copies, waits for them, and re-layouts  2.85 us (2%)
  matrix products  2.47 us (1%)
    all_to_all x7, blocking collectives, swap(): return lax.all_to_all(pieces, axis, 0, 0, axis_index_groups=[order])  95.7 us
    all_gather x9, blocking collectives, both_cores(): return lax.all_gather(block, 'core', axis=0)  33.5 us
    all_to_all x3, starting transfers between devices, swap(): return lax.all_to_all(pieces, axis, 0, 0, axis_index_groups=[order])  33 us
    all_to_all x3, waiting for transfers between devices, swap(): return lax.all_to_all(pieces, axis, 0, 0, axis_index_groups=[order])  3.9 us
  transfers between devices with their start and end apart: 3, of which 2 were waited for; matrix products, arithmetic and copies ran while one was open for 2% of the time, Pallas kernels for 0%

profile of v9, /device:TPU:1, one launch (start us, length us, event | category | flops | bytes accessed | tf_op | source)
XLA Modules:
  0.0 176.6 jit_solution(9803253682385701629)
XLA Ops:
  0.6 8.7 %all-gather = f32[6,16,512]{2,1,0:T(8,128)S(1)} all-gather(f32[3,16,512]{2,1,0:T(8,128)} %param.4), channel_id=2, replica_groups=mesh['row'=16,'eight'=8,'pair'=2,'core'=2] {'core'}, dimensions={0}, use_global_device_ids=true | all-gather | bytes 294912 | tf_op jit(solution)/shard_map/all_gather | solution.py:42
  9.3 0.7 broadcast_in_dim.16
  10.1 12.9 %all-to-all-start = ((bf16[16,32,256]{2,1,0:T(8,128)(2,1)}), bf16[16,32,256]{2,1,0:T(8,128)(2,1)S(1)}, u32[]{:S(2)}, u32[]{:S(2)}) async-start(bf16[16,32,256]{2,1,0:T(8,128)(2,1)} %broadcast_in_dim.16), calls=%async_computation | async-start | bytes 524288 | tf_op jit(solution)/shard_map/all_to_all | solution.py:20
  23.0 2.7 %all_gather.43 = bf16[2,256,512]{2,1,0:T(8,128)(2,1)S(1)} all-gather(bf16[1,256,512]{2,1,0:T(8,128)(2,1)S(1)} %get-tuple-element.65), channel_id=1, replica_groups=mesh['row'=16,'eight'=8,'pair'=2,'core'=2] {'core'}, dimensions={0}, use_global_device_ids=true | all-gather | bytes 786432 | tf_op jit(solution)/shard_map/all_gather | solution.py:42
  25.8 2.3 %all_gather.41 = bf16[2,256,512]{2,1,0:T(8,128)(2,1)S(1)} all-gather(bf16[1,256,512]{2,1,0:T(8,128)(2,1)S(1)} %get-tuple-element.66), channel_id=1, replica_groups=mesh['row'=16,'eight'=8,'pair'=2,'core'=2] {'core'}, dimensions={0}, use_global_device_ids=true | all-gather | bytes 786432 | tf_op jit(solution)/shard_map/all_gather | solution.py:42
  28.1 2.2 %all_gather.44 = bf16[2,512,256]{2,1,0:T(8,128)(2,1)S(1)} all-gather(bf16[1,512,256]{2,1,0:T(8,128)(2,1)S(1)} %get-tuple-element.63), channel_id=1, replica_groups=mesh['row'=16,'eight'=8,'pair'=2,'core'=2] {'core'}, dimensions={0}, use_global_device_ids=true | all-gather | bytes 786432 | tf_op jit(solution)/shard_map/all_gather | solution.py:42
  30.3 2.2 %all_gather.42 = bf16[2,512,256]{2,1,0:T(8,128)(2,1)S(1)} all-gather(bf16[1,512,256]{2,1,0:T(8,128)(2,1)S(1)} %get-tuple-element.64), channel_id=1, replica_groups=mesh['row'=16,'eight'=8,'pair'=2,'core'=2] {'core'}, dimensions={0}, use_global_device_ids=true | all-gather | bytes 786432 | tf_op jit(solution)/shard_map/all_gather | solution.py:42
  32.5 3.2 %all-to-all-done = bf16[16,32,256]{2,1,0:T(8,128)(2,1)S(1)} async-done(((bf16[16,32,256]{2,1,0:T(8,128)(2,1)}), bf16[16,32,256]{2,1,0:T(8,128)(2,1)S(1)}, u32[]{:S(2)}, u32[]{:S(2)}) %all-to-all-start) | async-done | bytes 262176 | tf_op jit(solution)/shard_map/all_to_all | solution.py:20
  35.7 0.3 convolution_convert_fusion.1
  36.0 11.2 %all_to_all.50 = bf16[16,32,256]{2,1,0:T(8,128)(2,1)S(1)} all-to-all(bf16[16,32,256]{2,1,0:T(8,128)(2,1)S(1)} %bitcast.98), channel_id=1, replica_groups={{320,352,384,416,448,480,0,32,64,96,128,160,192,224,256,288},{321,353,3..., dimensions={0} | all-to-all | bytes 524288 | tf_op jit(solution)/shard_map/all_to_all | solution.py:20
  47.4 10.4 %all_to_all.51 = bf16[16,32,256]{2,1,0:T(8,128)(2,1)S(1)} all-to-all(bf16[16,32,256]{2,1,0:T(8,128)(2,1)S(1)} %broadcast_in_dim.17), channel_id=1, replica_groups={{320,352,384,416,448,480,0,32,64,96,128,160,192,224,256,288},{321,353,3..., dimensions={0} | all-to-all | bytes 524288 | tf_op jit(solution)/shard_map/all_to_all | solution.py:20
  58.3 0.7 pad_maximum_fusion.4
  59.0 11.5 %all-to-all-start.3 = ((bf16[16,32,256]{2,1,0:T(8,128)(2,1)}), bf16[16,32,256]{2,1,0:T(8,128)(2,1)S(1)}, u32[]{:S(2)}, u32[]{:S(2)}) async-start(bf16[16,32,256]{2,1,0:T(8,128)(2,1)} %pad_maximum_fusion.4), calls=%async_computation.3 | async-start | bytes 524288 | tf_op jit(solution)/shard_map/all_to_all | solution.py:20
  71.0 5.2 %all-gather.1 = bf16[1024,256]{1,0:T(8,128)(2,1)S(1)} all-gather(bf16[512,256]{1,0:T(8,128)(2,1)S(1)} %bitcast.83), channel_id=3, replica_groups=mesh['row'=16,'eight'=8,'pair'=2,'core'=2] {'core'}, dimensions={0}, use_global_device_ids=true | all-gather | bytes 786432 | tf_op jit(solution)/shard_map/all_gather | solution.py:42
  76.2 0.9 copy-done.2
  77.1 2.2 %all-gather.2 = bf16[1024,256]{1,0:T(8,128)(2,1)S(1)} all-gather(bf16[512,256]{1,0:T(8,128)(2,1)S(1)} %bitcast.113), channel_id=4, replica_groups=mesh['row'=16,'eight'=8,'pair'=2,'core'=2] {'core'}, dimensions={0}, use_global_device_ids=true | all-gather | bytes 786432 | tf_op jit(solution)/shard_map/all_gather | solution.py:42
  79.3 0.3 fusion.4
  79.6 0.7 all-to-all-done.3
  80.3 22.4 %all_to_all.52 = bf16[16,32,256]{2,1,0:T(8,128)(2,1)S(1)} all-to-all(bf16[16,32,256]{2,1,0:T(8,128)(2,1)S(1)} %broadcast_in_dim.18), channel_id=1, replica_groups={{16,18,20,22,24,26,28,30,0,2,4,6,8,10,12,14},{17,19,21,23,25,27,29,31,1..., dimensions={0} | all-to-all | bytes 524288 | tf_op jit(solution)/shard_map/all_to_all | solution.py:20
  102.8 0.3 convolution_convert_fusion
  103.1 12.7 %all_to_all.53 = bf16[16,32,256]{2,1,0:T(8,128)(2,1)S(1)} all-to-all(bf16[16,32,256]{2,1,0:T(8,128)(2,1)S(1)} %bitcast.99), channel_id=1, replica_groups={{320,352,384,416,448,480,0,32,64,96,128,160,192,224,256,288},{321,353,3..., dimensions={0} | all-to-all | bytes 524288 | tf_op jit(solution)/shard_map/all_to_all | solution.py:20
  115.8 10.5 %all_to_all.54 = bf16[16,32,256]{2,1,0:T(8,128)(2,1)S(1)} all-to-all(bf16[16,32,256]{2,1,0:T(8,128)(2,1)S(1)} %broadcast_in_dim.19), channel_id=1, replica_groups={{320,352,384,416,448,480,0,32,64,96,128,160,192,224,256,288},{321,353,3..., dimensions={0} | all-to-all | bytes 524288 | tf_op jit(solution)/shard_map/all_to_all | solution.py:20
  126.9 6.3 %all_gather.49 = bf16[2,512,256]{2,1,0:T(8,128)(2,1)S(1)} all-gather(bf16[1,512,256]{2,1,0:T(8,128)(2,1)S(1)} %bitcast.85), channel_id=1, replica_groups=mesh['row'=16,'eight'=8,'pair'=2,'core'=2] {'core'}, dimensions={0}, use_global_device_ids=true | all-gather | bytes 786432 | tf_op jit(solution)/shard_map/all_gather | solution.py:42
  133.2 0.3 fusion.3
  133.5 7.4 %all_to_all.55 = bf16[2,272,256]{2,1,0:T(8,128)(2,1)S(1)} all-to-all(bf16[2,272,256]{2,1,0:T(8,128)(2,1)S(1)} %pad_maximum_fusion.2), channel_id=1, replica_groups={{0,2},{1,3},{4,6},{5,7},{8,10},{9,11},{12,14},{13,15},{16,18},{17,19},{..., dimensions={0} | all-to-all | bytes 557056 | tf_op jit(solution)/shard_map/all_to_all | solution.py:20
  141.0 21.0 %all_to_all.56 = bf16[8,48,256]{2,1,0:T(8,128)(2,1)S(1)} all-to-all(bf16[8,48,256]{2,1,0:T(8,128)(2,1)S(1)} %pad_maximum_fusion.9), channel_id=1, replica_groups={{16,20,24,28,0,4,8,12},{17,21,25,29,1,5,9,13},{18,22,26,30,2,6,10,14},{..., dimensions={0} | all-to-all | bytes 393216 | tf_op jit(solution)/shard_map/all_to_all | solution.py:20
  162.1 0.7 broadcast_in_dim.22
  162.9 8.7 %all-to-all-start.9 = ((bf16[32,16,256]{2,1,0:T(8,128)(2,1)}), bf16[32,16,256]{2,1,0:T(8,128)(2,1)S(1)}, u32[]{:S(2)}, u32[]{:S(2)}) async-start(bf16[32,16,256]{2,1,0:T(8,128)(2,1)} %broadcast_in_dim.22), calls=%async_computation.9 | async-start | bytes 524288 | tf_op jit(solution)/shard_map/all_to_all | solution.py:20
  171.6 1.9 %all-gather.3 = f32[64,256]{1,0:T(8,128)S(1)} all-gather(f32[32,256]{1,0:T(8,128)S(1)} %convert_reduce_fusion.4), channel_id=5, replica_groups=mesh['row'=16,'eight'=8,'pair'=2,'core'=2] {'core'}, dimensions={0}, use_global_device_ids=true | all-gather | bytes 98304 | tf_op jit(solution)/shard_map/all_gather | solution.py:42
  173.4 0.8 pad_maximum_fusion
  174.3 1.4 fusion.23
  175.7 0.9 pad_maximum_fusion.1
  (49 shorter events, 2.2 us)
Async XLA Ops:
  9.3 13.7 %copy-start = (bf16[2,256,512]{2,1,0:T(8,128)(2,1)S(1)}, bf16[2,256,512]{2,1,0:T(8,128)(2,1)}, u32[]{:S(2)}) copy-start(bf16[2,256,512]{2,1,0:T(8,128)(2,1)} %param.5) | copy-start | bytes 1572868
  10.1 25.6 %all-to-all-start = ((bf16[16,32,256]{2,1,0:T(8,128)(2,1)}), bf16[16,32,256]{2,1,0:T(8,128)(2,1)S(1)}, u32[]{:S(2)}, u32[]{:S(2)}) async-start(bf16[16,32,256]{2,1,0:T(8,128)(2,1)} %broadcast_in_dim.16), calls=%async_computation | async-start | bytes 524288 | tf_op jit(solution)/shard_map/all_to_all | solution.py:20
  25.8 2.3 %copy-start.1 = (bf16[2,512,256]{2,1,0:T(8,128)(2,1)S(1)}, bf16[2,512,256]{2,1,0:T(8,128)(2,1)}, u32[]{:S(2)}) copy-start(bf16[2,512,256]{2,1,0:T(8,128)(2,1)} %param.6) | copy-start | bytes 1572868
  59.0 21.2 %all-to-all-start.3 = ((bf16[16,32,256]{2,1,0:T(8,128)(2,1)}), bf16[16,32,256]{2,1,0:T(8,128)(2,1)S(1)}, u32[]{:S(2)}, u32[]{:S(2)}) async-start(bf16[16,32,256]{2,1,0:T(8,128)(2,1)} %pad_maximum_fusion.4), calls=%async_computation.3 | async-start | bytes 524288 | tf_op jit(solution)/shard_map/all_to_all | solution.py:20
  76.2 1.0 copy-start.2
  162.9 12.8 %all-to-all-start.9 = ((bf16[32,16,256]{2,1,0:T(8,128)(2,1)}), bf16[32,16,256]{2,1,0:T(8,128)(2,1)S(1)}, u32[]{:S(2)}, u32[]{:S(2)}) async-start(bf16[32,16,256]{2,1,0:T(8,128)(2,1)} %broadcast_in_dim.22), calls=%async_computation.9 | async-start | bytes 524288 | tf_op jit(solution)/shard_map/all_to_all | solution.py:20

commit v10 on v9

--- a/solution.py
+++ b/solution.py
@@ -25,8 +25,7 @@
 
 
 def spread(piece, axis, count):
-    pieces = swap(jnp.broadcast_to(piece[None], (count,) + piece.shape), axis)
-    return turn(pieces, count - FIRST[axis])
+    return swap(jnp.broadcast_to(piece[None], (count,) + piece.shape), axis)
 
 
 def cut(partial, axis):
@@ -50,7 +49,9 @@
     height = 2 * own
 
     def whiten(inverse, rows):
-        partial = jnp.dot(inverse, rows, preferred_element_type=F32)
+        depth = rows.shape[0] // 2
+        partial = jnp.dot(inverse[:, depth:], rows[:depth], preferred_element_type=F32)
+        partial = partial + jnp.dot(inverse[:, :depth], rows[depth:], preferred_element_type=F32)
         partial = partial.astype(BF).reshape(16, -1, half)
         piece = total(swap(partial, ROW)).astype(BF)
         pieces = jnp.broadcast_to(piece[None], (16,) + piece.shape)

time: 177 us -> 178 us (level)
  no operation moved by 1% of the time
where the time goes in v10:
time: 178 us; the launch traced here: 177 us
  blocking collectives  129 us (72%)
  starting transfers between devices  33 us (19%)
  waiting for transfers between devices  4.28 us (2%)
  other arithmetic  4.12 us (2%)
  local copies, waits for them, and re-layouts  2.83 us (2%)
  matrix products  2.77 us (2%)
    all_to_all x7, blocking collectives, swap(): return lax.all_to_all(pieces, axis, 0, 0, axis_index_groups=[order])  95.3 us
    all_gather x9, blocking collectives, both_cores(): return lax.all_gather(block, 'core', axis=0)  33.5 us
    all_to_all x3, starting transfers between devices, swap(): return lax.all_to_all(pieces, axis, 0, 0, axis_index_groups=[order])  33 us
    all_to_all x3, waiting for transfers between devices, swap(): return lax.all_to_all(pieces, axis, 0, 0, axis_index_groups=[order])  4.28 us
  transfers between devices with their start and end apart: 3, of which 2 were waited for; matrix products, arithmetic and copies ran while one was open for 2% of the time, Pallas kernels for 0%

profile of v10, /device:TPU:1, one launch (start us, length us, event | category | flops | bytes accessed | tf_op | source)
XLA Modules:
  0.0 176.8 jit_solution(7409848423514416663)
XLA Ops:
  0.6 8.7 %all-gather = f32[6,16,512]{2,1,0:T(8,128)S(1)} all-gather(f32[3,16,512]{2,1,0:T(8,128)} %param.4), channel_id=2, replica_groups=mesh['row'=16,'eight'=8,'pair'=2,'core'=2] {'core'}, dimensions={0}, use_global_device_ids=true | all-gather | bytes 294912 | tf_op jit(solution)/shard_map/all_gather | solution.py:41
  9.3 0.7 broadcast_in_dim.16
  10.1 12.9 %all-to-all-start = ((bf16[16,32,256]{2,1,0:T(8,128)(2,1)}), bf16[16,32,256]{2,1,0:T(8,128)(2,1)S(1)}, u32[]{:S(2)}, u32[]{:S(2)}) async-start(bf16[16,32,256]{2,1,0:T(8,128)(2,1)} %broadcast_in_dim.16), calls=%async_computation | async-start | bytes 524288 | tf_op jit(solution)/shard_map/all_to_all | solution.py:20
  23.0 2.7 %all_gather.43 = bf16[2,256,512]{2,1,0:T(8,128)(2,1)S(1)} all-gather(bf16[1,256,512]{2,1,0:T(8,128)(2,1)S(1)} %get-tuple-element.65), channel_id=1, replica_groups=mesh['row'=16,'eight'=8,'pair'=2,'core'=2] {'core'}, dimensions={0}, use_global_device_ids=true | all-gather | bytes 786432 | tf_op jit(solution)/shard_map/all_gather | solution.py:41
  25.8 2.3 %all_gather.41 = bf16[2,256,512]{2,1,0:T(8,128)(2,1)S(1)} all-gather(bf16[1,256,512]{2,1,0:T(8,128)(2,1)S(1)} %get-tuple-element.66), channel_id=1, replica_groups=mesh['row'=16,'eight'=8,'pair'=2,'core'=2] {'core'}, dimensions={0}, use_global_device_ids=true | all-gather | bytes 786432 | tf_op jit(solution)/shard_map/all_gather | solution.py:41
  28.1 2.2 %all_gather.44 = bf16[2,512,256]{2,1,0:T(8,128)(2,1)S(1)} all-gather(bf16[1,512,256]{2,1,0:T(8,128)(2,1)S(1)} %get-tuple-element.63), channel_id=1, replica_groups=mesh['row'=16,'eight'=8,'pair'=2,'core'=2] {'core'}, dimensions={0}, use_global_device_ids=true | all-gather | bytes 786432 | tf_op jit(solution)/shard_map/all_gather | solution.py:41
  30.3 2.2 %all_gather.42 = bf16[2,512,256]{2,1,0:T(8,128)(2,1)S(1)} all-gather(bf16[1,512,256]{2,1,0:T(8,128)(2,1)S(1)} %get-tuple-element.64), channel_id=1, replica_groups=mesh['row'=16,'eight'=8,'pair'=2,'core'=2] {'core'}, dimensions={0}, use_global_device_ids=true | all-gather | bytes 786432 | tf_op jit(solution)/shard_map/all_gather | solution.py:41
  32.5 3.2 %all-to-all-done = bf16[16,32,256]{2,1,0:T(8,128)(2,1)S(1)} async-done(((bf16[16,32,256]{2,1,0:T(8,128)(2,1)}), bf16[16,32,256]{2,1,0:T(8,128)(2,1)S(1)}, u32[]{:S(2)}, u32[]{:S(2)}) %all-to-all-start) | async-done | bytes 262176 | tf_op jit(solution)/shard_map/all_to_all | solution.py:20
  36.1 11.2 %all_to_all.50 = bf16[16,32,256]{2,1,0:T(8,128)(2,1)S(1)} all-to-all(bf16[16,32,256]{2,1,0:T(8,128)(2,1)S(1)} %bitcast.99), channel_id=1, replica_groups={{320,352,384,416,448,480,0,32,64,96,128,160,192,224,256,288},{321,353,3..., dimensions={0} | all-to-all | bytes 524288 | tf_op jit(solution)/shard_map/all_to_all | solution.py:20
  47.5 10.4 %all_to_all.51 = bf16[16,32,256]{2,1,0:T(8,128)(2,1)S(1)} all-to-all(bf16[16,32,256]{2,1,0:T(8,128)(2,1)S(1)} %broadcast_in_dim.17), channel_id=1, replica_groups={{320,352,384,416,448,480,0,32,64,96,128,160,192,224,256,288},{321,353,3..., dimensions={0} | all-to-all | bytes 524288 | tf_op jit(solution)/shard_map/all_to_all | solution.py:20
  58.1 0.2 fusion.3
  58.4 0.7 pad_maximum_fusion.3
  59.1 11.5 %all-to-all-start.3 = ((bf16[16,32,256]{2,1,0:T(8,128)(2,1)}), bf16[16,32,256]{2,1,0:T(8,128)(2,1)S(1)}, u32[]{:S(2)}, u32[]{:S(2)}) async-start(bf16[16,32,256]{2,1,0:T(8,128)(2,1)} %pad_maximum_fusion.3), calls=%async_computation.3 | async-start | bytes 524288 | tf_op jit(solution)/shard_map/all_to_all | solution.py:20
  71.1 5.2 %all-gather.1 = bf16[1024,256]{1,0:T(8,128)(2,1)S(1)} all-gather(bf16[512,256]{1,0:T(8,128)(2,1)S(1)} %bitcast.82), channel_id=3, replica_groups=mesh['row'=16,'eight'=8,'pair'=2,'core'=2] {'core'}, dimensions={0}, use_global_device_ids=true | all-gather | bytes 786432 | tf_op jit(solution)/shard_map/all_gather | solution.py:41
  76.3 0.9 copy-done.2
  77.2 2.2 %all-gather.2 = bf16[1024,256]{1,0:T(8,128)(2,1)S(1)} all-gather(bf16[512,256]{1,0:T(8,128)(2,1)S(1)} %bitcast.116), channel_id=4, replica_groups=mesh['row'=16,'eight'=8,'pair'=2,'core'=2] {'core'}, dimensions={0}, use_global_device_ids=true | all-gather | bytes 786432 | tf_op jit(solution)/shard_map/all_gather | solution.py:41
  79.4 0.3 fusion.9
  79.7 1.0 all-to-all-done.3
  80.8 22.0 %all_to_all.52 = bf16[16,32,256]{2,1,0:T(8,128)(2,1)S(1)} all-to-all(bf16[16,32,256]{2,1,0:T(8,128)(2,1)S(1)} %broadcast_in_dim.18), channel_id=1, replica_groups={{16,18,20,22,24,26,28,30,0,2,4,6,8,10,12,14},{17,19,21,23,25,27,29,31,1..., dimensions={0} | all-to-all | bytes 524288 | tf_op jit(solution)/shard_map/all_to_all | solution.py:20
  103.3 12.7 %all_to_all.53 = bf16[16,32,256]{2,1,0:T(8,128)(2,1)S(1)} all-to-all(bf16[16,32,256]{2,1,0:T(8,128)(2,1)S(1)} %bitcast.100), channel_id=1, replica_groups={{320,352,384,416,448,480,0,32,64,96,128,160,192,224,256,288},{321,353,3..., dimensions={0} | all-to-all | bytes 524288 | tf_op jit(solution)/shard_map/all_to_all | solution.py:20
  116.1 10.5 %all_to_all.54 = bf16[16,32,256]{2,1,0:T(8,128)(2,1)S(1)} all-to-all(bf16[16,32,256]{2,1,0:T(8,128)(2,1)S(1)} %broadcast_in_dim.19), channel_id=1, replica_groups={{320,352,384,416,448,480,0,32,64,96,128,160,192,224,256,288},{321,353,3..., dimensions={0} | all-to-all | bytes 524288 | tf_op jit(solution)/shard_map/all_to_all | solution.py:20
  126.8 0.2 fusion.1
  127.1 6.3 %all_gather.49 = bf16[2,512,256]{2,1,0:T(8,128)(2,1)S(1)} all-gather(bf16[1,512,256]{2,1,0:T(8,128)(2,1)S(1)} %bitcast.84), channel_id=1, replica_groups=mesh['row'=16,'eight'=8,'pair'=2,'core'=2] {'core'}, dimensions={0}, use_global_device_ids=true | all-gather | bytes 786432 | tf_op jit(solution)/shard_map/all_gather | solution.py:41
  133.4 0.3 fusion.5
  133.7 7.4 %all_to_all.55 = bf16[2,272,256]{2,1,0:T(8,128)(2,1)S(1)} all-to-all(bf16[2,272,256]{2,1,0:T(8,128)(2,1)S(1)} %pad_maximum_fusion.2), channel_id=1, replica_groups={{0,2},{1,3},{4,6},{5,7},{8,10},{9,11},{12,14},{13,15},{16,18},{17,19},{..., dimensions={0} | all-to-all | bytes 557056 | tf_op jit(solution)/shard_map/all_to_all | solution.py:20
  141.2 21.0 %all_to_all.56 = bf16[8,48,256]{2,1,0:T(8,128)(2,1)S(1)} all-to-all(bf16[8,48,256]{2,1,0:T(8,128)(2,1)S(1)} %pad_maximum_fusion.7), channel_id=1, replica_groups={{16,20,24,28,0,4,8,12},{17,21,25,29,1,5,9,13},{18,22,26,30,2,6,10,14},{..., dimensions={0} | all-to-all | bytes 393216 | tf_op jit(solution)/shard_map/all_to_all | solution.py:20
  162.3 0.7 broadcast_in_dim.22
  163.1 8.7 %all-to-all-start.9 = ((bf16[32,16,256]{2,1,0:T(8,128)(2,1)}), bf16[32,16,256]{2,1,0:T(8,128)(2,1)S(1)}, u32[]{:S(2)}, u32[]{:S(2)}) async-start(bf16[32,16,256]{2,1,0:T(8,128)(2,1)} %broadcast_in_dim.22), calls=%async_computation.9 | async-start | bytes 524288 | tf_op jit(solution)/shard_map/all_to_all | solution.py:20
  171.8 1.9 %all-gather.3 = f32[64,256]{1,0:T(8,128)S(1)} all-gather(f32[32,256]{1,0:T(8,128)S(1)} %convert_reduce_fusion.4), channel_id=5, replica_groups=mesh['row'=16,'eight'=8,'pair'=2,'core'=2] {'core'}, dimensions={0}, use_global_device_ids=true | all-gather | bytes 98304 | tf_op jit(solution)/shard_map/all_gather | solution.py:41
  173.7 0.8 pad_maximum_fusion
  174.5 1.4 fusion.33
  175.9 0.9 pad_maximum_fusion.1
  (48 shorter events, 2.6 us)
Async XLA Ops:
  9.3 13.7 %copy-start = (bf16[2,256,512]{2,1,0:T(8,128)(2,1)S(1)}, bf16[2,256,512]{2,1,0:T(8,128)(2,1)}, u32[]{:S(2)}) copy-start(bf16[2,256,512]{2,1,0:T(8,128)(2,1)} %param.5) | copy-start | bytes 1572868
  10.1 25.6 %all-to-all-start = ((bf16[16,32,256]{2,1,0:T(8,128)(2,1)}), bf16[16,32,256]{2,1,0:T(8,128)(2,1)S(1)}, u32[]{:S(2)}, u32[]{:S(2)}) async-start(bf16[16,32,256]{2,1,0:T(8,128)(2,1)} %broadcast_in_dim.16), calls=%async_computation | async-start | bytes 524288 | tf_op jit(solution)/shard_map/all_to_all | solution.py:20
  25.8 2.3 %copy-start.1 = (bf16[2,512,256]{2,1,0:T(8,128)(2,1)S(1)}, bf16[2,512,256]{2,1,0:T(8,128)(2,1)}, u32[]{:S(2)}) copy-start(bf16[2,512,256]{2,1,0:T(8,128)(2,1)} %param.6) | copy-start | bytes 1572868
  59.1 21.6 %all-to-all-start.3 = ((bf16[16,32,256]{2,1,0:T(8,128)(2,1)}), bf16[16,32,256]{2,1,0:T(8,128)(2,1)S(1)}, u32[]{:S(2)}, u32[]{:S(2)}) async-start(bf16[16,32,256]{2,1,0:T(8,128)(2,1)} %pad_maximum_fusion.3), calls=%async_computation.3 | async-start | bytes 524288 | tf_op jit(solution)/shard_map/all_to_all | solution.py:20
  76.3 1.0 copy-start.2
  163.1 12.8 %all-to-all-start.9 = ((bf16[32,16,256]{2,1,0:T(8,128)(2,1)}), bf16[32,16,256]{2,1,0:T(8,128)(2,1)S(1)}, u32[]{:S(2)}, u32[]{:S(2)}) async-start(bf16[32,16,256]{2,1,0:T(8,128)(2,1)} %broadcast_in_dim.22), calls=%async_computation.9 | async-start | bytes 524288 | tf_op jit(solution)/shard_map/all_to_all | solution.py:20
